TPU v7x, 256 devices: a whole 4x4x8 slice. The times are simulated.
256 devices in a mesh: band: 8 (over x_lo, y), sector: 32 (over x_hi, z, core).
Axes of the slice: x: 4 (x_hi: 2, x_lo: 2; x = x_hi * 2 + x_lo), y: 4, z: 8, core: 2. Of those that a mesh axis runs over, the one named last changes fastest.
Arguments:
- grid_lat: bfloat16 [64, 2048, 512], P('band', 'sector'), may hold values from -6 to 6
- mesh_lat: bfloat16 [32768, 512], P(('band', 'sector')), may hold values from -6 to 6
- edge_feat: bfloat16 [393216, 512], P(('band', 'sector')), may hold values from -24 to 24
- edge_src: int32 [393216], P(('band', 'sector')), may hold values from 0 to 255, as said below
- edge_dst: int32 [393216], P(('band', 'sector')), may hold values from 0 to 511, as said below
- send_rows: int32 [32768], P(('band', 'sector')), may hold values from 0 to 127
- w_edge1: bfloat16 [1536, 512], replicated, may hold values from -0.15625 to 0.15625
- w_edge2: bfloat16 [512, 512], replicated, may hold values from -0.25 to 0.25
- edge_gain: float32 [512], replicated, may hold values from 0.25 to 1.75
- w_node1: bfloat16 [1024, 512], replicated, may hold values from -0.1875 to 0.1875
- w_node2: bfloat16 [512, 512], replicated, may hold values from -0.25 to 0.25
- node_gain: float32 [512], replicated, may hold values from 0.25 to 1.75
- cotangent: bfloat16 [64, 2048, 512], P('band', 'sector'), may hold values from -6 to 6
Outputs:
- grid_out: bfloat16 [64, 2048, 512], P('band', 'sector')
- grad_grid: bfloat16 [64, 2048, 512], P('band', 'sector')
- grad_mesh: bfloat16 [32768, 512], P(('band', 'sector'))
- grad_w_edge1: float32 [1536, 512], P('sector')
Inputs may be any that keep to these rules, and one draw needn't show every extreme that they name: `edge_src`: A device's mesh table is its 128 own rows followed by 32 rows each from the sector neighbour below, the sector neighbour above, the band neighbour below and the band neighbour above; devices of the first band never read the rows from below, those of the last band never the rows from above. `edge_dst`: each grid point of a device is the destination of exactly 3 of that device's edges; edges are in no particular order.
All inputs are finite; a program needn't handle non-finite values.
Results may differ from a plain program's by a relative error of at most 0.02.
Values may be sent and summed in bfloat16 or wider, within the bound.
No kernel may reach another device: no remote copies, remote signals or barrier semaphores. Data moves between devices by JAX's collectives and lax.ppermute only.
A program may use at most 64 MiB of HBM per device.

v0:
```python
import math

import jax
import jax.numpy as jnp
from jax import lax
from jax.sharding import PartitionSpec as P

EPSILON = 1e-05


def with_halo(shard, sides, width, wrap):
    for axis, dim in sides:
        devices, length = (lax.axis_size(axis), shard.shape[dim])
        up = [(i, (i + 1) % devices) for i in range(devices if wrap else devices - 1)]
        down = [(j, i) for i, j in up]
        last = lax.slice_in_dim(shard, length - width, length, axis=dim)
        initial = lax.slice_in_dim(shard, 0, width, axis=dim)
        before = lax.ppermute(last, axis, up)
        after = lax.ppermute(initial, axis, down)
        shard = jnp.concatenate([before, shard, after], axis=dim)
    return shard


def swish(values):
    return values * jax.nn.sigmoid(values)


def layer_norm(values, gain_vector):
    average = jnp.mean(values, axis=-1, keepdims=True)
    centred = values - average
    spread = jnp.mean(centred * centred, axis=-1, keepdims=True)
    return centred * lax.rsqrt(spread + EPSILON) * gain_vector


def decode_tail(pre_act, grid_wide, edge_dst, w_edge2, edge_gain, w_node1, w_node2, node_gain):
    hidden = swish(pre_act).astype(jnp.bfloat16)
    edge_raw = jnp.dot(hidden, w_edge2, preferred_element_type=jnp.float32)
    message = layer_norm(edge_raw, edge_gain).astype(jnp.bfloat16)
    points = grid_wide.shape[0]
    onehot = (edge_dst[None, :] == jnp.arange(points, dtype=jnp.int32)[:, None]).astype(
        jnp.bfloat16
    )
    aggregated = jnp.dot(onehot, message, preferred_element_type=jnp.float32).astype(jnp.bfloat16)
    node_input = jnp.concatenate([aggregated, grid_wide.astype(jnp.bfloat16)], axis=1)
    node_hidden = swish(jnp.dot(node_input, w_node1, preferred_element_type=jnp.float32)).astype(
        jnp.bfloat16
    )
    node_raw = jnp.dot(node_hidden, w_node2, preferred_element_type=jnp.float32)
    return (grid_wide + layer_norm(node_raw, node_gain)).astype(jnp.bfloat16)


def shards(
    grid_lat,
    mesh_lat,
    edge_feat,
    edge_src,
    edge_dst,
    send_rows,
    w_edge1,
    w_edge2,
    edge_gain,
    w_node1,
    w_node2,
    node_gain,
    cotangent,
):
    feature_width = w_edge2.shape[0]
    lat_rows = grid_lat.shape[0]
    lon_cols = grid_lat.shape[1]
    grid_block = grid_lat.reshape(lat_rows * lon_cols, feature_width)
    cot_block = cotangent.reshape(lat_rows * lon_cols, feature_width)
    own_rows = mesh_lat.shape[0]
    margin = send_rows.shape[0] // 4
    picked = jnp.take(mesh_lat, send_rows, axis=0)
    sector_recv = with_halo(picked[: 2 * margin], (("sector", 0),), margin, True)
    band_recv = with_halo(picked[2 * margin :], (("band", 0),), margin, False)
    mesh_table = jnp.concatenate(
        [
            mesh_lat,
            sector_recv[:margin],
            sector_recv[3 * margin :],
            band_recv[:margin],
            band_recv[3 * margin :],
        ],
        axis=0,
    )
    inputs = jnp.concatenate([edge_feat, mesh_table[edge_src], grid_block[edge_dst]], axis=1)
    pre_act = jnp.dot(inputs, w_edge1, preferred_element_type=jnp.float32)
    grid_wide = grid_block.astype(jnp.float32)

    def finish(pre_values, grid_values):
        return decode_tail(
            pre_values, grid_values, edge_dst, w_edge2, edge_gain, w_node1, w_node2, node_gain
        )

    result, pullback = jax.vjp(finish, pre_act, grid_wide)
    grad_pre, grad_tail = pullback(cot_block)
    grad_pre_b = grad_pre.astype(jnp.bfloat16)
    grad_inputs = lax.dot_general(
        grad_pre_b,
        w_edge1[feature_width:],
        (((1,), (1,)), ((), ())),
        preferred_element_type=jnp.float32,
    )
    grad_table = jax.ops.segment_sum(
        grad_inputs[:, :feature_width], edge_src, num_segments=mesh_table.shape[0]
    )
    grad_grid = grad_tail + jax.ops.segment_sum(
        grad_inputs[:, feature_width:], edge_dst, num_segments=grid_block.shape[0]
    )
    sector_back = with_halo(
        grad_table[own_rows : own_rows + 2 * margin].astype(jnp.bfloat16),
        (("sector", 0),),
        margin,
        True,
    ).astype(jnp.float32)
    band_back = with_halo(
        grad_table[own_rows + 2 * margin :].astype(jnp.bfloat16), (("band", 0),), margin, False
    ).astype(jnp.float32)
    returned = jnp.concatenate(
        [
            sector_back[:margin],
            sector_back[3 * margin :],
            band_back[:margin],
            band_back[3 * margin :],
        ],
        axis=0,
    )
    grad_mesh = (
        grad_table[:own_rows] + jax.ops.segment_sum(returned, send_rows, num_segments=own_rows)
    ).astype(jnp.bfloat16)
    total_edges = edge_feat.shape[0] * lax.axis_size("band") * lax.axis_size("sector")
    grad_scale = 1.0 / math.sqrt(total_edges)
    rows_out = 3 * feature_width // lax.axis_size("sector")
    full_grad = lax.dot_general(
        inputs, grad_pre_b, (((0,), (0,)), ((), ())), preferred_element_type=jnp.float32
    )
    summed = lax.psum(full_grad, ("band", "sector"))
    share_rows = lax.dynamic_slice_in_dim(summed, lax.axis_index("sector") * rows_out, rows_out, 0)
    grad_w_edge1 = share_rows * grad_scale
    grid_out = result.reshape(lat_rows, lon_cols, feature_width)
    grad_grid_out = grad_grid.astype(jnp.bfloat16).reshape(lat_rows, lon_cols, feature_width)
    return (grid_out, grad_grid_out, grad_mesh, grad_w_edge1)


def solution(mesh):
    in_specs = (
        P("band", "sector", None),
        P(("band", "sector"), None),
        P(("band", "sector"), None),
        P(("band", "sector")),
        P(("band", "sector")),
        P(("band", "sector")),
        P(),
        P(),
        P(),
        P(),
        P(),
        P(),
        P("band", "sector", None),
    )
    out_specs = (
        P("band", "sector", None),
        P("band", "sector", None),
        P(("band", "sector"), None),
        P("sector", None),
    )
    return jax.shard_map(shards, mesh=mesh, in_specs=in_specs, out_specs=out_specs, check_vma=False)
```

profile of v0, /device:TPU:32, one launch (start us, length us, event | category | flops | bytes accessed | tf_op | source)
XLA Modules:
  0.0 341.2 jit_solution(3824243465645055062)
XLA Ops:
  8.7 1.8 gather_fusion
  11.2 1.7 collective-permute-start.1
  13.0 3.5 %collective-permute-start.2 = (bf16[32,512]{1,0:T(8,128)(2,1)}, bf16[32,512]{1,0:T(8,128)(2,1)S(1)}, u32[]{:S(2)}, u32[]{:S(2)}) collective-permute-start(bf16[32,512]{1,0:T(8,128)(2,1)} %get-tuple-element.20), channel_id=1, source_target_pairs={{0,32},{32,64},{64,96},{96,128},{128,160},{160,192},{192,224},{1,3... | collective-permute-start | bytes 98312 | tf_op jit(solution)/shard_map/ppermute | solution.py:18
  16.5 1.3 collective-permute-start.3
  18.7 2.7 constant_dynamic-update-slice_fusion.7
  21.4 4.8 %gather_fusion.2 = bf16[1536,512]{1,0:T(8,128)(2,1)S(1)} fusion(bf16[512,512]{1,0:T(8,128)(2,1)S(1)} %bitcast.21, s32[2048]{0:T(1024)S(1)} %pad_clamp_fusion), kind=kCustom, calls=%fused_computation.2 | custom fusion | bytes 3151872 | tf_op jit(solution)/shard_map/gather | solution.py:87
  26.4 5.4 %gather_fusion.1 = bf16[1536,512]{1,0:T(8,128)(2,1)} fusion(bf16[256,512]{1,0:T(8,128)(2,1)S(1)} %constant_dynamic-update-slice_fusion, s32[2048]{0:T(1024)S(1)} %pad_clamp_fusion.1), kind=kCustom, calls=%fused_computation.1 | custom fusion | bytes 3151872 | tf_op jit(solution)/shard_map/gather | solution.py:87
  31.8 2.8 constant_dynamic-update-slice_fusion.6
  34.6 1.3 constant_dynamic-update-slice_fusion.5
  35.9 4.5 %fusion.69 = f32[1536,512]{1,0:T(8,128)S(1)} fusion(bf16[1536,1536]{1,0:T(8,128)(2,1)} %constant_dynamic-update-slice_fusion.5, bf16[1536,512]{1,0:T(8,128)(2,1)S(1)} %copy-done.10), kind=kOutput, calls=%fused_computation.121 | convolution fusion | flops 2415919104 | bytes 9437184 | tf_op jit(solution)/shard_map/dot_general | solution.py:88
  46.9 1.3 fusion.63
  48.2 3.6 %convolution_convert_fusion = bf16[512,1024]{1,0:T(8,128)(2,1)} fusion(bf16[1024,512]{1,0:T(8,128)(2,1)S(1)} %copy-done, f32[512,512]{1,0:T(8,128)} %copy-done.15, bf16[512,512]{1,0:T(8,128)(2,1)} %param.23, f32[512,512]{1,0:T(8,128)S(1)} %get-tuple-element.7, f32[512]{0:T(512)S(1)} %negate_multiply_fusion.1), kind=kOutput, calls=%fused_computation.39 | convolution fusion | flops 808976384 | bytes 4720640 | tf_op jit(solution)/shard_map/transpose(jvp())/dot_general | solution.py:45
  51.8 3.5 %multiply_reduce_fusion = (f32[1536]{0:T(1024)S(1)}, bf16[1536,512]{0,1:T(8,128)(2,1)S(1)}) fusion(f32[1536,512]{0,1:T(8,128)} %copy-done.2, f32[512]{0:T(512)S(1)} %copy-done.9, f32[1536]{0:T(1024)S(1)} %broadcast_multiply_fusion, bf16[512,1024]{1,0:T(8,128)(2,1)} %convolution_convert_fusion, s32[1536]{0:T(1024)S(1)} %copy-done.8), kind=kOutput, calls=%fused_computation.19 | convolution fusion | flops 810809856 | bytes 5263360 | tf_op jit(solution)/shard_map/transpose(jvp())/dot_general | solution.py:43
  57.4 2.6 fusion.1
  61.2 4.3 %fusion.70 = f32[1536,512]{1,0:T(8,128)} fusion(bf16[1536,1536]{1,0:T(8,128)(2,1)S(1)} %bitcast.26, bf16[1536,512]{1,0:T(8,128)(2,1)S(1)} %fusion.1), kind=kOutput, calls=%fused_computation.122 | convolution fusion | flops 2415919104 | bytes 9437184 | tf_op jit(solution)/shard_map/dot_general | solution.py:135
  65.5 6.2 %fusion.36 = f32[1536,1024]{1,0:T(8,128)} fusion(bf16[1536,512]{1,0:T(8,128)(2,1)} %copy-done.14, bf16[1536,512]{1,0:T(8,128)(2,1)} %param.19), kind=kOutput, calls=%fused_computation.55 | convolution fusion | flops 1610612736 | bytes 8912896 | tf_op jit(solution)/shard_map/dot_general | solution.py:99
  71.7 10.6 %scatter_custom_fusion.1 = f32[256,512]{1,0:T(8,128)S(1)} fusion(s32[1536]{0:T(1024)} %param.16, f32[1536,1024]{1,0:T(8,128)} %fusion.36, f32[]{:T(128)} %constant.22.clone.1), kind=kCustom, calls=%fused_computation.13 | custom fusion | flops 786432 | bytes 3670528 | tf_op jit(solution)/shard_map/scatter-add | solution.py:105
  82.3 1.3 collective-permute-start.7
  83.6 5.2 %collective-permute-start.6 = (bf16[32,512]{1,0:T(8,128)(2,1)S(1)}, bf16[32,512]{1,0:T(8,128)(2,1)S(1)}, u32[]{:S(2)}, u32[]{:S(2)}) collective-permute-start(bf16[32,512]{1,0:T(8,128)(2,1)S(1)} %get-tuple-element.11), channel_id=1, source_target_pairs={{0,32},{32,64},{64,96},{96,128},{128,160},{160,192},{192,224},{1,3... | collective-permute-start | bytes 98312 | tf_op jit(solution)/shard_map/ppermute | solution.py:18
  90.1 10.9 %scatter_custom_fusion = f32[512,512]{1,0:T(8,128)S(1)} fusion(f32[512,512]{1,0:T(8,128)S(1)} %convert_add_fusion, s32[1536]{0:T(1024)S(1)} %copy-done.8, f32[1536,1024]{1,0:T(8,128)} %fusion.36), kind=kCustom, calls=%fused_computation.15 | custom fusion | flops 786432 | bytes 4194304 | tf_op jit(solution)/shard_map/scatter-add | solution.py:108
  103.4 6.3 %collective-permute-done.4 = bf16[32,512]{1,0:T(8,128)(2,1)S(1)} collective-permute-done((bf16[32,512]{1,0:T(8,128)(2,1)S(1)}, bf16[32,512]{1,0:T(8,128)(2,1)S(1)}, u32[]{:S(2)}, u32[]{:S(2)}) %collective-permute-start.4) | collective-permute-done | bytes 32800 | tf_op jit(solution)/shard_map/ppermute | solution.py:18
  109.7 1.6 scatter_custom_fusion.2
  112.0 220.8 %all-reduce.2.cloned.1.call-done = f32[1536,512]{1,0:T(8,128)} async-done(((f32[1536,512]{1,0:T(8,128)}), f32[1536,512]{1,0:T(8,128)}) %all-reduce.2.cloned.1.call-update) | async-done | bytes 3145744 | tf_op jit(solution)/shard_map/psum | solution.py:138
  332.8 1.5 dynamic-slice_multiply_fusion
  (90 shorter events, 17.2 us)
Async XLA Ops:
  7.2 36.8 %copy-start = (bf16[1024,512]{1,0:T(8,128)(2,1)S(1)}, bf16[1024,512]{1,0:T(8,128)(2,1)}, u32[]{:S(2)}) copy-start(bf16[1024,512]{1,0:T(8,128)(2,1)} %param.22) | copy-start | bytes 3145732
  7.2 14.2 %copy-start.6 = (s32[1536]{0:T(1024)S(1)}, s32[1536]{0:T(1024)}, u32[]{:S(2)}) copy-start(s32[1536]{0:T(1024)} %param.16) | copy-start | bytes 18436
  7.2 14.2 %copy-start.7 = (s32[1536]{0:T(1024)S(1)}, s32[1536]{0:T(1024)}, u32[]{:S(2)}) copy-start(s32[1536]{0:T(1024)} %param.17) | copy-start | bytes 18436
  7.2 14.2 %copy-start.1 = (bf16[8,64,512]{2,1,0:T(8,128)(2,1)S(1)}, bf16[8,64,512]{2,1,0:T(8,128)(2,1)}, u32[]{:S(2)}) copy-start(bf16[8,64,512]{2,1,0:T(8,128)(2,1)} %param.13) | copy-start | bytes 1572868
  7.2 325.6 %all-reduce.2.cloned.1.call-start = ((), (), s32[]{:S(2)}) async-start(), calls=%async_computation | async-start | bytes 6291456 | tf_op jit(solution)/shard_map/psum | solution.py:138
  11.2 15.0 %collective-permute-start = (bf16[32,512]{1,0:T(8,128)(2,1)}, bf16[32,512]{1,0:T(8,128)(2,1)S(1)}, u32[]{:S(2)}, u32[]{:S(2)}) collective-permute-start(bf16[32,512]{1,0:T(8,128)(2,1)} %get-tuple-element.22), channel_id=1, source_target_pairs={{0,1},{1,2},{2,3},{3,4},{4,5},{5,6},{6,7},{7,8},{8,9},{9,10},{10,1... | collective-permute-start | bytes 98312 | tf_op jit(solution)/shard_map/ppermute | solution.py:18
  11.2 15.1 %collective-permute-start.1 = (bf16[32,512]{1,0:T(8,128)(2,1)}, bf16[32,512]{1,0:T(8,128)(2,1)S(1)}, u32[]{:S(2)}, u32[]{:S(2)}) collective-permute-start(bf16[32,512]{1,0:T(8,128)(2,1)} %get-tuple-element.21), channel_id=1, source_target_pairs={{1,0},{2,1},{3,2},{4,3},{5,4},{6,5},{7,6},{8,7},{9,8},{10,9},{11,1... | collective-permute-start | bytes 98312 | tf_op jit(solution)/shard_map/ppermute | solution.py:19
  13.0 13.3 %collective-permute-start.2 = (bf16[32,512]{1,0:T(8,128)(2,1)}, bf16[32,512]{1,0:T(8,128)(2,1)S(1)}, u32[]{:S(2)}, u32[]{:S(2)}) collective-permute-start(bf16[32,512]{1,0:T(8,128)(2,1)} %get-tuple-element.20), channel_id=1, source_target_pairs={{0,32},{32,64},{64,96},{96,128},{128,160},{160,192},{192,224},{1,3... | collective-permute-start | bytes 98312 | tf_op jit(solution)/shard_map/ppermute | solution.py:18
  16.5 9.9 %collective-permute-start.3 = (bf16[32,512]{1,0:T(8,128)(2,1)}, bf16[32,512]{1,0:T(8,128)(2,1)S(1)}, u32[]{:S(2)}, u32[]{:S(2)}) collective-permute-start(bf16[32,512]{1,0:T(8,128)(2,1)} %get-tuple-element.19), channel_id=1, source_target_pairs={{32,0},{64,32},{96,64},{128,96},{160,128},{192,160},{224,192},{33,... | collective-permute-start | bytes 98312 | tf_op jit(solution)/shard_map/ppermute | solution.py:19
  31.8 4.1 %copy-start.10 = (bf16[1536,512]{1,0:T(8,128)(2,1)S(1)}, bf16[1536,512]{1,0:T(8,128)(2,1)}, u32[]{:S(2)}) copy-start(bf16[1536,512]{1,0:T(8,128)(2,1)} %param.19) | copy-start | bytes 4718596
  35.9 4.5 %copy-start.12 = (bf16[512,512]{1,0:T(8,128)(2,1)S(1)}, bf16[512,512]{1,0:T(8,128)(2,1)}, u32[]{:S(2)}) copy-start(bf16[512,512]{1,0:T(8,128)(2,1)} %param.20) | copy-start | bytes 1572868
  40.4 1.6 copy-start.16
  42.1 1.9 copy-start.2
  45.1 1.4 copy-start.4
  45.1 1.4 copy-start.5
  51.8 3.5 %copy-start.3 = (f32[1536,512]{0,1:T(8,128)S(1)}, f32[1536,512]{0,1:T(8,128)}, u32[]{:S(2)}) copy-start(f32[1536,512]{0,1:T(8,128)} %copy-done.2) | copy-start | bytes 9437188
  55.3 2.1 copy-start.17
  55.4 5.8 %slice-start = ((s8[4718592]{0:T(1024)(128)(4,1)}), s8[4194304]{0:T(1024)(128)(4,1)S(1)}, s32[]{:S(2)}) async-start(s8[4718592]{0:T(1024)(128)(4,1)} %bitcast.25), calls=%async_computation.1 | async-start | bytes 8388608
  57.4 3.8 %slice-start.1 = ((s8[4718592]{0:T(1024)(128)(4,1)}), s8[524288]{0:T(1024)(128)(4,1)S(1)}, s32[]{:S(2)}) async-start(s8[4718592]{0:T(1024)(128)(4,1)} %bitcast.25), calls=%async_computation.2 | async-start | bytes 1048576
  60.0 1.2 copy-start.14
  82.3 20.0 %collective-permute-start.7 = (bf16[32,512]{1,0:T(8,128)(2,1)S(1)}, bf16[32,512]{1,0:T(8,128)(2,1)S(1)}, u32[]{:S(2)}, u32[]{:S(2)}) collective-permute-start(bf16[32,512]{1,0:T(8,128)(2,1)S(1)} %get-tuple-element.10), channel_id=1, source_target_pairs={{32,0},{64,32},{96,64},{128,96},{160,128},{192,160},{224,192},{33,... | collective-permute-start | bytes 98312 | tf_op jit(solution)/shard_map/ppermute | solution.py:19
  83.6 18.7 %collective-permute-start.6 = (bf16[32,512]{1,0:T(8,128)(2,1)S(1)}, bf16[32,512]{1,0:T(8,128)(2,1)S(1)}, u32[]{:S(2)}, u32[]{:S(2)}) collective-permute-start(bf16[32,512]{1,0:T(8,128)(2,1)S(1)} %get-tuple-element.11), channel_id=1, source_target_pairs={{0,32},{32,64},{64,96},{96,128},{128,160},{160,192},{192,224},{1,3... | collective-permute-start | bytes 98312 | tf_op jit(solution)/shard_map/ppermute | solution.py:18
  101.8 1.6 collective-permute-start.5
  101.8 7.9 %collective-permute-start.4 = (bf16[32,512]{1,0:T(8,128)(2,1)S(1)}, bf16[32,512]{1,0:T(8,128)(2,1)S(1)}, u32[]{:S(2)}, u32[]{:S(2)}) collective-permute-start(bf16[32,512]{1,0:T(8,128)(2,1)S(1)} %get-tuple-element.9), channel_id=1, source_target_pairs={{0,1},{1,2},{2,3},{3,4},{4,5},{5,6},{6,7},{7,8},{8,9},{9,10},{10,1... | collective-permute-start | bytes 98312 | tf_op jit(solution)/shard_map/ppermute | solution.py:18
  (5 other events, 4.5 us)
Sparse Core Ops, SparseCore 0:
  65.6 267.1 all-reduce.1
where the time goes:
time: 344 us; the launch traced here: 341 us
  waiting for transfers between devices  228 us (66%)
  other arithmetic  32 us (9%)
  matrix products  28.2 us (8%)
  local copies, waits for them, and re-layouts  24.8 us (7%)
  between operations  14.5 us (4%)
  starting transfers between devices  13.5 us (4%)
    psum x1, waiting for transfers between devices, shards(): summed = lax.psum(full_grad, ('band', 'sector'))  221 us
    scatter-add x1, other arithmetic, shards(): jax.ops.segment_sum(grad_inputs[:, feature_width:], edge_dst, num_segment...  10.9 us
    unnamed x46, local copies, waits for them, and re-layouts  10.8 us
    scatter-add x1, other arithmetic, shards(): jax.ops.segment_sum(grad_inputs[:, :feature_width], edge_src, num_segment...  10.6 us
    ppermute x4, starting transfers between devices, with_halo(): before = lax.ppermute(last, axis, up)  9.15 us
  transfers between devices with their start and end apart: 9, of which 3 were waited for; matrix products, arithmetic and copies ran while one was open for 12% of the time, Pallas kernels for 0%

commit v1 on v0

v1 whole, which is shorter than its diff:
```python
import math

import jax
import jax.numpy as jnp
from jax import lax
from jax.experimental import pallas as pl
from jax.experimental.pallas import tpu as pltpu
from jax.sharding import PartitionSpec as P

EPSILON = 1e-05
BF16 = jnp.bfloat16
F32 = jnp.float32
ANY = pl.BlockSpec(memory_space=pl.ANY)
VM = pl.BlockSpec(memory_space=pltpu.VMEM)


def mm(a, b):
    return lax.dot_general(a, b, (((1,), (0,)), ((), ())), preferred_element_type=F32)


def mm_nt(a, b):
    return lax.dot_general(a, b, (((1,), (1,)), ((), ())), preferred_element_type=F32)


def mm_tn(a, b):
    return lax.dot_general(a, b, (((0,), (0,)), ((), ())), preferred_element_type=F32)


def onehot_rows(index_row, rows):
    n = index_row.shape[1]
    return (lax.broadcasted_iota(jnp.int32, (rows, n), 0) == index_row).astype(BF16)


def onehot_cols(index_col, cols):
    n = index_col.shape[0]
    return (lax.broadcasted_iota(jnp.int32, (n, cols), 1) == index_col).astype(BF16)


def column_of(index_row):
    n = index_row.shape[1]
    return jnp.transpose(jnp.broadcast_to(index_row, (8, n)))[:, 0:1]


def swish_parts(pre):
    sig = 0.5 * jnp.tanh(0.5 * pre) + 0.5
    value = pre * sig
    return value, sig + value * (1.0 - sig)


def norm_parts(raw):
    width = raw.shape[1]
    centred = raw - jnp.sum(raw, axis=1, keepdims=True) * (1.0 / width)
    spread = jnp.sum(centred * centred, axis=1, keepdims=True) * (1.0 / width)
    scale = lax.rsqrt(spread + EPSILON)
    return centred * scale, scale


def norm_back(grad, unit, scale):
    width = grad.shape[1]
    first = jnp.sum(grad, axis=1, keepdims=True) * (1.0 / width)
    second = jnp.sum(grad * unit, axis=1, keepdims=True) * (1.0 / width)
    return (grad - first - unit * second) * scale


def pick_kernel(send_ref, mesh_ref, *outs):
    rows = mesh_ref.shape[0]
    hot = onehot_rows(send_ref[...], rows)
    picked = mm_tn(hot, mesh_ref[...]).astype(BF16)
    margin = picked.shape[0] // 4
    for i, out in enumerate(outs):
        out[...] = picked[i * margin : (i + 1) * margin]


def pick(send_rows, mesh_lat):
    n, width = send_rows.shape[0], mesh_lat.shape[1]
    part = jax.ShapeDtypeStruct((n // 4, width), BF16)
    return pl.pallas_call(
        pick_kernel,
        out_shape=[part] * 4,
        in_specs=[VM, VM],
        out_specs=[VM] * 4,
        name="pick",
        cost_estimate=pl.CostEstimate(flops=2 * n * n * width, bytes_accessed=2 * n * width * 2, transcendentals=0),
    )(send_rows.reshape(1, n), mesh_lat)


TILE = 512


def early_kernel(dst_ref, grid_ref, edge_ref, w_edge_ref, w_grid_ref, w_node_ref, base_ref, node_ref, prod_ref):
    grid = grid_ref[...]
    width = grid.shape[1]
    prod_ref[...] = mm(grid, w_grid_ref[...]).astype(BF16)
    node_ref[...] = mm(grid, w_node_ref[...])
    points = grid.shape[0]
    for t in range(edge_ref.shape[0] // TILE):
        rows = slice(t * TILE, (t + 1) * TILE)
        hot = onehot_cols(column_of(dst_ref[:, rows]), points)
        base_ref[rows, :] = mm(edge_ref[rows, :], w_edge_ref[...]) + mm(hot, prod_ref[...])


def early(edge_dst, grid_block, edge_feat, w_edge1, w_node1):
    edges, width = edge_feat.shape
    points = grid_block.shape[0]
    block = lambda i: pl.BlockSpec((width, width), lambda k: (i, 0))
    return pl.pallas_call(
        early_kernel,
        out_shape=[
            jax.ShapeDtypeStruct((edges, width), F32),
            jax.ShapeDtypeStruct((points, width), F32),
        ],
        in_specs=[VM, VM, VM, block(0), block(2), block(1)],
        out_specs=[VM, VM],
        scratch_shapes=[pltpu.VMEM((points, width), BF16)],
        compiler_params=pltpu.CompilerParams(vmem_limit_bytes=40 << 20),
        grid=(1,),
        name="early",
        cost_estimate=pl.CostEstimate(
            flops=4 * edges * width * width + 4 * points * width * width,
            bytes_accessed=10 * edges * width,
            transcendentals=0,
        ),
    )(edge_dst.reshape(1, edges), grid_block, edge_feat, w_edge1, w_edge1, w_node1)


def main_kernel(
    src_ref,
    dst_ref,
    mesh_ref,
    r0_ref,
    r1_ref,
    r2_ref,
    r3_ref,
    eg_ref,
    ng_ref,
    base_hbm,
    node_hbm,
    edge_hbm,
    grid_hbm,
    cot_hbm,
    w1_hbm,
    w2_hbm,
    n1_hbm,
    n2_hbm,
    out_ref,
    dnpre_ref,
    sm_ref,
    sg_ref,
    gw_ref,
    base,
    node,
    edge,
    grid,
    cot,
    wm,
    w2,
    n1,
    n2,
    table,
    prod,
    hot_s,
    hot_d,
    hot_st,
    hot_dt,
    slope,
    unit,
    scale,
    msg,
    gp,
    sems,
):
    width = w2.shape[0]
    edges, points, rows_table = base.shape[0], grid.shape[0], table.shape[0]
    tiles = [slice(t * TILE, (t + 1) * TILE) for t in range(edges // TILE)]
    copies = [
        pltpu.make_async_copy(w1_hbm.at[pl.ds(width, width), :], wm, sems.at[0]),
        pltpu.make_async_copy(base_hbm, base, sems.at[1]),
        pltpu.make_async_copy(w2_hbm, w2, sems.at[2]),
        pltpu.make_async_copy(n1_hbm.at[pl.ds(0, width), :], n1, sems.at[3]),
        pltpu.make_async_copy(node_hbm, node, sems.at[4]),
        pltpu.make_async_copy(n2_hbm, n2, sems.at[5]),
        pltpu.make_async_copy(cot_hbm, cot, sems.at[6]),
        pltpu.make_async_copy(grid_hbm, grid, sems.at[7]),
        pltpu.make_async_copy(edge_hbm, edge, sems.at[8]),
    ]
    for copy in copies:
        copy.start()
    own, margin = mesh_ref.shape[0], r0_ref.shape[0]
    table[0:own, :] = mesh_ref[...]
    for i, part in enumerate((r0_ref, r1_ref, r2_ref, r3_ref)):
        table[own + i * margin : own + (i + 1) * margin, :] = part[...]
    hot_s[...] = onehot_cols(column_of(src_ref[...]), rows_table)
    hot_d[...] = onehot_cols(column_of(dst_ref[...]), points)
    hot_st[...] = onehot_rows(src_ref[...], rows_table)
    hot_dt[...] = onehot_rows(dst_ref[...], points)
    edge_gain, node_gain = eg_ref[...], ng_ref[...]

    copies[0].wait()
    prod[...] = mm(table[...], wm[...]).astype(BF16)
    copies[1].wait()
    copies[2].wait()
    for rows in tiles:
        pre = base[rows, :] + mm(hot_s[rows, :], prod[...])
        hidden, steep = swish_parts(pre)
        slope[rows, :] = steep
        normed, inv = norm_parts(mm(hidden.astype(BF16), w2[...]))
        unit[rows, :] = normed
        scale[rows, :] = inv
        msg[rows, :] = (normed * edge_gain).astype(BF16)
    for copy in copies[3:8]:
        copy.wait()
    agg = mm(hot_dt[...], msg[...]).astype(BF16)
    node_hidden, node_slope = swish_parts(mm(agg, n1[...]) + node[...])
    node_unit, node_inv = norm_parts(mm(node_hidden.astype(BF16), n2[...]))
    out_ref[...] = (grid[...].astype(F32) + node_unit * node_gain).astype(BF16)
    d_raw = norm_back(cot[...].astype(F32) * node_gain, node_unit, node_inv)
    d_hidden = mm_nt(d_raw.astype(BF16), n2[...]).astype(BF16).astype(F32)
    d_pre = (d_hidden * node_slope).astype(BF16)
    dnpre_ref[...] = d_pre
    d_agg = mm_nt(d_pre, n1[...]).astype(BF16)
    for rows in tiles:
        d_msg = mm(hot_d[rows, :], d_agg)
        d_edge = norm_back(d_msg * edge_gain, unit[rows, :], scale[rows, :])
        d_hid = mm_nt(d_edge.astype(BF16), w2[...]).astype(BF16).astype(F32)
        gp[rows, :] = (d_hid * slope[rows, :]).astype(BF16)
    copies[8].wait()
    gw_ref[0:width, :] = mm_tn(edge[...], gp[...]).astype(BF16)
    sm = mm(hot_st[...], gp[...]).astype(BF16)
    sm_ref[...] = sm
    gw_ref[width : 2 * width, :] = mm_tn(table[...], sm).astype(BF16)
    sg = mm(hot_dt[...], gp[...]).astype(BF16)
    sg_ref[...] = sg
    gw_ref[2 * width : 3 * width, :] = mm_tn(grid[...], sg).astype(BF16)


def main(edge_src, edge_dst, mesh_lat, received, edge_gain, node_gain, base, node, edge_feat, grid_block, cot_block, w1, w2, n1, n2):
    edges, width = edge_feat.shape
    points = grid_block.shape[0]
    table = mesh_lat.shape[0] + 4 * received[0].shape[0]
    sds = jax.ShapeDtypeStruct
    square = pltpu.VMEM((width, width), BF16)
    nodes = pltpu.VMEM((points, width), BF16)
    return pl.pallas_call(
        main_kernel,
        out_shape=[
            sds((points, width), BF16),
            sds((points, width), BF16),
            sds((table, width), BF16),
            sds((points, width), BF16),
            sds((3 * width, width), BF16),
        ],
        in_specs=[VM] * 9 + [ANY] * 9,
        out_specs=[VM] * 5,
        scratch_shapes=[
            pltpu.VMEM((edges, width), F32),
            pltpu.VMEM((points, width), F32),
            pltpu.VMEM((edges, width), BF16),
            nodes,
            nodes,
            square,
            square,
            square,
            square,
            pltpu.VMEM((table, width), BF16),
            pltpu.VMEM((table, width), BF16),
            pltpu.VMEM((edges, table), BF16),
            pltpu.VMEM((edges, points), BF16),
            pltpu.VMEM((table, edges), BF16),
            pltpu.VMEM((points, edges), BF16),
            pltpu.VMEM((edges, width), F32),
            pltpu.VMEM((edges, width), F32),
            pltpu.VMEM((edges, 1), F32),
            pltpu.VMEM((edges, width), BF16),
            pltpu.VMEM((edges, width), BF16),
            pltpu.SemaphoreType.DMA((9,)),
        ],
        compiler_params=pltpu.CompilerParams(vmem_limit_bytes=56 << 20),
        name="main",
        cost_estimate=pl.CostEstimate(
            flops=16 * edges * width * width,
            bytes_accessed=14 * edges * width,
            transcendentals=edges * width,
        ),
    )(
        edge_src.reshape(1, edges),
        edge_dst.reshape(1, edges),
        mesh_lat,
        *received,
        edge_gain.reshape(1, width),
        node_gain.reshape(1, width),
        base,
        node,
        edge_feat,
        grid_block,
        cot_block,
        w1,
        w2,
        n1,
        n2,
    )


def table_kernel(sm_ref, w_ref, own_ref, *outs):
    grad = mm_nt(sm_ref[...], w_ref[...])
    own, margin = own_ref.shape[0], outs[0].shape[0]
    own_ref[...] = grad[0:own]
    for i, out in enumerate(outs):
        out[...] = grad[own + i * margin : own + (i + 1) * margin].astype(BF16)


def table_grads(sm, w1, own, margin):
    width = sm.shape[1]
    sds = jax.ShapeDtypeStruct
    return pl.pallas_call(
        table_kernel,
        out_shape=[sds((own, width), F32)] + [sds((margin, width), BF16)] * 4,
        in_specs=[VM, pl.BlockSpec((width, width), lambda k: (1, 0))],
        out_specs=[VM] * 5,
        grid=(1,),
        name="table_grads",
        cost_estimate=pl.CostEstimate(flops=2 * sm.shape[0] * width * width, bytes_accessed=1 << 20, transcendentals=0),
    )(sm, w1)


def grid_kernel(sg_ref, w1_ref, dnpre_ref, n1_ref, cot_ref, out_ref):
    total = cot_ref[...].astype(F32) + mm_nt(dnpre_ref[...], n1_ref[...]) + mm_nt(sg_ref[...], w1_ref[...])
    out_ref[...] = total.astype(BF16)


def grid_grads(sg, w1, dnpre, n1, cot_block):
    points, width = sg.shape
    return pl.pallas_call(
        grid_kernel,
        out_shape=jax.ShapeDtypeStruct((points, width), BF16),
        in_specs=[VM, pl.BlockSpec((width, width), lambda k: (2, 0)), VM, pl.BlockSpec((width, width), lambda k: (1, 0)), VM],
        out_specs=VM,
        grid=(1,),
        name="grid_grads",
        cost_estimate=pl.CostEstimate(flops=4 * points * width * width, bytes_accessed=3 << 20, transcendentals=0),
    )(sg, w1, dnpre, n1, cot_block)


def mesh_kernel(send_ref, own_ref, r0_ref, r1_ref, r2_ref, r3_ref, out_ref):
    own = own_ref.shape[0]
    hot = onehot_rows(send_ref[...], own)
    margin = r0_ref.shape[0]
    total = own_ref[...]
    for i, part in enumerate((r0_ref, r1_ref, r2_ref, r3_ref)):
        total = total + mm(hot[:, i * margin : (i + 1) * margin], part[...])
    out_ref[...] = total.astype(BF16)


def mesh_grads(send_rows, own, returned):
    n = send_rows.shape[0]
    return pl.pallas_call(
        mesh_kernel,
        out_shape=jax.ShapeDtypeStruct(own.shape, BF16),
        in_specs=[VM] * 6,
        out_specs=VM,
        name="mesh_grads",
        cost_estimate=pl.CostEstimate(flops=2 * n * n * own.shape[1], bytes_accessed=1 << 19, transcendentals=0),
    )(send_rows.reshape(1, n), own, *returned)


def steps(axis, wrap):
    devices = lax.axis_size(axis)
    up = [(i, (i + 1) % devices) for i in range(devices if wrap else devices - 1)]
    return up, [(j, i) for i, j in up]


def swap(parts):
    sector_up, sector_down = steps("sector", True)
    band_up, band_down = steps("band", False)
    return [
        lax.ppermute(parts[1], "sector", sector_up),
        lax.ppermute(parts[0], "sector", sector_down),
        lax.ppermute(parts[3], "band", band_up),
        lax.ppermute(parts[2], "band", band_down),
    ]


def reduce_weights(gw):
    sectors = lax.axis_size("sector")
    parts = lax.all_to_all(gw.reshape(sectors, gw.shape[0] // sectors, gw.shape[1]), "sector", 0, 0)
    part = jnp.sum(parts.astype(F32), axis=0).astype(BF16)
    bands = lax.axis_size("band")
    others = [lax.ppermute(part, "band", [(i, i ^ d) for i in range(bands)]) for d in range(1, bands)]
    total = part.astype(F32)
    for other in others:
        total = total + other.astype(F32)
    return total


def shards(
    grid_lat,
    mesh_lat,
    edge_feat,
    edge_src,
    edge_dst,
    send_rows,
    w_edge1,
    w_edge2,
    edge_gain,
    w_node1,
    w_node2,
    node_gain,
    cotangent,
):
    lat_rows, lon_cols, width = grid_lat.shape
    grid_block = grid_lat.reshape(lat_rows * lon_cols, width)
    cot_block = cotangent.reshape(lat_rows * lon_cols, width)
    own, margin = mesh_lat.shape[0], send_rows.shape[0] // 4
    received = swap(pick(send_rows, mesh_lat))
    base, node = early(edge_dst, grid_block, edge_feat, w_edge1, w_node1)
    result, dnpre, sm, sg, gw = main(
        edge_src, edge_dst, mesh_lat, received, edge_gain, node_gain, base, node, edge_feat, grid_block, cot_block, w_edge1, w_edge2, w_node1, w_node2
    )
    own_grad, *borrowed = table_grads(sm, w_edge1, own, margin)
    returned = swap(borrowed)
    grad_grid = grid_grads(sg, w_edge1, dnpre, w_node1, cot_block)
    grad_mesh = mesh_grads(send_rows, own_grad, returned)
    total_edges = edge_feat.shape[0] * lax.axis_size("band") * lax.axis_size("sector")
    grad_w = reduce_weights(gw) * (1.0 / math.sqrt(total_edges))
    return (
        result.reshape(lat_rows, lon_cols, width),
        grad_grid.reshape(lat_rows, lon_cols, width),
        grad_mesh,
        grad_w,
    )


def solution(mesh):
    rows = P(("band", "sector"), None)
    flat = P(("band", "sector"))
    grid = P("band", "sector", None)
    in_specs = (grid, rows, rows, flat, flat, flat, P(), P(), P(), P(), P(), P(), grid)
    out_specs = (grid, grid, rows, P("sector", None))
    return jax.shard_map(shards, mesh=mesh, in_specs=in_specs, out_specs=out_specs, check_vma=False)
```

time: 344 us -> 117 us (0.34)
  waiting for transfers between devices: 228 us -> 39.4 us
  other arithmetic: 32 us -> 0.93 us
  matrix products: 28.2 us -> 0 us
  Pallas kernels: 0 us -> 26.5 us
  starting transfers between devices: 13.5 us -> 39 us
  local copies, waits for them, and re-layouts: 24.8 us -> 9.65 us
  between operations: 14.5 us -> 0.86 us
    psum x1 -> x0, waiting for transfers between devices: 221 us -> none  [shards(): summed = lax.psum(full_grad, ('band', 'sector'))]
    all_to_all x0 -> x1, waiting for transfers between devices: none -> 39.3 us  [reduce_weights(): lax.all_to_all(gw.reshape(sectors, gw.shape[0] // sectors, gw.shape[1]),...]
    dot_general x10 -> x0, matrix products: 28.2 us -> none  [the longest x1 6.2 us: shards(): lax.dot_general(grad_pre_b, w_edge1[feature_width:], (((1,), (1,)), ((),...]
    pallas_call x0 -> x6, Pallas kernels: none -> 26.5 us  [the longest x1 15 us: main(): pl.pallas_call(main_kernel, out_shape=[sds((points, width), BF16), sds((p...]
    scatter-add x3 -> x0, other arithmetic: 23.1 us -> none  [the longest x1 10.9 us: shards(): jax.ops.segment_sum(grad_inputs[:, feature_width:], edge_dst, num_segment...]
    ppermute x8 -> x15, starting transfers between devices: 13.5 us -> 26.6 us  [the longest x7 17.2 us: reduce_weights(): lax.ppermute(part, 'band', [(i, i ^ d) for i in range(bands)])]
    all_to_all x0 -> x1, starting transfers between devices: none -> 12.4 us  [reduce_weights(): lax.all_to_all(gw.reshape(sectors, gw.shape[0] // sectors, gw.shape[1]),...]
    gather x3 -> x0, local copies, waits for them, and re-layouts: 12 us -> none  [the longest x1 5.43 us: shards(): mesh_table[edge_src]]
  transfers between devices with their start and end apart: 9 -> 16, of which waited for: 3 -> 1; matrix products, arithmetic and copies ran while one was open for 12% -> 1% of each run, Pallas kernels for 0% -> 8%
where the time goes in v1:
time: 117 us; the launch traced here: 116 us
  waiting for transfers between devices  39.4 us (34%)
  starting transfers between devices  39 us (33%)
  Pallas kernels  26.5 us (23%)
  local copies, waits for them, and re-layouts  9.65 us (8%)
    all_to_all x1, waiting for transfers between devices, reduce_weights(): lax.all_to_all(gw.reshape(sectors, gw.shape[0] // sectors, gw.shape[1]),...  39.3 us
    ppermute x7, starting transfers between devices, reduce_weights(): lax.ppermute(part, 'band', [(i, i ^ d) for i in range(bands)])  17.2 us
    pallas_call x1, Pallas kernels, main(): pl.pallas_call(main_kernel, out_shape=[sds((points, width), BF16), sds((p...  15 us
    all_to_all x1, starting transfers between devices, reduce_weights(): lax.all_to_all(gw.reshape(sectors, gw.shape[0] // sectors, gw.shape[1]),...  12.4 us
    unnamed x38, local copies, waits for them, and re-layouts  8.35 us
    ppermute x2, starting transfers between devices, swap(): lax.ppermute(parts[3], 'band', band_up)  4.83 us
    pallas_call x1, Pallas kernels, grid_grads(): pl.pallas_call(grid_kernel, out_shape=jax.ShapeDtypeStruct((points, width...  3.2 us
    ppermute x2, starting transfers between devices, swap(): lax.ppermute(parts[2], 'band', band_down)  2.58 us
  transfers between devices with their start and end apart: 16, of which 1 were waited for; matrix products, arithmetic and copies ran while one was open for 1% of the time, Pallas kernels for 8%

profile of v1, /device:TPU:32, one launch (start us, length us, event | category | flops | bytes accessed | tf_op | source)
XLA Modules:
  0.0 116.3 jit_solution(13117536444168567987)
XLA Ops:
  0.6 1.8 %pick.1 = (bf16[32,512]{1,0:T(8,128)(2,1)}, bf16[32,512]{1,0:T(8,128)(2,1)}, bf16[32,512]{1,0:T(8,128)(2,1)}, bf16[32,512]{1,0:T(8,128)(2,1)}) custom-call(s32[1,128]{1,0:T(1,128)} %bitcast.14, bf16[128,512]{1,0:T(8,128)(2,1)} %mesh_ref.3), custom_call_target="tpu_custom_call" | custom-call | flops 16777216 | bytes 262144 | tf_op jit(solution)/shard_map/pick/pallas_call | solution.py:77
  2.4 1.7 %collective-permute-start.1 = (bf16[32,512]{1,0:T(8,128)(2,1)}, bf16[32,512]{1,0:T(8,128)(2,1)S(1)}, u32[]{:S(2)}, u32[]{:S(2)}) collective-permute-start(bf16[32,512]{1,0:T(8,128)(2,1)} %get-tuple-element.21), channel_id=1, source_target_pairs={{1,0},{2,1},{3,2},{4,3},{5,4},{6,5},{7,6},{8,7},{9,8},{10,9},{11,1... | collective-permute-start | bytes 98312 | tf_op jit(solution)/shard_map/ppermute | solution.py:376
  4.1 3.5 %collective-permute-start.2 = (bf16[32,512]{1,0:T(8,128)(2,1)}, bf16[32,512]{1,0:T(8,128)(2,1)S(1)}, u32[]{:S(2)}, u32[]{:S(2)}) collective-permute-start(bf16[32,512]{1,0:T(8,128)(2,1)} %get-tuple-element.22), channel_id=1, source_target_pairs={{0,32},{32,64},{64,96},{96,128},{128,160},{160,192},{192,224},{1,3... | collective-permute-start | bytes 98312 | tf_op jit(solution)/shard_map/ppermute | solution.py:377
  7.6 1.3 %collective-permute-start.3 = (bf16[32,512]{1,0:T(8,128)(2,1)}, bf16[32,512]{1,0:T(8,128)(2,1)S(1)}, u32[]{:S(2)}, u32[]{:S(2)}) collective-permute-start(bf16[32,512]{1,0:T(8,128)(2,1)} %get-tuple-element.23), channel_id=1, source_target_pairs={{32,0},{64,32},{96,64},{128,96},{160,128},{192,160},{224,192},{33,... | collective-permute-start | bytes 98312 | tf_op jit(solution)/shard_map/ppermute | solution.py:378
  9.6 1.4 %copy-done = bf16[1536,512]{1,0:T(8,128)(2,1)S(1)} copy-done((bf16[1536,512]{1,0:T(8,128)(2,1)S(1)}, bf16[1536,512]{1,0:T(8,128)(2,1)}, u32[]{:S(2)}) %copy-start) | copy-done | bytes 1572888
  11.0 1.2 %copy-done.1 = bf16[1024,512]{1,0:T(8,128)(2,1)S(1)} copy-done((bf16[1024,512]{1,0:T(8,128)(2,1)S(1)}, bf16[1024,512]{1,0:T(8,128)(2,1)}, u32[]{:S(2)}) %copy-start.1) | copy-done | bytes 1048600
  12.3 1.4 %copy-done.3 = bf16[1536,512]{1,0:T(8,128)(2,1)S(1)} copy-done((bf16[1536,512]{1,0:T(8,128)(2,1)S(1)}, bf16[1536,512]{1,0:T(8,128)(2,1)}, u32[]{:S(2)}) %copy-start.3) | copy-done | bytes 1572888
  13.7 1.0 copy-done.4
  14.7 2.4 %early.1 = (f32[1536,512]{1,0:T(8,128)S(1)}, f32[512,512]{1,0:T(8,128)S(1)}) custom-call(s32[1,1536]{1,0:T(1,128)S(1)} %reshape.41.dst_ref, bf16[512,512]{1,0:T(8,128)(2,1)S(1)} %bitcast.9, bf16[1536,512]{1,0:T(8,128)(2,1)S(1)} %copy-done.3, bf16[1536,512]{1,0:T(8,128)(2,1)S(1)} %copy-done, bf16[1536,512]{1,0:T(8,128)(2,1)S(1)} %copy-done, ...), custom_call_target="tpu_custom_call" | custom-call | flops 2147483648 | bytes 7864320 | tf_op jit(solution)/shard_map/early/pallas_call | solution.py:106
  17.1 1.6 %copy-done.5 = f32[1536,512]{1,0:T(8,128)} copy-done((f32[1536,512]{1,0:T(8,128)}, f32[1536,512]{1,0:T(8,128)S(1)}, u32[]{:S(2)}) %copy-start.5) | copy-done | bytes 3145752
  18.8 1.0 copy-done.6
  21.0 15.0 %main.1 = (bf16[512,512]{1,0:T(8,128)(2,1)}, bf16[512,512]{1,0:T(8,128)(2,1)}, bf16[256,512]{1,0:T(8,128)(2,1)}, bf16[512,512]{1,0:T(8,128)(2,1)}, bf16[1536,512]{1,0:T(8,128)(2,1)}) custom-call(s32[1,1536]{1,0:T(1,128)} %reshape.40.src_ref, s32[1,1536]{1,0:T(1,128)} %copy-done.2, bf16[128,512]{1,0:T(8,128)(2,1)} %mesh_ref.3, bf16[32,512]{1,0:T(8,128)(2,1)} %copy-done.14, ...), custom_call_target="tpu_custom_call" | custom-call | flops 6442450944 | bytes 11010048 | tf_op jit(solution)/shard_map/main/pallas_call | solution.py:243
  36.1 12.4 %all-to-all-start = ((bf16[32,48,512]{2,1,0:T(8,128)(2,1)}), bf16[32,48,512]{2,1,0:T(8,128)(2,1)S(1)}, u32[]{:S(2)}, u32[]{:S(2)}) async-start(bf16[32,48,512]{2,1,0:T(8,128)(2,1)} %bitcast.10), calls=%async_computation | async-start | bytes 3145728 | tf_op jit(solution)/shard_map/all_to_all | solution.py:384
  48.5 2.2 %table_grads.1 = (f32[128,512]{1,0:T(8,128)}, bf16[32,512]{1,0:T(8,128)(2,1)}, bf16[32,512]{1,0:T(8,128)(2,1)}, bf16[32,512]{1,0:T(8,128)(2,1)}, bf16[32,512]{1,0:T(8,128)(2,1)}) custom-call(bf16[256,512]{1,0:T(8,128)(2,1)} %get-tuple-element.29.sm_ref, bf16[1536,512]{1,0:T(8,128)(2,1)} %w_ref.1), custom_call_target="tpu_custom_call" | custom-call | flops 134217728 | bytes 1048576 | tf_op jit(solution)/shard_map/table_grads/pallas_call | solution.py:314
  50.9 39.3 %all-to-all-done = bf16[32,48,512]{2,1,0:T(8,128)(2,1)S(1)} async-done(((bf16[32,48,512]{2,1,0:T(8,128)(2,1)}), bf16[32,48,512]{2,1,0:T(8,128)(2,1)S(1)}, u32[]{:S(2)}, u32[]{:S(2)}) %all-to-all-start) | async-done | bytes 1572896 | tf_op jit(solution)/shard_map/all_to_all | solution.py:384
  90.4 4.2 %collective-permute-start.14 = (bf16[48,512]{1,0:T(8,128)(2,1)S(1)}, bf16[48,512]{1,0:T(8,128)(2,1)S(1)}, u32[]{:S(2)}, u32[]{:S(2)}) collective-permute-start(bf16[48,512]{1,0:T(8,128)(2,1)S(1)} %reduce_sum.12), channel_id=1, source_target_pairs={{0,224},{32,192},{64,160},{96,128},{128,96},{160,64},{192,32},{224... | collective-permute-start | bytes 147464 | tf_op jit(solution)/shard_map/ppermute | solution.py:387
  94.6 1.5 %collective-permute-start.13 = (bf16[48,512]{1,0:T(8,128)(2,1)S(1)}, bf16[48,512]{1,0:T(8,128)(2,1)S(1)}, u32[]{:S(2)}, u32[]{:S(2)}) collective-permute-start(bf16[48,512]{1,0:T(8,128)(2,1)S(1)} %reduce_sum.12), channel_id=1, source_target_pairs={{0,192},{32,224},{64,128},{96,160},{128,64},{160,96},{192,0},{224,... | collective-permute-start | bytes 147464 | tf_op jit(solution)/shard_map/ppermute | solution.py:387
  96.1 1.4 %collective-permute-start.6 = (bf16[32,512]{1,0:T(8,128)(2,1)S(1)}, bf16[32,512]{1,0:T(8,128)(2,1)S(1)}, u32[]{:S(2)}, u32[]{:S(2)}) collective-permute-start(bf16[32,512]{1,0:T(8,128)(2,1)S(1)} %copy-done.13), channel_id=1, source_target_pairs={{0,32},{32,64},{64,96},{96,128},{128,160},{160,192},{192,224},{1,3... | collective-permute-start | bytes 98312 | tf_op jit(solution)/shard_map/ppermute | solution.py:377
  97.5 1.3 %collective-permute-start.7 = (bf16[32,512]{1,0:T(8,128)(2,1)S(1)}, bf16[32,512]{1,0:T(8,128)(2,1)S(1)}, u32[]{:S(2)}, u32[]{:S(2)}) collective-permute-start(bf16[32,512]{1,0:T(8,128)(2,1)S(1)} %copy-done.12), channel_id=1, source_target_pairs={{32,0},{64,32},{96,64},{128,96},{160,128},{192,160},{224,192},{33,... | collective-permute-start | bytes 98312 | tf_op jit(solution)/shard_map/ppermute | solution.py:378
  98.9 5.9 %collective-permute-start.12 = (bf16[48,512]{1,0:T(8,128)(2,1)S(1)}, bf16[48,512]{1,0:T(8,128)(2,1)S(1)}, u32[]{:S(2)}, u32[]{:S(2)}) collective-permute-start(bf16[48,512]{1,0:T(8,128)(2,1)S(1)} %reduce_sum.12), channel_id=1, source_target_pairs={{0,160},{32,128},{64,224},{96,192},{128,32},{160,0},{192,96},{224,... | collective-permute-start | bytes 147464 | tf_op jit(solution)/shard_map/ppermute | solution.py:387
  105.0 4.4 %collective-permute-start.10 = (bf16[48,512]{1,0:T(8,128)(2,1)S(1)}, bf16[48,512]{1,0:T(8,128)(2,1)S(1)}, u32[]{:S(2)}, u32[]{:S(2)}) collective-permute-start(bf16[48,512]{1,0:T(8,128)(2,1)S(1)} %reduce_sum.12), channel_id=1, source_target_pairs={{0,96},{32,64},{64,32},{96,0},{128,224},{160,192},{192,160},{224,1... | collective-permute-start | bytes 147464 | tf_op jit(solution)/shard_map/ppermute | solution.py:387
  109.4 0.9 collective-permute-start.8
  110.4 3.2 %grid_grads.1 = bf16[512,512]{1,0:T(8,128)(2,1)} custom-call(bf16[512,512]{1,0:T(8,128)(2,1)} %get-tuple-element.27.sg_ref, bf16[1536,512]{1,0:T(8,128)(2,1)} %w_ref.1, bf16[512,512]{1,0:T(8,128)(2,1)} %get-tuple-element.28.dnpre_ref, bf16[1024,512]{1,0:T(8,128)(2,1)} %n1_ref.1, bf16[512,512]{1,0:T(8,128)(2,1)} %bitcast.12), custom_call_target="tpu_custom_call" | custom-call | flops 536870912 | bytes 3145728 | tf_op jit(solution)/shard_map/grid_grads/pallas_call | solution.py:332
  113.6 1.9 %mesh_grads.1 = bf16[128,512]{1,0:T(8,128)(2,1)} custom-call(s32[1,128]{1,0:T(1,128)} %bitcast.15, f32[128,512]{1,0:T(8,128)} %get-tuple-element.30.own_ref, bf16[32,512]{1,0:T(8,128)(2,1)} %copy-done.7, bf16[32,512]{1,0:T(8,128)(2,1)} %copy-done.8, bf16[32,512]{1,0:T(8,128)(2,1)} %copy-done.9, bf16[32,512]{1,0:T(8,128)(2,1)} %copy-done.10), custom_call_target="tpu_custom_call" | custom-call | flops 16777216 | bytes 524288 | tf_op jit(solution)/shard_map/mesh_grads/pallas_call | solution.py:355
  (56 shorter events, 3.4 us)
Async XLA Ops:
  2.4 18.0 %collective-permute-start = (bf16[32,512]{1,0:T(8,128)(2,1)}, bf16[32,512]{1,0:T(8,128)(2,1)S(1)}, u32[]{:S(2)}, u32[]{:S(2)}) collective-permute-start(bf16[32,512]{1,0:T(8,128)(2,1)} %get-tuple-element.20), channel_id=1, source_target_pairs={{0,1},{1,2},{2,3},{3,4},{4,5},{5,6},{6,7},{7,8},{8,9},{9,10},{10,1... | collective-permute-start | bytes 98312 | tf_op jit(solution)/shard_map/ppermute | solution.py:375
  2.4 18.0 %collective-permute-start.1 = (bf16[32,512]{1,0:T(8,128)(2,1)}, bf16[32,512]{1,0:T(8,128)(2,1)S(1)}, u32[]{:S(2)}, u32[]{:S(2)}) collective-permute-start(bf16[32,512]{1,0:T(8,128)(2,1)} %get-tuple-element.21), channel_id=1, source_target_pairs={{1,0},{2,1},{3,2},{4,3},{5,4},{6,5},{7,6},{8,7},{9,8},{10,9},{11,1... | collective-permute-start | bytes 98312 | tf_op jit(solution)/shard_map/ppermute | solution.py:376
  4.1 16.3 %collective-permute-start.2 = (bf16[32,512]{1,0:T(8,128)(2,1)}, bf16[32,512]{1,0:T(8,128)(2,1)S(1)}, u32[]{:S(2)}, u32[]{:S(2)}) collective-permute-start(bf16[32,512]{1,0:T(8,128)(2,1)} %get-tuple-element.22), channel_id=1, source_target_pairs={{0,32},{32,64},{64,96},{96,128},{128,160},{160,192},{192,224},{1,3... | collective-permute-start | bytes 98312 | tf_op jit(solution)/shard_map/ppermute | solution.py:377
  7.6 12.8 %collective-permute-start.3 = (bf16[32,512]{1,0:T(8,128)(2,1)}, bf16[32,512]{1,0:T(8,128)(2,1)S(1)}, u32[]{:S(2)}, u32[]{:S(2)}) collective-permute-start(bf16[32,512]{1,0:T(8,128)(2,1)} %get-tuple-element.23), channel_id=1, source_target_pairs={{32,0},{64,32},{96,64},{128,96},{160,128},{192,160},{224,192},{33,... | collective-permute-start | bytes 98312 | tf_op jit(solution)/shard_map/ppermute | solution.py:378
  9.6 7.5 %copy-start.2 = (s32[1,1536]{1,0:T(1,128)}, s32[1,1536]{1,0:T(1,128)S(1)}, u32[]{:S(2)}) copy-start(s32[1,1536]{1,0:T(1,128)S(1)} %reshape.41.dst_ref) | copy-start | bytes 18436
  36.1 54.1 %all-to-all-start = ((bf16[32,48,512]{2,1,0:T(8,128)(2,1)}), bf16[32,48,512]{2,1,0:T(8,128)(2,1)S(1)}, u32[]{:S(2)}, u32[]{:S(2)}) async-start(bf16[32,48,512]{2,1,0:T(8,128)(2,1)} %bitcast.10), calls=%async_computation | async-start | bytes 3145728 | tf_op jit(solution)/shard_map/all_to_all | solution.py:384
  50.6 45.5 %copy-start.15 = (bf16[32,512]{1,0:T(8,128)(2,1)S(1)}, bf16[32,512]{1,0:T(8,128)(2,1)}, u32[]{:S(2)}) copy-start(bf16[32,512]{1,0:T(8,128)(2,1)} %get-tuple-element.32) | copy-start | bytes 98308
  50.6 45.5 %copy-start.13 = (bf16[32,512]{1,0:T(8,128)(2,1)S(1)}, bf16[32,512]{1,0:T(8,128)(2,1)}, u32[]{:S(2)}) copy-start(bf16[32,512]{1,0:T(8,128)(2,1)} %get-tuple-element.33) | copy-start | bytes 98308
  50.6 46.9 %copy-start.12 = (bf16[32,512]{1,0:T(8,128)(2,1)S(1)}, bf16[32,512]{1,0:T(8,128)(2,1)}, u32[]{:S(2)}) copy-start(bf16[32,512]{1,0:T(8,128)(2,1)} %get-tuple-element.34) | copy-start | bytes 98308
  50.7 46.9 %collective-permute-start.4 = (bf16[32,512]{1,0:T(8,128)(2,1)}, bf16[32,512]{1,0:T(8,128)(2,1)S(1)}, u32[]{:S(2)}, u32[]{:S(2)}) collective-permute-start(bf16[32,512]{1,0:T(8,128)(2,1)} %get-tuple-element.31), channel_id=1, source_target_pairs={{0,1},{1,2},{2,3},{3,4},{4,5},{5,6},{6,7},{7,8},{8,9},{9,10},{10,1... | collective-permute-start | bytes 98312 | tf_op jit(solution)/shard_map/ppermute | solution.py:375
  90.4 19.0 %collective-permute-start.14 = (bf16[48,512]{1,0:T(8,128)(2,1)S(1)}, bf16[48,512]{1,0:T(8,128)(2,1)S(1)}, u32[]{:S(2)}, u32[]{:S(2)}) collective-permute-start(bf16[48,512]{1,0:T(8,128)(2,1)S(1)} %reduce_sum.12), channel_id=1, source_target_pairs={{0,224},{32,192},{64,160},{96,128},{128,96},{160,64},{192,32},{224... | collective-permute-start | bytes 147464 | tf_op jit(solution)/shard_map/ppermute | solution.py:387
  94.6 14.8 %collective-permute-start.13 = (bf16[48,512]{1,0:T(8,128)(2,1)S(1)}, bf16[48,512]{1,0:T(8,128)(2,1)S(1)}, u32[]{:S(2)}, u32[]{:S(2)}) collective-permute-start(bf16[48,512]{1,0:T(8,128)(2,1)S(1)} %reduce_sum.12), channel_id=1, source_target_pairs={{0,192},{32,224},{64,128},{96,160},{128,64},{160,96},{192,0},{224,... | collective-permute-start | bytes 147464 | tf_op jit(solution)/shard_map/ppermute | solution.py:387
  96.1 2.7 %collective-permute-start.5 = (bf16[32,512]{1,0:T(8,128)(2,1)S(1)}, bf16[32,512]{1,0:T(8,128)(2,1)S(1)}, u32[]{:S(2)}, u32[]{:S(2)}) collective-permute-start(bf16[32,512]{1,0:T(8,128)(2,1)S(1)} %copy-done.15), channel_id=1, source_target_pairs={{1,0},{2,1},{3,2},{4,3},{5,4},{6,5},{7,6},{8,7},{9,8},{10,9},{11,1... | collective-permute-start | bytes 98312 | tf_op jit(solution)/shard_map/ppermute | solution.py:376
  96.1 8.6 %collective-permute-start.6 = (bf16[32,512]{1,0:T(8,128)(2,1)S(1)}, bf16[32,512]{1,0:T(8,128)(2,1)S(1)}, u32[]{:S(2)}, u32[]{:S(2)}) collective-permute-start(bf16[32,512]{1,0:T(8,128)(2,1)S(1)} %copy-done.13), channel_id=1, source_target_pairs={{0,32},{32,64},{64,96},{96,128},{128,160},{160,192},{192,224},{1,3... | collective-permute-start | bytes 98312 | tf_op jit(solution)/shard_map/ppermute | solution.py:377
  97.5 16.0 %copy-start.7 = (bf16[32,512]{1,0:T(8,128)(2,1)}, bf16[32,512]{1,0:T(8,128)(2,1)S(1)}, u32[]{:S(2)}) copy-start(bf16[32,512]{1,0:T(8,128)(2,1)S(1)} %collective-permute-done.4.r0_ref) | copy-start | bytes 98308
  97.5 7.4 %collective-permute-start.7 = (bf16[32,512]{1,0:T(8,128)(2,1)S(1)}, bf16[32,512]{1,0:T(8,128)(2,1)S(1)}, u32[]{:S(2)}, u32[]{:S(2)}) collective-permute-start(bf16[32,512]{1,0:T(8,128)(2,1)S(1)} %copy-done.12), channel_id=1, source_target_pairs={{32,0},{64,32},{96,64},{128,96},{160,128},{192,160},{224,192},{33,... | collective-permute-start | bytes 98312 | tf_op jit(solution)/shard_map/ppermute | solution.py:378
  98.9 14.7 %copy-start.8 = (bf16[32,512]{1,0:T(8,128)(2,1)}, bf16[32,512]{1,0:T(8,128)(2,1)S(1)}, u32[]{:S(2)}) copy-start(bf16[32,512]{1,0:T(8,128)(2,1)S(1)} %collective-permute-done.5.r1_ref) | copy-start | bytes 98308
  98.9 16.6 %collective-permute-start.12 = (bf16[48,512]{1,0:T(8,128)(2,1)S(1)}, bf16[48,512]{1,0:T(8,128)(2,1)S(1)}, u32[]{:S(2)}, u32[]{:S(2)}) collective-permute-start(bf16[48,512]{1,0:T(8,128)(2,1)S(1)} %reduce_sum.12), channel_id=1, source_target_pairs={{0,160},{32,128},{64,224},{96,192},{128,32},{160,0},{192,96},{224,... | collective-permute-start | bytes 147464 | tf_op jit(solution)/shard_map/ppermute | solution.py:387
  104.7 8.8 %copy-start.9 = (bf16[32,512]{1,0:T(8,128)(2,1)}, bf16[32,512]{1,0:T(8,128)(2,1)S(1)}, u32[]{:S(2)}) copy-start(bf16[32,512]{1,0:T(8,128)(2,1)S(1)} %collective-permute-done.6.r2_ref) | copy-start | bytes 98308
  104.7 10.8 %collective-permute-start.11 = (bf16[48,512]{1,0:T(8,128)(2,1)S(1)}, bf16[48,512]{1,0:T(8,128)(2,1)S(1)}, u32[]{:S(2)}, u32[]{:S(2)}) collective-permute-start(bf16[48,512]{1,0:T(8,128)(2,1)S(1)} %reduce_sum.12), channel_id=1, source_target_pairs={{0,128},{32,160},{64,192},{96,224},{128,0},{160,32},{192,64},{224,... | collective-permute-start | bytes 147464 | tf_op jit(solution)/shard_map/ppermute | solution.py:387
  105.0 8.6 %copy-start.10 = (bf16[32,512]{1,0:T(8,128)(2,1)}, bf16[32,512]{1,0:T(8,128)(2,1)S(1)}, u32[]{:S(2)}) copy-start(bf16[32,512]{1,0:T(8,128)(2,1)S(1)} %collective-permute-done.7.r3_ref) | copy-start | bytes 98308
  105.0 10.5 %collective-permute-start.10 = (bf16[48,512]{1,0:T(8,128)(2,1)S(1)}, bf16[48,512]{1,0:T(8,128)(2,1)S(1)}, u32[]{:S(2)}, u32[]{:S(2)}) collective-permute-start(bf16[48,512]{1,0:T(8,128)(2,1)S(1)} %reduce_sum.12), channel_id=1, source_target_pairs={{0,96},{32,64},{64,32},{96,0},{128,224},{160,192},{192,160},{224,1... | collective-permute-start | bytes 147464 | tf_op jit(solution)/shard_map/ppermute | solution.py:387
  109.4 6.1 %collective-permute-start.9 = (bf16[48,512]{1,0:T(8,128)(2,1)S(1)}, bf16[48,512]{1,0:T(8,128)(2,1)S(1)}, u32[]{:S(2)}, u32[]{:S(2)}) collective-permute-start(bf16[48,512]{1,0:T(8,128)(2,1)S(1)} %reduce_sum.12), channel_id=1, source_target_pairs={{0,64},{32,96},{64,0},{96,32},{128,192},{160,224},{192,128},{224,1... | collective-permute-start | bytes 147464 | tf_op jit(solution)/shard_map/ppermute | solution.py:387
  109.4 6.1 %collective-permute-start.8 = (bf16[48,512]{1,0:T(8,128)(2,1)S(1)}, bf16[48,512]{1,0:T(8,128)(2,1)S(1)}, u32[]{:S(2)}, u32[]{:S(2)}) collective-permute-start(bf16[48,512]{1,0:T(8,128)(2,1)S(1)} %reduce_sum.12), channel_id=1, source_target_pairs={{0,32},{32,0},{64,96},{96,64},{128,160},{160,128},{192,224},{224,1... | collective-permute-start | bytes 147464 | tf_op jit(solution)/shard_map/ppermute | solution.py:387
  (11 other events, 15.2 us)

commit v2 on v1

--- a/solution.py
+++ b/solution.py
@@ -36,9 +36,18 @@
     return (lax.broadcasted_iota(jnp.int32, (n, cols), 1) == index_col).astype(BF16)
 
 
-def column_of(index_row):
-    n = index_row.shape[1]
-    return jnp.transpose(jnp.broadcast_to(index_row, (8, n)))[:, 0:1]
+LANES = 128
+
+
+def fill_rows(index_ref, hot_ref):
+    for j in range(index_ref.shape[0]):
+        hot_ref[:, j * LANES : (j + 1) * LANES] = onehot_rows(index_ref[j : j + 1, :], hot_ref.shape[0])
+
+
+def fill_cols(index_ref, hot_ref):
+    turned = jnp.transpose(index_ref[...])
+    for j in range(index_ref.shape[0]):
+        hot_ref[j * LANES : (j + 1) * LANES, :] = onehot_cols(turned[:, j : j + 1], hot_ref.shape[1])
 
 
 def swish_parts(pre):
@@ -62,13 +71,20 @@
     return (grad - first - unit * second) * scale
 
 
-def pick_kernel(send_ref, mesh_ref, *outs):
-    rows = mesh_ref.shape[0]
-    hot = onehot_rows(send_ref[...], rows)
-    picked = mm_tn(hot, mesh_ref[...]).astype(BF16)
-    margin = picked.shape[0] // 4
-    for i, out in enumerate(outs):
-        out[...] = picked[i * margin : (i + 1) * margin]
+def parity(axis):
+    return lax.axis_index(axis) % 2
+
+
+def pick_kernel(send_ref, mesh_ref, *refs):
+    outs, picked = refs[:4], refs[4]
+    hot = onehot_rows(send_ref[...], mesh_ref.shape[0])
+    picked[...] = mm_tn(hot, mesh_ref[...]).astype(BF16)
+    margin = outs[0].shape[0]
+    for pair, axis in enumerate(("sector", "band")):
+        odd = parity(axis)
+        for turn in range(2):
+            group = 2 * pair + (1 - odd if turn == 0 else odd)
+            outs[2 * pair + turn][...] = picked[pl.ds(pl.multiple_of(group * margin, margin), margin), :]
 
 
 def pick(send_rows, mesh_lat):
@@ -79,6 +95,7 @@
         out_shape=[part] * 4,
         in_specs=[VM, VM],
         out_specs=[VM] * 4,
+        scratch_shapes=[pltpu.VMEM((n, width), BF16)],
         name="pick",
         cost_estimate=pl.CostEstimate(flops=2 * n * n * width, bytes_accessed=2 * n * width * 2, transcendentals=0),
     )(send_rows.reshape(1, n), mesh_lat)
@@ -87,40 +104,85 @@
 TILE = 512
 
 
-def early_kernel(dst_ref, grid_ref, edge_ref, w_edge_ref, w_grid_ref, w_node_ref, base_ref, node_ref, prod_ref):
-    grid = grid_ref[...]
+def early_kernel(
+    dst_ref, grid_hbm, edge_hbm, w1_hbm, n1_hbm, base_hbm, node_hbm, grid, edge, w_edge, w_grid, w_node, prod, hot, base, node, sems
+):
     width = grid.shape[1]
-    prod_ref[...] = mm(grid, w_grid_ref[...]).astype(BF16)
-    node_ref[...] = mm(grid, w_node_ref[...])
-    points = grid.shape[0]
-    for t in range(edge_ref.shape[0] // TILE):
-        rows = slice(t * TILE, (t + 1) * TILE)
-        hot = onehot_cols(column_of(dst_ref[:, rows]), points)
-        base_ref[rows, :] = mm(edge_ref[rows, :], w_edge_ref[...]) + mm(hot, prod_ref[...])
+    edges = edge.shape[0]
+    tiles = [pl.ds(t * TILE, TILE) for t in range(edges // TILE)]
+    copies = [
+        pltpu.make_async_copy(grid_hbm, grid, sems.at[0]),
+        pltpu.make_async_copy(w1_hbm.at[pl.ds(2 * width, width), :], w_grid, sems.at[1]),
+        pltpu.make_async_copy(n1_hbm.at[pl.ds(width, width), :], w_node, sems.at[2]),
+        pltpu.make_async_copy(w1_hbm.at[pl.ds(0, width), :], w_edge, sems.at[3]),
+    ]
+    loads = [pltpu.make_async_copy(edge_hbm.at[rows, :], edge.at[rows, :], sems.at[4 + t]) for t, rows in enumerate(tiles)]
+    for copy in copies + loads:
+        copy.start()
+    fill_cols(dst_ref, hot)
+    copies[0].wait()
+    copies[1].wait()
+    prod[...] = mm(grid[...], w_grid[...]).astype(BF16)
+    copies[2].wait()
+    node[...] = mm(grid[...], w_node[...])
+    stores = [pltpu.make_async_copy(node, node_hbm, sems.at[4 + len(tiles)])]
+    stores[0].start()
+    copies[3].wait()
+    for t, rows in enumerate(tiles):
+        loads[t].wait()
+        base[rows, :] = mm(edge[rows, :], w_edge[...]) + mm(hot[rows, :], prod[...])
+        store = pltpu.make_async_copy(base.at[rows, :], base_hbm.at[rows, :], sems.at[5 + len(tiles) + t])
+        store.start()
+        stores.append(store)
+    for store in stores:
+        store.wait()
 
 
 def early(edge_dst, grid_block, edge_feat, w_edge1, w_node1):
     edges, width = edge_feat.shape
     points = grid_block.shape[0]
-    block = lambda i: pl.BlockSpec((width, width), lambda k: (i, 0))
+    square = pltpu.VMEM((width, width), BF16)
     return pl.pallas_call(
         early_kernel,
         out_shape=[
             jax.ShapeDtypeStruct((edges, width), F32),
             jax.ShapeDtypeStruct((points, width), F32),
         ],
-        in_specs=[VM, VM, VM, block(0), block(2), block(1)],
-        out_specs=[VM, VM],
-        scratch_shapes=[pltpu.VMEM((points, width), BF16)],
-        compiler_params=pltpu.CompilerParams(vmem_limit_bytes=40 << 20),
-        grid=(1,),
+        in_specs=[VM] + [ANY] * 4,
+        out_specs=[ANY, ANY],
+        scratch_shapes=[
+            pltpu.VMEM((points, width), BF16),
+            pltpu.VMEM((edges, width), BF16),
+            square,
+            square,
+            square,
+            pltpu.VMEM((points, width), BF16),
+            pltpu.VMEM((edges, points), BF16),
+            pltpu.VMEM((edges, width), F32),
+            pltpu.VMEM((points, width), F32),
+            pltpu.SemaphoreType.DMA((5 + 2 * (edges // TILE),)),
+        ],
+        compiler_params=pltpu.CompilerParams(vmem_limit_bytes=58 << 20),
         name="early",
         cost_estimate=pl.CostEstimate(
             flops=4 * edges * width * width + 4 * points * width * width,
             bytes_accessed=10 * edges * width,
             transcendentals=0,
         ),
-    )(edge_dst.reshape(1, edges), grid_block, edge_feat, w_edge1, w_edge1, w_node1)
+    )(edge_dst.reshape(edges // LANES, LANES), grid_block, edge_feat, w_edge1, w_node1)
+
+
+def gray(value):
+    return value ^ (value >> 1)
+
+
+def piece_order():
+    pieces = []
+    for block in range(16):
+        code = (block >> 3) | ((block >> 2) & 1) << 1 | ((block >> 1) & 1) << 2
+        z = next(i for i in range(8) if gray(i) == code)
+        pieces.append((block & 1) * 8 + z)
+    return pieces
 
 
 def main_kernel(
@@ -144,9 +206,16 @@
     n2_hbm,
     out_ref,
     dnpre_ref,
-    sm_ref,
     sg_ref,
-    gw_ref,
+    own_ref,
+    b0_ref,
+    b1_ref,
+    b2_ref,
+    b3_ref,
+    send_a,
+    send_b,
+    keep_a,
+    keep_b,
     base,
     node,
     edge,
@@ -167,6 +236,8 @@
     scale,
     msg,
     gp,
+    gw,
+    borrowed,
     sems,
 ):
     width = w2.shape[0]
@@ -187,12 +258,17 @@
         copy.start()
     own, margin = mesh_ref.shape[0], r0_ref.shape[0]
     table[0:own, :] = mesh_ref[...]
-    for i, part in enumerate((r0_ref, r1_ref, r2_ref, r3_ref)):
-        table[own + i * margin : own + (i + 1) * margin, :] = part[...]
-    hot_s[...] = onehot_cols(column_of(src_ref[...]), rows_table)
-    hot_d[...] = onehot_cols(column_of(dst_ref[...]), points)
-    hot_st[...] = onehot_rows(src_ref[...], rows_table)
-    hot_dt[...] = onehot_rows(dst_ref[...], points)
+    starts = []
+    for pair, axis in enumerate(("sector", "band")):
+        odd = parity(axis)
+        for slot in (1 - odd, odd):
+            starts.append(pl.multiple_of((2 * pair + slot) * margin, margin))
+    for start, part in zip(starts, (r0_ref, r1_ref, r2_ref, r3_ref)):
+        table[pl.ds(own + start, margin), :] = part[...]
+    fill_cols(src_ref, hot_s)
+    fill_cols(dst_ref, hot_d)
+    fill_rows(src_ref, hot_st)
+    fill_rows(dst_ref, hot_dt)
     edge_gain, node_gain = eg_ref[...], ng_ref[...]
 
     copies[0].wait()
@@ -224,13 +300,28 @@
         d_hid = mm_nt(d_edge.astype(BF16), w2[...]).astype(BF16).astype(F32)
         gp[rows, :] = (d_hid * slope[rows, :]).astype(BF16)
     copies[8].wait()
-    gw_ref[0:width, :] = mm_tn(edge[...], gp[...]).astype(BF16)
+    gw[0:width, :] = mm_tn(edge[...], gp[...]).astype(BF16)
     sm = mm(hot_st[...], gp[...]).astype(BF16)
-    sm_ref[...] = sm
-    gw_ref[width : 2 * width, :] = mm_tn(table[...], sm).astype(BF16)
+    gw[width : 2 * width, :] = mm_tn(table[...], sm).astype(BF16)
     sg = mm(hot_dt[...], gp[...]).astype(BF16)
     sg_ref[...] = sg
-    gw_ref[2 * width : 3 * width, :] = mm_tn(grid[...], sg).astype(BF16)
+    gw[2 * width : 3 * width, :] = mm_tn(grid[...], sg).astype(BF16)
+    core = parity("sector")
+    half = width // 2
+    piece = gw.shape[0] // (2 * len(piece_order()))
+    for i, j in enumerate(piece_order()):
+        rows = slice(i * piece, (i + 1) * piece)
+        mine = pl.ds(pl.multiple_of((2 * j + core) * piece, piece), piece)
+        other = pl.ds(pl.multiple_of((2 * j + 1 - core) * piece, piece), piece)
+        send_a[rows, :] = gw[other, 0:half]
+        send_b[rows, :] = gw[other, half:width]
+        keep_a[rows, :] = gw[mine, 0:half]
+        keep_b[rows, :] = gw[mine, half:width]
+    grad_table = mm_nt(sm, wm[...])
+    own_ref[...] = grad_table[0:own]
+    borrowed[...] = grad_table[own:].astype(BF16)
+    for start, out in zip(starts, (b0_ref, b1_ref, b2_ref, b3_ref)):
+        out[...] = borrowed[pl.ds(start, margin), :]
 
 
 def main(edge_src, edge_dst, mesh_lat, received, edge_gain, node_gain, base, node, edge_feat, grid_block, cot_block, w1, w2, n1, n2):
@@ -245,12 +336,13 @@
         out_shape=[
             sds((points, width), BF16),
             sds((points, width), BF16),
-            sds((table, width), BF16),
             sds((points, width), BF16),
-            sds((3 * width, width), BF16),
-        ],
+            sds(mesh_lat.shape, F32),
+        ]
+        + [sds(received[0].shape, BF16)] * 4
+        + [sds((3 * width // 2, width // 2), BF16)] * 4,
         in_specs=[VM] * 9 + [ANY] * 9,
-        out_specs=[VM] * 5,
+        out_specs=[VM] * 12,
         scratch_shapes=[
             pltpu.VMEM((edges, width), F32),
             pltpu.VMEM((points, width), F32),
@@ -272,6 +364,8 @@
             pltpu.VMEM((edges, 1), F32),
             pltpu.VMEM((edges, width), BF16),
             pltpu.VMEM((edges, width), BF16),
+            pltpu.VMEM((3 * width, width), BF16),
+            pltpu.VMEM((table - mesh_lat.shape[0], width), BF16),
             pltpu.SemaphoreType.DMA((9,)),
         ],
         compiler_params=pltpu.CompilerParams(vmem_limit_bytes=56 << 20),
@@ -282,8 +376,8 @@
             transcendentals=edges * width,
         ),
     )(
-        edge_src.reshape(1, edges),
-        edge_dst.reshape(1, edges),
+        edge_src.reshape(edges // LANES, LANES),
+        edge_dst.reshape(edges // LANES, LANES),
         mesh_lat,
         *received,
         edge_gain.reshape(1, width),
@@ -300,28 +394,6 @@
     )
 
 
-def table_kernel(sm_ref, w_ref, own_ref, *outs):
-    grad = mm_nt(sm_ref[...], w_ref[...])
-    own, margin = own_ref.shape[0], outs[0].shape[0]
-    own_ref[...] = grad[0:own]
-    for i, out in enumerate(outs):
-        out[...] = grad[own + i * margin : own + (i + 1) * margin].astype(BF16)
-
-
-def table_grads(sm, w1, own, margin):
-    width = sm.shape[1]
-    sds = jax.ShapeDtypeStruct
-    return pl.pallas_call(
-        table_kernel,
-        out_shape=[sds((own, width), F32)] + [sds((margin, width), BF16)] * 4,
-        in_specs=[VM, pl.BlockSpec((width, width), lambda k: (1, 0))],
-        out_specs=[VM] * 5,
-        grid=(1,),
-        name="table_grads",
-        cost_estimate=pl.CostEstimate(flops=2 * sm.shape[0] * width * width, bytes_accessed=1 << 20, transcendentals=0),
-    )(sm, w1)
-
-
 def grid_kernel(sg_ref, w1_ref, dnpre_ref, n1_ref, cot_ref, out_ref):
     total = cot_ref[...].astype(F32) + mm_nt(dnpre_ref[...], n1_ref[...]) + mm_nt(sg_ref[...], w1_ref[...])
     out_ref[...] = total.astype(BF16)
@@ -340,14 +412,15 @@
     )(sg, w1, dnpre, n1, cot_block)
 
 
-def mesh_kernel(send_ref, own_ref, r0_ref, r1_ref, r2_ref, r3_ref, out_ref):
-    own = own_ref.shape[0]
-    hot = onehot_rows(send_ref[...], own)
+def mesh_kernel(send_ref, own_ref, r0_ref, r1_ref, r2_ref, r3_ref, out_ref, back):
     margin = r0_ref.shape[0]
-    total = own_ref[...]
-    for i, part in enumerate((r0_ref, r1_ref, r2_ref, r3_ref)):
-        total = total + mm(hot[:, i * margin : (i + 1) * margin], part[...])
-    out_ref[...] = total.astype(BF16)
+    parts = (r0_ref, r1_ref, r2_ref, r3_ref)
+    for pair, axis in enumerate(("sector", "band")):
+        odd = parity(axis)
+        for turn, group in enumerate((1 - odd, odd)):
+            back[pl.ds(pl.multiple_of((2 * pair + group) * margin, margin), margin), :] = parts[2 * pair + turn][...]
+    hot = onehot_rows(send_ref[...], own_ref.shape[0])
+    out_ref[...] = (own_ref[...] + mm(hot, back[...])).astype(BF16)
 
 
 def mesh_grads(send_rows, own, returned):
@@ -357,38 +430,92 @@
         out_shape=jax.ShapeDtypeStruct(own.shape, BF16),
         in_specs=[VM] * 6,
         out_specs=VM,
+        scratch_shapes=[pltpu.VMEM((n, own.shape[1]), BF16)],
         name="mesh_grads",
         cost_estimate=pl.CostEstimate(flops=2 * n * n * own.shape[1], bytes_accessed=1 << 19, transcendentals=0),
     )(send_rows.reshape(1, n), own, *returned)
 
 
-def steps(axis, wrap):
-    devices = lax.axis_size(axis)
-    up = [(i, (i + 1) % devices) for i in range(devices if wrap else devices - 1)]
-    return up, [(j, i) for i, j in up]
-
-
 def swap(parts):
-    sector_up, sector_down = steps("sector", True)
-    band_up, band_down = steps("band", False)
+    sectors, bands = lax.axis_size("sector"), lax.axis_size("band")
+
+    def pairs(first, count, devices):
+        ups = [(i, (i + 1) % devices) for i in range(first, count, 2)]
+        return ups + [(j, i) for i, j in ups]
+
     return [
-        lax.ppermute(parts[1], "sector", sector_up),
-        lax.ppermute(parts[0], "sector", sector_down),
-        lax.ppermute(parts[3], "band", band_up),
-        lax.ppermute(parts[2], "band", band_down),
+        lax.ppermute(parts[0], "sector", pairs(0, sectors, sectors)),
+        lax.ppermute(parts[1], "sector", pairs(1, sectors, sectors)),
+        lax.ppermute(parts[2], "band", pairs(0, bands - 1, bands)),
+        lax.ppermute(parts[3], "band", pairs(1, bands - 1, bands)),
     ]
 
 
-def reduce_weights(gw):
-    sectors = lax.axis_size("sector")
-    parts = lax.all_to_all(gw.reshape(sectors, gw.shape[0] // sectors, gw.shape[1]), "sector", 0, 0)
-    part = jnp.sum(parts.astype(F32), axis=0).astype(BF16)
-    bands = lax.axis_size("band")
-    others = [lax.ppermute(part, "band", [(i, i ^ d) for i in range(bands)]) for d in range(1, bands)]
-    total = part.astype(F32)
-    for other in others:
-        total = total + other.astype(F32)
-    return total
+def coordinates(band, sector):
+    return {
+        "x_lo": band // 4,
+        "y": gray(band % 4),
+        "x_hi": sector // 16,
+        "z": gray(sector % 16 // 2),
+        "core": sector % 2,
+    }
+
+
+def send(values, flips):
+    place = {}
+    for band in range(lax.axis_size("band")):
+        for sector in range(lax.axis_size("sector")):
+            place[tuple(coordinates(band, sector).values())] = band * lax.axis_size("sector") + sector
+    names = list(coordinates(0, 0))
+    pairs = []
+    for spot, source in place.items():
+        target = list(spot)
+        for name, bit in flips:
+            target[names.index(name)] ^= 1 << bit
+        pairs.append((source, place[tuple(target)]))
+    return lax.ppermute(values, ("band", "sector"), sorted(pairs))
+
+
+def plus(a, b):
+    return (a.astype(F32) + b.astype(F32)).astype(BF16)
+
+
+def halve(low, high, bit, flip):
+    return plus(jnp.where(bit, high, low), send(jnp.where(bit, low, high), [flip]))
+
+
+def reduce_weights(send_a, send_b, keep_a, keep_b):
+    here = coordinates(lax.axis_index("band"), lax.axis_index("sector"))
+
+    def bit(name, k):
+        return ((here[name] >> k) & 1) == 1
+
+    def rows(values, name, k):
+        n = values.shape[0] // 2
+        return halve(values[:n], values[n:], bit(name, k), (name, k))
+
+    def cols(values, name, k):
+        n = values.shape[1] // 2
+        return halve(values[:, :n], values[:, n:], bit(name, k), (name, k))
+
+    part_a = plus(keep_a, send(send_a, [("core", 0)]))
+    part_b = plus(keep_b, send(send_b, [("core", 0)]))
+    part_a = cols(rows(part_a, "z", 0), "y", 0)
+    part_b = rows(cols(part_b, "y", 0), "z", 0)
+    part = halve(part_a, part_b, bit("x_lo", 0), ("x_lo", 0))
+    part = rows(rows(part, "z", 1), "z", 2)
+    part = rows(part, "x_hi", 0)
+    part = plus(part, send(part, [("y", 1)]))
+    by_y = send(part, [("y", 0)])
+    by_x = send(part, [("x_lo", 0)])
+    by_both = send(part, [("y", 0), ("x_lo", 0)])
+    odd_y, odd_x = bit("y", 0), bit("x_lo", 0)
+
+    def ordered(mine, other):
+        return jnp.concatenate([jnp.where(odd_y, other, mine), jnp.where(odd_y, mine, other)], axis=1)
+
+    near, far = ordered(part, by_y), ordered(by_x, by_both)
+    return jnp.concatenate([jnp.where(odd_x, far, near), jnp.where(odd_x, near, far)], axis=1).astype(F32)
 
 
 def shards(
@@ -409,18 +536,17 @@
     lat_rows, lon_cols, width = grid_lat.shape
     grid_block = grid_lat.reshape(lat_rows * lon_cols, width)
     cot_block = cotangent.reshape(lat_rows * lon_cols, width)
-    own, margin = mesh_lat.shape[0], send_rows.shape[0] // 4
     received = swap(pick(send_rows, mesh_lat))
     base, node = early(edge_dst, grid_block, edge_feat, w_edge1, w_node1)
-    result, dnpre, sm, sg, gw = main(
+    result, dnpre, sg, own_grad, *rest = main(
         edge_src, edge_dst, mesh_lat, received, edge_gain, node_gain, base, node, edge_feat, grid_block, cot_block, w_edge1, w_edge2, w_node1, w_node2
     )
-    own_grad, *borrowed = table_grads(sm, w_edge1, own, margin)
-    returned = swap(borrowed)
+    grad_w = reduce_weights(*rest[4:])
+    returned = swap(rest[:4])
     grad_grid = grid_grads(sg, w_edge1, dnpre, w_node1, cot_block)
     grad_mesh = mesh_grads(send_rows, own_grad, returned)
     total_edges = edge_feat.shape[0] * lax.axis_size("band") * lax.axis_size("sector")
-    grad_w = reduce_weights(gw) * (1.0 / math.sqrt(total_edges))
+    grad_w = grad_w * (1.0 / math.sqrt(total_edges))
     return (
         result.reshape(lat_rows, lon_cols, width),
         grad_grid.reshape(lat_rows, lon_cols, width),

time: 117 us -> 95.6 us (0.82)
  waiting for transfers between devices: 39.4 us -> 27.3 us
  local copies, waits for them, and re-layouts: 9.65 us -> 1.22 us
  starting transfers between devices: 39 us -> 34.6 us
  Pallas kernels: 26.5 us -> 28.7 us
  other arithmetic: 0.93 us -> 2.33 us
    all_to_all x1 -> x0, waiting for transfers between devices: 39.3 us -> none  [reduce_weights(): lax.all_to_all(gw.reshape(sectors, gw.shape[0] // sectors, gw.shape[1]),...]
    ppermute x15 -> x22, waiting for transfers between devices: 0.04 us -> 27.3 us  [the longest x14 27.2 us: send(): return lax.ppermute(values, ('band', 'sector'), sorted(pairs))]
    all_to_all x1 -> x0, starting transfers between devices: 12.4 us -> none  [reduce_weights(): lax.all_to_all(gw.reshape(sectors, gw.shape[0] // sectors, gw.shape[1]),...]
    ppermute x15 -> x22, starting transfers between devices: 26.6 us -> 34.6 us  [the longest x14 30.3 us: send(): return lax.ppermute(values, ('band', 'sector'), sorted(pairs))]
    unnamed x38 -> x26, local copies, waits for them, and re-layouts: 8.35 us -> 1.22 us
    pallas_call x1, Pallas kernels: 2.39 us -> 5.96 us  [early(): pl.pallas_call(early_kernel, out_shape=[jax.ShapeDtypeStruct((edges, widt...]
    pallas_call x1 -> x0, Pallas kernels: 2.15 us -> none  [table_grads(): pl.pallas_call(table_kernel, out_shape=[sds((own, width), F32)] + [sds((m...]
    convert_element_type x0 -> x9, other arithmetic: none -> 1.45 us  [plus(): return (a.astype(F32) + b.astype(F32)).astype(BF16)]
  transfers between devices with their start and end apart: 16 -> 22, of which waited for: 1 -> 10; matrix products, arithmetic and copies ran while one was open for 1% -> 2% of each run, Pallas kernels for 8% -> 12%
where the time goes in v2:
time: 95.6 us; the launch traced here: 95.1 us
  starting transfers between devices  34.6 us (36%)
  Pallas kernels  28.7 us (30%)
  waiting for transfers between devices  27.3 us (29%)
  other arithmetic  2.33 us (2%)
  local copies, waits for them, and re-layouts  1.22 us (1%)
  between operations  0.98 us (1%)
    ppermute x14, starting transfers between devices, send(): return lax.ppermute(values, ('band', 'sector'), sorted(pairs))  30.3 us
    ppermute x14, waiting for transfers between devices, send(): return lax.ppermute(values, ('band', 'sector'), sorted(pairs))  27.2 us
    pallas_call x1, Pallas kernels, main(): pl.pallas_call(main_kernel, out_shape=[sds((points, width), BF16), sds((p...  15.9 us
    pallas_call x1, Pallas kernels, early(): pl.pallas_call(early_kernel, out_shape=[jax.ShapeDtypeStruct((edges, widt...  5.96 us
    pallas_call x1, Pallas kernels, grid_grads(): pl.pallas_call(grid_kernel, out_shape=jax.ShapeDtypeStruct((points, width...  3.21 us
    ppermute x2, starting transfers between devices, swap(): lax.ppermute(parts[1], 'sector', pairs(1, sectors, sectors))  2.05 us
  transfers between devices with their start and end apart: 22, of which 10 were waited for; matrix products, arithmetic and copies ran while one was open for 2% of the time, Pallas kernels for 12%

profile of v2, /device:TPU:32, one launch (start us, length us, event | category | flops | bytes accessed | tf_op | source)
XLA Modules:
  0.0 95.1 jit_solution(9265913712545418431)
XLA Ops:
  0.6 1.8 %pick.1 = (bf16[32,512]{1,0:T(8,128)(2,1)}, bf16[32,512]{1,0:T(8,128)(2,1)}, bf16[32,512]{1,0:T(8,128)(2,1)}, bf16[32,512]{1,0:T(8,128)(2,1)}) custom-call(s32[1,128]{1,0:T(1,128)} %bitcast.12, bf16[128,512]{1,0:T(8,128)(2,1)} %mesh_ref.3), custom_call_target="tpu_custom_call" | custom-call | flops 16777216 | bytes 262144 | tf_op jit(solution)/shard_map/pick/pallas_call | solution.py:93
  2.4 2.0 %collective-permute-start.1 = (bf16[32,512]{1,0:T(8,128)(2,1)}, bf16[32,512]{1,0:T(8,128)(2,1)S(1)}, u32[]{:S(2)}, u32[]{:S(2)}) collective-permute-start(bf16[32,512]{1,0:T(8,128)(2,1)} %get-tuple-element.23), channel_id=1, source_target_pairs={{1,2},{3,4},{5,6},{7,8},{9,10},{11,12},{13,14},{15,16},{17,18},{19... | collective-permute-start | bytes 98312 | tf_op jit(solution)/shard_map/ppermute | solution.py:448
  5.0 6.0 %early.1 = (f32[1536,512]{1,0:T(8,128)}, f32[512,512]{1,0:T(8,128)}) custom-call(s32[12,128]{1,0:T(8,128)} %bitcast.17, bf16[512,512]{1,0:T(8,128)(2,1)} %bitcast.14, bf16[1536,512]{1,0:T(8,128)(2,1)} %edge_hbm.3, bf16[1536,512]{1,0:T(8,128)(2,1)} %w1_ref.1, bf16[1024,512]{1,0:T(8,128)(2,1)} %n1_ref.1), custom_call_target="tpu_custom_call" | custom-call | flops 2147483648 | bytes 7864320 | tf_op jit(solution)/shard_map/early/pallas_call | solution.py:145
  11.7 15.9 %main.1 = (bf16[512,512]{1,0:T(8,128)(2,1)}, bf16[512,512]{1,0:T(8,128)(2,1)}, bf16[512,512]{1,0:T(8,128)(2,1)}, f32[128,512]{1,0:T(8,128)}, bf16[32,512]{1,0:T(...) custom-call(s32[12,128]{1,0:T(8,128)} %bitcast.16, ...), custom_call_target="tpu_custom_call" | custom-call | flops 6442450944 | bytes 11010048 | tf_op jit(solution)/shard_map/main/pallas_call | solution.py:334
  27.6 1.4 %collective-permute-start.8 = (bf16[768,256]{1,0:T(8,128)(2,1)}, bf16[768,256]{1,0:T(8,128)(2,1)S(1)}, u32[]{:S(2)}, u32[]{:S(2)}) collective-permute-start(bf16[768,256]{1,0:T(8,128)(2,1)} %get-tuple-element.37), channel_id=1, source_target_pairs={{0,1},{1,0},{2,3},{3,2},{4,5},{5,4},{6,7},{7,6},{8,9},{9,8},{10,11... | collective-permute-start | bytes 1179656 | tf_op jit(solution)/shard_map/ppermute | solution.py:476
  29.2 1.4 %collective-permute-done.8 = bf16[768,256]{1,0:T(8,128)(2,1)S(1)} collective-permute-done((bf16[768,256]{1,0:T(8,128)(2,1)}, bf16[768,256]{1,0:T(8,128)(2,1)S(1)}, u32[]{:S(2)}, u32[]{:S(2)}) %collective-permute-start.8) | collective-permute-done | bytes 393248 | tf_op jit(solution)/shard_map/ppermute | solution.py:476
  30.6 1.1 %add_convert_fusion.1 = bf16[768,256]{1,0:T(8,128)(2,1)S(1)} fusion(bf16[768,256]{1,0:T(8,128)(2,1)S(1)} %collective-permute-done.8, bf16[768,256]{1,0:T(8,128)(2,1)} %get-tuple-element.36), kind=kLoop, calls=%fused_computation.1 | loop fusion | flops 786432 | bytes 1179648 | tf_op jit(solution)/shard_map/convert_element_type | solution.py:480
  31.8 3.9 %collective-permute-start.9 = (bf16[768,128]{1,0:T(8,128)(2,1)S(1)}, bf16[768,128]{1,0:T(8,128)(2,1)S(1)}, u32[]{:S(2)}, u32[]{:S(2)}) collective-permute-start(bf16[768,128]{1,0:T(8,128)(2,1)S(1)} %broadcast_select_fusion.1), channel_id=1, source_target_pairs={{0,32},{1,33},{2,34},{3,35},{4,36},{5,37},{6,38},{7,39},{8,40},{9,... | collective-permute-start | bytes 589832 | tf_op jit(solution)/shard_map/ppermute | solution.py:476
  35.9 7.5 %collective-permute-start.12 = (bf16[384,256]{1,0:T(8,128)(2,1)S(1)}, bf16[384,256]{1,0:T(8,128)(2,1)S(1)}, u32[]{:S(2)}, u32[]{:S(2)}) collective-permute-start(bf16[384,256]{1,0:T(8,128)(2,1)S(1)} %broadcast_select_fusion), channel_id=1, source_target_pairs={{0,2},{1,3},{2,0},{3,1},{4,6},{5,7},{6,4},{7,5},{8,10},{9,11},{10,... | collective-permute-start | bytes 589832 | tf_op jit(solution)/shard_map/ppermute | solution.py:476
  43.5 5.0 %collective-permute-start.10 = (bf16[384,128]{1,0:T(8,128)(2,1)S(1)}, bf16[384,128]{1,0:T(8,128)(2,1)S(1)}, u32[]{:S(2)}, u32[]{:S(2)}) collective-permute-start(bf16[384,128]{1,0:T(8,128)(2,1)S(1)} %broadcast_select_fusion.3), channel_id=1, source_target_pairs={{0,2},{1,3},{2,0},{3,1},{4,6},{5,7},{6,4},{7,5},{8,10},{9,11},{10,... | collective-permute-start | bytes 294920 | tf_op jit(solution)/shard_map/ppermute | solution.py:476
  48.7 1.8 %collective-permute-start.13 = (bf16[384,128]{1,0:T(8,128)(2,1)S(1)}, bf16[384,128]{1,0:T(8,128)(2,1)S(1)}, u32[]{:S(2)}, u32[]{:S(2)}) collective-permute-start(bf16[384,128]{1,0:T(8,128)(2,1)S(1)} %broadcast_select_fusion.2), channel_id=1, source_target_pairs={{0,32},{1,33},{2,34},{3,35},{4,36},{5,37},{6,38},{7,39},{8,40},{9,... | collective-permute-start | bytes 294920 | tf_op jit(solution)/shard_map/ppermute | solution.py:476
  51.1 2.2 %collective-permute-done.13 = bf16[384,128]{1,0:T(8,128)(2,1)S(1)} collective-permute-done((bf16[384,128]{1,0:T(8,128)(2,1)S(1)}, bf16[384,128]{1,0:T(8,128)(2,1)S(1)}, u32[]{:S(2)}, u32[]{:S(2)}) %collective-permute-start.13) | collective-permute-done | bytes 98336 | tf_op jit(solution)/shard_map/ppermute | solution.py:476
  53.5 2.6 %collective-permute-start.14 = (bf16[384,128]{1,0:T(8,128)(2,1)S(1)}, bf16[384,128]{1,0:T(8,128)(2,1)S(1)}, u32[]{:S(2)}, u32[]{:S(2)}) collective-permute-start(bf16[384,128]{1,0:T(8,128)(2,1)S(1)} %get-tuple-element.40), channel_id=1, source_target_pairs={{0,128},{1,129},{2,130},{3,131},{4,132},{5,133},{6,134},{7,135},{8... | collective-permute-start | bytes 294920 | tf_op jit(solution)/shard_map/ppermute | solution.py:476
  56.1 2.6 %collective-permute-done.14 = bf16[384,128]{1,0:T(8,128)(2,1)S(1)} collective-permute-done((bf16[384,128]{1,0:T(8,128)(2,1)S(1)}, bf16[384,128]{1,0:T(8,128)(2,1)S(1)}, u32[]{:S(2)}, u32[]{:S(2)}) %collective-permute-start.14) | collective-permute-done | bytes 98336 | tf_op jit(solution)/shard_map/ppermute | solution.py:476
  58.8 4.1 %collective-permute-done.15 = bf16[192,128]{1,0:T(8,128)(2,1)S(1)} collective-permute-done((bf16[192,128]{1,0:T(8,128)(2,1)S(1)}, bf16[192,128]{1,0:T(8,128)(2,1)S(1)}, u32[]{:S(2)}, u32[]{:S(2)}) %collective-permute-start.15) | collective-permute-done | bytes 49184 | tf_op jit(solution)/shard_map/ppermute | solution.py:476
  63.1 6.8 %collective-permute-done.16 = bf16[96,128]{1,0:T(8,128)(2,1)S(1)} collective-permute-done((bf16[96,128]{1,0:T(8,128)(2,1)S(1)}, bf16[96,128]{1,0:T(8,128)(2,1)S(1)}, u32[]{:S(2)}, u32[]{:S(2)}) %collective-permute-start.16) | collective-permute-done | bytes 24608 | tf_op jit(solution)/shard_map/ppermute | solution.py:476
  70.5 4.7 %collective-permute-done.17 = bf16[48,128]{1,0:T(8,128)(2,1)S(1)} collective-permute-done((bf16[48,128]{1,0:T(8,128)(2,1)S(1)}, bf16[48,128]{1,0:T(8,128)(2,1)S(1)}, u32[]{:S(2)}, u32[]{:S(2)}) %collective-permute-start.17) | collective-permute-done | bytes 12320 | tf_op jit(solution)/shard_map/ppermute | solution.py:476
  75.2 2.2 %collective-permute-start.18 = (bf16[48,128]{1,0:T(8,128)(2,1)S(1)}, bf16[48,128]{1,0:T(8,128)(2,1)S(1)}, u32[]{:S(2)}, u32[]{:S(2)}) collective-permute-start(bf16[48,128]{1,0:T(8,128)(2,1)S(1)} %add_convert_fusion.10), channel_id=1, source_target_pairs={{0,96},{1,97},{2,98},{3,99},{4,100},{5,101},{6,102},{7,103},{8,104... | collective-permute-start | bytes 36872 | tf_op jit(solution)/shard_map/ppermute | solution.py:476
  79.1 1.1 %collective-permute-done.18 = bf16[48,128]{1,0:T(8,128)(2,1)S(1)} collective-permute-done((bf16[48,128]{1,0:T(8,128)(2,1)S(1)}, bf16[48,128]{1,0:T(8,128)(2,1)S(1)}, u32[]{:S(2)}, u32[]{:S(2)}) %collective-permute-start.18) | collective-permute-done | bytes 12320 | tf_op jit(solution)/shard_map/ppermute | solution.py:476
  80.2 2.8 %collective-permute-start.21 = (bf16[48,128]{1,0:T(8,128)(2,1)S(1)}, bf16[48,128]{1,0:T(8,128)(2,1)S(1)}, u32[]{:S(2)}, u32[]{:S(2)}) collective-permute-start(bf16[48,128]{1,0:T(8,128)(2,1)S(1)} %add_convert_fusion.9), channel_id=1, source_target_pairs={{0,32},{1,33},{2,34},{3,35},{4,36},{5,37},{6,38},{7,39},{8,40},{9,... | collective-permute-start | bytes 36872 | tf_op jit(solution)/shard_map/ppermute | solution.py:476
  83.1 3.2 %grid_grads.1 = bf16[512,512]{1,0:T(8,128)(2,1)} custom-call(bf16[512,512]{1,0:T(8,128)(2,1)} %get-tuple-element.29.sg_ref, bf16[1536,512]{1,0:T(8,128)(2,1)} %w1_ref.1, bf16[512,512]{1,0:T(8,128)(2,1)} %get-tuple-element.30.dnpre_ref, bf16[1024,512]{1,0:T(8,128)(2,1)} %n1_ref.1, bf16[512,512]{1,0:T(8,128)(2,1)} %bitcast.10), custom_call_target="tpu_custom_call" | custom-call | flops 536870912 | bytes 3145728 | tf_op jit(solution)/shard_map/grid_grads/pallas_call | solution.py:404
  86.9 1.8 %mesh_grads.1 = bf16[128,512]{1,0:T(8,128)(2,1)} custom-call(s32[1,128]{1,0:T(1,128)} %bitcast.13, f32[128,512]{1,0:T(8,128)} %get-tuple-element.31.own_ref, bf16[32,512]{1,0:T(8,128)(2,1)} %copy-done.1, bf16[32,512]{1,0:T(8,128)(2,1)} %copy-done.2, bf16[32,512]{1,0:T(8,128)(2,1)} %copy-done.3, bf16[32,512]{1,0:T(8,128)(2,1)} %copy-done.4), custom_call_target="tpu_custom_call" | custom-call | flops 16777216 | bytes 524288 | tf_op jit(solution)/shard_map/mesh_grads/pallas_call | solution.py:428
  88.7 2.0 %collective-permute-start.19 = (bf16[48,128]{1,0:T(8,128)(2,1)S(1)}, bf16[48,128]{1,0:T(8,128)(2,1)S(1)}, u32[]{:S(2)}, u32[]{:S(2)}) collective-permute-start(bf16[48,128]{1,0:T(8,128)(2,1)S(1)} %add_convert_fusion.9), channel_id=1, source_target_pairs={{0,160},{1,161},{2,162},{3,163},{4,164},{5,165},{6,166},{7,167},{8... | collective-permute-start | bytes 36872 | tf_op jit(solution)/shard_map/ppermute | solution.py:476
  90.7 2.7 %collective-permute-done.19 = bf16[48,128]{1,0:T(8,128)(2,1)S(1)} collective-permute-done((bf16[48,128]{1,0:T(8,128)(2,1)S(1)}, bf16[48,128]{1,0:T(8,128)(2,1)S(1)}, u32[]{:S(2)}, u32[]{:S(2)}) %collective-permute-start.19) | collective-permute-done | bytes 12320 | tf_op jit(solution)/shard_map/ppermute | solution.py:476
  (72 shorter events, 7.3 us)
Async XLA Ops:
  2.4 8.6 %collective-permute-start = (bf16[32,512]{1,0:T(8,128)(2,1)}, bf16[32,512]{1,0:T(8,128)(2,1)S(1)}, u32[]{:S(2)}, u32[]{:S(2)}) collective-permute-start(bf16[32,512]{1,0:T(8,128)(2,1)} %get-tuple-element.22), channel_id=1, source_target_pairs={{0,1},{2,3},{4,5},{6,7},{8,9},{10,11},{12,13},{14,15},{16,17},{18,... | collective-permute-start | bytes 98312 | tf_op jit(solution)/shard_map/ppermute | solution.py:447
  2.4 8.6 %collective-permute-start.1 = (bf16[32,512]{1,0:T(8,128)(2,1)}, bf16[32,512]{1,0:T(8,128)(2,1)S(1)}, u32[]{:S(2)}, u32[]{:S(2)}) collective-permute-start(bf16[32,512]{1,0:T(8,128)(2,1)} %get-tuple-element.23), channel_id=1, source_target_pairs={{1,2},{3,4},{5,6},{7,8},{9,10},{11,12},{13,14},{15,16},{17,18},{19... | collective-permute-start | bytes 98312 | tf_op jit(solution)/shard_map/ppermute | solution.py:448
  4.4 6.7 %collective-permute-start.2 = (bf16[32,512]{1,0:T(8,128)(2,1)}, bf16[32,512]{1,0:T(8,128)(2,1)S(1)}, u32[]{:S(2)}, u32[]{:S(2)}) collective-permute-start(bf16[32,512]{1,0:T(8,128)(2,1)} %get-tuple-element.24), channel_id=1, source_target_pairs={{0,32},{64,96},{128,160},{192,224},{32,0},{96,64},{160,128},{224,1... | collective-permute-start | bytes 98312 | tf_op jit(solution)/shard_map/ppermute | solution.py:449
  4.4 6.7 %collective-permute-start.3 = (bf16[32,512]{1,0:T(8,128)(2,1)}, bf16[32,512]{1,0:T(8,128)(2,1)S(1)}, u32[]{:S(2)}, u32[]{:S(2)}) collective-permute-start(bf16[32,512]{1,0:T(8,128)(2,1)} %get-tuple-element.25), channel_id=1, source_target_pairs={{32,64},{96,128},{160,192},{64,32},{128,96},{192,160},{33,65},{97,... | collective-permute-start | bytes 98312 | tf_op jit(solution)/shard_map/ppermute | solution.py:450
  27.6 3.0 %collective-permute-start.8 = (bf16[768,256]{1,0:T(8,128)(2,1)}, bf16[768,256]{1,0:T(8,128)(2,1)S(1)}, u32[]{:S(2)}, u32[]{:S(2)}) collective-permute-start(bf16[768,256]{1,0:T(8,128)(2,1)} %get-tuple-element.37), channel_id=1, source_target_pairs={{0,1},{1,0},{2,3},{3,2},{4,5},{5,4},{6,7},{7,6},{8,9},{9,8},{10,11... | collective-permute-start | bytes 1179656 | tf_op jit(solution)/shard_map/ppermute | solution.py:476
  29.1 6.6 %collective-permute-start.11 = (bf16[768,256]{1,0:T(8,128)(2,1)}, bf16[768,256]{1,0:T(8,128)(2,1)S(1)}, u32[]{:S(2)}, u32[]{:S(2)}) collective-permute-start(bf16[768,256]{1,0:T(8,128)(2,1)} %get-tuple-element.39), channel_id=1, source_target_pairs={{0,1},{1,0},{2,3},{3,2},{4,5},{5,4},{6,7},{7,6},{8,9},{9,8},{10,11... | collective-permute-start | bytes 1179656 | tf_op jit(solution)/shard_map/ppermute | solution.py:476
  31.8 11.6 %collective-permute-start.9 = (bf16[768,128]{1,0:T(8,128)(2,1)S(1)}, bf16[768,128]{1,0:T(8,128)(2,1)S(1)}, u32[]{:S(2)}, u32[]{:S(2)}) collective-permute-start(bf16[768,128]{1,0:T(8,128)(2,1)S(1)} %broadcast_select_fusion.1), channel_id=1, source_target_pairs={{0,32},{1,33},{2,34},{3,35},{4,36},{5,37},{6,38},{7,39},{8,40},{9,... | collective-permute-start | bytes 589832 | tf_op jit(solution)/shard_map/ppermute | solution.py:476
  35.9 12.7 %collective-permute-start.12 = (bf16[384,256]{1,0:T(8,128)(2,1)S(1)}, bf16[384,256]{1,0:T(8,128)(2,1)S(1)}, u32[]{:S(2)}, u32[]{:S(2)}) collective-permute-start(bf16[384,256]{1,0:T(8,128)(2,1)S(1)} %broadcast_select_fusion), channel_id=1, source_target_pairs={{0,2},{1,3},{2,0},{3,1},{4,6},{5,7},{6,4},{7,5},{8,10},{9,11},{10,... | collective-permute-start | bytes 589832 | tf_op jit(solution)/shard_map/ppermute | solution.py:476
  43.5 34.1 %copy-start.6 = (bf16[32,512]{1,0:T(8,128)(2,1)S(1)}, bf16[32,512]{1,0:T(8,128)(2,1)}, u32[]{:S(2)}) copy-start(bf16[32,512]{1,0:T(8,128)(2,1)} %get-tuple-element.34) | copy-start | bytes 98308
  43.5 35.0 %copy-start.5 = (bf16[32,512]{1,0:T(8,128)(2,1)S(1)}, bf16[32,512]{1,0:T(8,128)(2,1)}, u32[]{:S(2)}) copy-start(bf16[32,512]{1,0:T(8,128)(2,1)} %get-tuple-element.35) | copy-start | bytes 98308
  43.5 7.6 %collective-permute-start.10 = (bf16[384,128]{1,0:T(8,128)(2,1)S(1)}, bf16[384,128]{1,0:T(8,128)(2,1)S(1)}, u32[]{:S(2)}, u32[]{:S(2)}) collective-permute-start(bf16[384,128]{1,0:T(8,128)(2,1)S(1)} %broadcast_select_fusion.3), channel_id=1, source_target_pairs={{0,2},{1,3},{2,0},{3,1},{4,6},{5,7},{6,4},{7,5},{8,10},{9,11},{10,... | collective-permute-start | bytes 294920 | tf_op jit(solution)/shard_map/ppermute | solution.py:476
  48.7 4.7 %collective-permute-start.13 = (bf16[384,128]{1,0:T(8,128)(2,1)S(1)}, bf16[384,128]{1,0:T(8,128)(2,1)S(1)}, u32[]{:S(2)}, u32[]{:S(2)}) collective-permute-start(bf16[384,128]{1,0:T(8,128)(2,1)S(1)} %broadcast_select_fusion.2), channel_id=1, source_target_pairs={{0,32},{1,33},{2,34},{3,35},{4,36},{5,37},{6,38},{7,39},{8,40},{9,... | collective-permute-start | bytes 294920 | tf_op jit(solution)/shard_map/ppermute | solution.py:476
  53.5 5.2 %collective-permute-start.14 = (bf16[384,128]{1,0:T(8,128)(2,1)S(1)}, bf16[384,128]{1,0:T(8,128)(2,1)S(1)}, u32[]{:S(2)}, u32[]{:S(2)}) collective-permute-start(bf16[384,128]{1,0:T(8,128)(2,1)S(1)} %get-tuple-element.40), channel_id=1, source_target_pairs={{0,128},{1,129},{2,130},{3,131},{4,132},{5,133},{6,134},{7,135},{8... | collective-permute-start | bytes 294920 | tf_op jit(solution)/shard_map/ppermute | solution.py:476
  58.7 4.2 %collective-permute-start.15 = (bf16[192,128]{1,0:T(8,128)(2,1)S(1)}, bf16[192,128]{1,0:T(8,128)(2,1)S(1)}, u32[]{:S(2)}, u32[]{:S(2)}) collective-permute-start(bf16[192,128]{1,0:T(8,128)(2,1)S(1)} %broadcast_select_fusion.5), channel_id=1, source_target_pairs={{0,6},{1,7},{2,4},{3,5},{4,2},{5,3},{6,0},{7,1},{8,14},{9,15},{10,... | collective-permute-start | bytes 147464 | tf_op jit(solution)/shard_map/ppermute | solution.py:476
  63.0 6.9 %collective-permute-start.16 = (bf16[96,128]{1,0:T(8,128)(2,1)S(1)}, bf16[96,128]{1,0:T(8,128)(2,1)S(1)}, u32[]{:S(2)}, u32[]{:S(2)}) collective-permute-start(bf16[96,128]{1,0:T(8,128)(2,1)S(1)} %broadcast_select_fusion.6), channel_id=1, source_target_pairs={{0,14},{1,15},{2,12},{3,13},{4,10},{5,11},{6,8},{7,9},{8,6},{9,7},... | collective-permute-start | bytes 73736 | tf_op jit(solution)/shard_map/ppermute | solution.py:476
  69.9 5.3 %collective-permute-start.17 = (bf16[48,128]{1,0:T(8,128)(2,1)S(1)}, bf16[48,128]{1,0:T(8,128)(2,1)S(1)}, u32[]{:S(2)}, u32[]{:S(2)}) collective-permute-start(bf16[48,128]{1,0:T(8,128)(2,1)S(1)} %broadcast_select_fusion.9), channel_id=1, source_target_pairs={{0,16},{1,17},{2,18},{3,19},{4,20},{5,21},{6,22},{7,23},{8,24},{9,... | collective-permute-start | bytes 36872 | tf_op jit(solution)/shard_map/ppermute | solution.py:476
  75.2 5.0 %collective-permute-start.18 = (bf16[48,128]{1,0:T(8,128)(2,1)S(1)}, bf16[48,128]{1,0:T(8,128)(2,1)S(1)}, u32[]{:S(2)}, u32[]{:S(2)}) collective-permute-start(bf16[48,128]{1,0:T(8,128)(2,1)S(1)} %add_convert_fusion.10), channel_id=1, source_target_pairs={{0,96},{1,97},{2,98},{3,99},{4,100},{5,101},{6,102},{7,103},{8,104... | collective-permute-start | bytes 36872 | tf_op jit(solution)/shard_map/ppermute | solution.py:476
  77.5 8.8 %collective-permute-start.4 = (bf16[32,512]{1,0:T(8,128)(2,1)S(1)}, bf16[32,512]{1,0:T(8,128)(2,1)S(1)}, u32[]{:S(2)}, u32[]{:S(2)}) collective-permute-start(bf16[32,512]{1,0:T(8,128)(2,1)S(1)} %copy-done.8), channel_id=1, source_target_pairs={{0,1},{2,3},{4,5},{6,7},{8,9},{10,11},{12,13},{14,15},{16,17},{18,... | collective-permute-start | bytes 98312 | tf_op jit(solution)/shard_map/ppermute | solution.py:447
  77.5 8.8 %collective-permute-start.5 = (bf16[32,512]{1,0:T(8,128)(2,1)S(1)}, bf16[32,512]{1,0:T(8,128)(2,1)S(1)}, u32[]{:S(2)}, u32[]{:S(2)}) collective-permute-start(bf16[32,512]{1,0:T(8,128)(2,1)S(1)} %copy-done.7), channel_id=1, source_target_pairs={{1,2},{3,4},{5,6},{7,8},{9,10},{11,12},{13,14},{15,16},{17,18},{19... | collective-permute-start | bytes 98312 | tf_op jit(solution)/shard_map/ppermute | solution.py:448
  77.6 8.7 %collective-permute-start.6 = (bf16[32,512]{1,0:T(8,128)(2,1)S(1)}, bf16[32,512]{1,0:T(8,128)(2,1)S(1)}, u32[]{:S(2)}, u32[]{:S(2)}) collective-permute-start(bf16[32,512]{1,0:T(8,128)(2,1)S(1)} %copy-done.6), channel_id=1, source_target_pairs={{0,32},{64,96},{128,160},{192,224},{32,0},{96,64},{160,128},{224,1... | collective-permute-start | bytes 98312 | tf_op jit(solution)/shard_map/ppermute | solution.py:449
  78.5 7.8 %collective-permute-start.7 = (bf16[32,512]{1,0:T(8,128)(2,1)S(1)}, bf16[32,512]{1,0:T(8,128)(2,1)S(1)}, u32[]{:S(2)}, u32[]{:S(2)}) collective-permute-start(bf16[32,512]{1,0:T(8,128)(2,1)S(1)} %copy-done.5), channel_id=1, source_target_pairs={{32,64},{96,128},{160,192},{64,32},{128,96},{192,160},{33,65},{97,... | collective-permute-start | bytes 98312 | tf_op jit(solution)/shard_map/ppermute | solution.py:450
  80.2 10.5 %collective-permute-start.21 = (bf16[48,128]{1,0:T(8,128)(2,1)S(1)}, bf16[48,128]{1,0:T(8,128)(2,1)S(1)}, u32[]{:S(2)}, u32[]{:S(2)}) collective-permute-start(bf16[48,128]{1,0:T(8,128)(2,1)S(1)} %add_convert_fusion.9), channel_id=1, source_target_pairs={{0,32},{1,33},{2,34},{3,35},{4,36},{5,37},{6,38},{7,39},{8,40},{9,... | collective-permute-start | bytes 36872 | tf_op jit(solution)/shard_map/ppermute | solution.py:476
  88.7 4.7 %collective-permute-start.19 = (bf16[48,128]{1,0:T(8,128)(2,1)S(1)}, bf16[48,128]{1,0:T(8,128)(2,1)S(1)}, u32[]{:S(2)}, u32[]{:S(2)}) collective-permute-start(bf16[48,128]{1,0:T(8,128)(2,1)S(1)} %add_convert_fusion.9), channel_id=1, source_target_pairs={{0,160},{1,161},{2,162},{3,163},{4,164},{5,165},{6,166},{7,167},{8... | collective-permute-start | bytes 36872 | tf_op jit(solution)/shard_map/ppermute | solution.py:476
  90.7 3.7 %collective-permute-start.20 = (bf16[48,128]{1,0:T(8,128)(2,1)S(1)}, bf16[48,128]{1,0:T(8,128)(2,1)S(1)}, u32[]{:S(2)}, u32[]{:S(2)}) collective-permute-start(bf16[48,128]{1,0:T(8,128)(2,1)S(1)} %add_convert_fusion.9), channel_id=1, source_target_pairs={{0,128},{1,129},{2,130},{3,131},{4,132},{5,133},{6,134},{7,135},{8... | collective-permute-start | bytes 36872 | tf_op jit(solution)/shard_map/ppermute | solution.py:476
  (11 other events, 80.9 us)

commit v3 on v2

--- a/solution.py
+++ b/solution.py
@@ -104,74 +104,6 @@
 TILE = 512
 
 
-def early_kernel(
-    dst_ref, grid_hbm, edge_hbm, w1_hbm, n1_hbm, base_hbm, node_hbm, grid, edge, w_edge, w_grid, w_node, prod, hot, base, node, sems
-):
-    width = grid.shape[1]
-    edges = edge.shape[0]
-    tiles = [pl.ds(t * TILE, TILE) for t in range(edges // TILE)]
-    copies = [
-        pltpu.make_async_copy(grid_hbm, grid, sems.at[0]),
-        pltpu.make_async_copy(w1_hbm.at[pl.ds(2 * width, width), :], w_grid, sems.at[1]),
-        pltpu.make_async_copy(n1_hbm.at[pl.ds(width, width), :], w_node, sems.at[2]),
-        pltpu.make_async_copy(w1_hbm.at[pl.ds(0, width), :], w_edge, sems.at[3]),
-    ]
-    loads = [pltpu.make_async_copy(edge_hbm.at[rows, :], edge.at[rows, :], sems.at[4 + t]) for t, rows in enumerate(tiles)]
-    for copy in copies + loads:
-        copy.start()
-    fill_cols(dst_ref, hot)
-    copies[0].wait()
-    copies[1].wait()
-    prod[...] = mm(grid[...], w_grid[...]).astype(BF16)
-    copies[2].wait()
-    node[...] = mm(grid[...], w_node[...])
-    stores = [pltpu.make_async_copy(node, node_hbm, sems.at[4 + len(tiles)])]
-    stores[0].start()
-    copies[3].wait()
-    for t, rows in enumerate(tiles):
-        loads[t].wait()
-        base[rows, :] = mm(edge[rows, :], w_edge[...]) + mm(hot[rows, :], prod[...])
-        store = pltpu.make_async_copy(base.at[rows, :], base_hbm.at[rows, :], sems.at[5 + len(tiles) + t])
-        store.start()
-        stores.append(store)
-    for store in stores:
-        store.wait()
-
-
-def early(edge_dst, grid_block, edge_feat, w_edge1, w_node1):
-    edges, width = edge_feat.shape
-    points = grid_block.shape[0]
-    square = pltpu.VMEM((width, width), BF16)
-    return pl.pallas_call(
-        early_kernel,
-        out_shape=[
-            jax.ShapeDtypeStruct((edges, width), F32),
-            jax.ShapeDtypeStruct((points, width), F32),
-        ],
-        in_specs=[VM] + [ANY] * 4,
-        out_specs=[ANY, ANY],
-        scratch_shapes=[
-            pltpu.VMEM((points, width), BF16),
-            pltpu.VMEM((edges, width), BF16),
-            square,
-            square,
-            square,
-            pltpu.VMEM((points, width), BF16),
-            pltpu.VMEM((edges, points), BF16),
-            pltpu.VMEM((edges, width), F32),
-            pltpu.VMEM((points, width), F32),
-            pltpu.SemaphoreType.DMA((5 + 2 * (edges // TILE),)),
-        ],
-        compiler_params=pltpu.CompilerParams(vmem_limit_bytes=58 << 20),
-        name="early",
-        cost_estimate=pl.CostEstimate(
-            flops=4 * edges * width * width + 4 * points * width * width,
-            bytes_accessed=10 * edges * width,
-            transcendentals=0,
-        ),
-    )(edge_dst.reshape(edges // LANES, LANES), grid_block, edge_feat, w_edge1, w_node1)
-
-
 def gray(value):
     return value ^ (value >> 1)
 
@@ -195,8 +127,6 @@
     r3_ref,
     eg_ref,
     ng_ref,
-    base_hbm,
-    node_hbm,
     edge_hbm,
     grid_hbm,
     cot_hbm,
@@ -216,17 +146,16 @@
     send_b,
     keep_a,
     keep_b,
-    base,
-    node,
     edge,
     grid,
     cot,
-    wm,
+    w1,
     w2,
     n1,
     n2,
     table,
     prod,
+    prod_g,
     hot_s,
     hot_d,
     hot_st,
@@ -241,18 +170,13 @@
     sems,
 ):
     width = w2.shape[0]
-    edges, points, rows_table = base.shape[0], grid.shape[0], table.shape[0]
+    edges, points, rows_table = edge.shape[0], grid.shape[0], table.shape[0]
     tiles = [slice(t * TILE, (t + 1) * TILE) for t in range(edges // TILE)]
-    copies = [
-        pltpu.make_async_copy(w1_hbm.at[pl.ds(width, width), :], wm, sems.at[0]),
-        pltpu.make_async_copy(base_hbm, base, sems.at[1]),
-        pltpu.make_async_copy(w2_hbm, w2, sems.at[2]),
-        pltpu.make_async_copy(n1_hbm.at[pl.ds(0, width), :], n1, sems.at[3]),
-        pltpu.make_async_copy(node_hbm, node, sems.at[4]),
-        pltpu.make_async_copy(n2_hbm, n2, sems.at[5]),
-        pltpu.make_async_copy(cot_hbm, cot, sems.at[6]),
-        pltpu.make_async_copy(grid_hbm, grid, sems.at[7]),
-        pltpu.make_async_copy(edge_hbm, edge, sems.at[8]),
+    grid_copy, w1_copy, edge_copy, w2_copy, n1_copy, n2_copy, cot_copy = copies = [
+        pltpu.make_async_copy(source, target, sems.at[i])
+        for i, (source, target) in enumerate(
+            ((grid_hbm, grid), (w1_hbm, w1), (edge_hbm, edge), (w2_hbm, w2), (n1_hbm, n1), (n2_hbm, n2), (cot_hbm, cot))
+        )
     ]
     for copy in copies:
         copy.start()
@@ -271,35 +195,38 @@
     fill_rows(dst_ref, hot_dt)
     edge_gain, node_gain = eg_ref[...], ng_ref[...]
 
-    copies[0].wait()
-    prod[...] = mm(table[...], wm[...]).astype(BF16)
-    copies[1].wait()
-    copies[2].wait()
+    grid_copy.wait()
+    w1_copy.wait()
+    w_edge, w_mesh, w_grid = (w1.at[pl.ds(i * width, width), :] for i in range(3))
+    prod[...] = mm(table[...], w_mesh[...]).astype(BF16)
+    prod_g[...] = mm(grid[...], w_grid[...]).astype(BF16)
+    edge_copy.wait()
+    w2_copy.wait()
     for rows in tiles:
-        pre = base[rows, :] + mm(hot_s[rows, :], prod[...])
+        pre = mm(edge[rows, :], w_edge[...]) + mm(hot_s[rows, :], prod[...]) + mm(hot_d[rows, :], prod_g[...])
         hidden, steep = swish_parts(pre)
         slope[rows, :] = steep
         normed, inv = norm_parts(mm(hidden.astype(BF16), w2[...]))
         unit[rows, :] = normed
         scale[rows, :] = inv
         msg[rows, :] = (normed * edge_gain).astype(BF16)
-    for copy in copies[3:8]:
+    for copy in (n1_copy, n2_copy, cot_copy):
         copy.wait()
+    n1_agg, n1_grid = (n1.at[pl.ds(i * width, width), :] for i in range(2))
     agg = mm(hot_dt[...], msg[...]).astype(BF16)
-    node_hidden, node_slope = swish_parts(mm(agg, n1[...]) + node[...])
+    node_hidden, node_slope = swish_parts(mm(agg, n1_agg[...]) + mm(grid[...], n1_grid[...]))
     node_unit, node_inv = norm_parts(mm(node_hidden.astype(BF16), n2[...]))
     out_ref[...] = (grid[...].astype(F32) + node_unit * node_gain).astype(BF16)
     d_raw = norm_back(cot[...].astype(F32) * node_gain, node_unit, node_inv)
     d_hidden = mm_nt(d_raw.astype(BF16), n2[...]).astype(BF16).astype(F32)
     d_pre = (d_hidden * node_slope).astype(BF16)
     dnpre_ref[...] = d_pre
-    d_agg = mm_nt(d_pre, n1[...]).astype(BF16)
+    d_agg = mm_nt(d_pre, n1_agg[...]).astype(BF16)
     for rows in tiles:
         d_msg = mm(hot_d[rows, :], d_agg)
         d_edge = norm_back(d_msg * edge_gain, unit[rows, :], scale[rows, :])
         d_hid = mm_nt(d_edge.astype(BF16), w2[...]).astype(BF16).astype(F32)
         gp[rows, :] = (d_hid * slope[rows, :]).astype(BF16)
-    copies[8].wait()
     gw[0:width, :] = mm_tn(edge[...], gp[...]).astype(BF16)
     sm = mm(hot_st[...], gp[...]).astype(BF16)
     gw[width : 2 * width, :] = mm_tn(table[...], sm).astype(BF16)
@@ -317,14 +244,14 @@
         send_b[rows, :] = gw[other, half:width]
         keep_a[rows, :] = gw[mine, 0:half]
         keep_b[rows, :] = gw[mine, half:width]
-    grad_table = mm_nt(sm, wm[...])
+    grad_table = mm_nt(sm, w_mesh[...])
     own_ref[...] = grad_table[0:own]
     borrowed[...] = grad_table[own:].astype(BF16)
     for start, out in zip(starts, (b0_ref, b1_ref, b2_ref, b3_ref)):
         out[...] = borrowed[pl.ds(start, margin), :]
 
 
-def main(edge_src, edge_dst, mesh_lat, received, edge_gain, node_gain, base, node, edge_feat, grid_block, cot_block, w1, w2, n1, n2):
+def main(edge_src, edge_dst, mesh_lat, received, edge_gain, node_gain, edge_feat, grid_block, cot_block, w1, w2, n1, n2):
     edges, width = edge_feat.shape
     points = grid_block.shape[0]
     table = mesh_lat.shape[0] + 4 * received[0].shape[0]
@@ -341,20 +268,19 @@
         ]
         + [sds(received[0].shape, BF16)] * 4
         + [sds((3 * width // 2, width // 2), BF16)] * 4,
-        in_specs=[VM] * 9 + [ANY] * 9,
+        in_specs=[VM] * 9 + [ANY] * 7,
         out_specs=[VM] * 12,
         scratch_shapes=[
-            pltpu.VMEM((edges, width), F32),
-            pltpu.VMEM((points, width), F32),
             pltpu.VMEM((edges, width), BF16),
             nodes,
             nodes,
+            pltpu.VMEM(w1.shape, BF16),
             square,
-            square,
-            square,
+            pltpu.VMEM(n1.shape, BF16),
             square,
             pltpu.VMEM((table, width), BF16),
             pltpu.VMEM((table, width), BF16),
+            nodes,
             pltpu.VMEM((edges, table), BF16),
             pltpu.VMEM((edges, points), BF16),
             pltpu.VMEM((table, edges), BF16),
@@ -366,12 +292,12 @@
             pltpu.VMEM((edges, width), BF16),
             pltpu.VMEM((3 * width, width), BF16),
             pltpu.VMEM((table - mesh_lat.shape[0], width), BF16),
-            pltpu.SemaphoreType.DMA((9,)),
+            pltpu.SemaphoreType.DMA((7,)),
         ],
         compiler_params=pltpu.CompilerParams(vmem_limit_bytes=56 << 20),
         name="main",
         cost_estimate=pl.CostEstimate(
-            flops=16 * edges * width * width,
+            flops=22 * edges * width * width,
             bytes_accessed=14 * edges * width,
             transcendentals=edges * width,
         ),
@@ -382,8 +308,6 @@
         *received,
         edge_gain.reshape(1, width),
         node_gain.reshape(1, width),
-        base,
-        node,
         edge_feat,
         grid_block,
         cot_block,
@@ -476,40 +400,57 @@
     return lax.ppermute(values, ("band", "sector"), sorted(pairs))
 
 
+def total(*terms):
+    return sum(term.astype(F32) for term in terms).astype(BF16)
+
+
 def plus(a, b):
-    return (a.astype(F32) + b.astype(F32)).astype(BF16)
-
-
-def halve(low, high, bit, flip):
-    return plus(jnp.where(bit, high, low), send(jnp.where(bit, low, high), [flip]))
-
-
-def reduce_weights(send_a, send_b, keep_a, keep_b):
+    return total(a, b)
+
+
+def reduce_weights(send_a, send_b, keep_a, keep_b, tails):
     here = coordinates(lax.axis_index("band"), lax.axis_index("sector"))
 
-    def bit(name, k):
+    def bit(name, k=0):
         return ((here[name] >> k) & 1) == 1
 
-    def rows(values, name, k):
-        n = values.shape[0] // 2
-        return halve(values[:n], values[n:], bit(name, k), (name, k))
-
-    def cols(values, name, k):
-        n = values.shape[1] // 2
-        return halve(values[:, :n], values[:, n:], bit(name, k), (name, k))
+    def halve(low, high, name, k=0):
+        mine = bit(name, k)
+        return jnp.where(mine, high, low), send(jnp.where(mine, low, high), [(name, k)])
+
+    def quarter(values, first, second):
+        parts = values.reshape(2, 2, values.shape[0] // 4, values.shape[1])
+        one, two = bit(*first), bit(*second)
+
+        def part(swap_one, swap_two):
+            low, high = (jnp.where(two != swap_two, row[1], row[0]) for row in parts)
+            return jnp.where(one != swap_one, high, low)
+
+        return part(False, False), send(part(True, False), [first]), send(part(False, True), [second]), send(part(True, True), [first, second])
+
+    def halves(values, axis):
+        return jnp.split(values, 2, axis=axis)
 
     part_a = plus(keep_a, send(send_a, [("core", 0)]))
     part_b = plus(keep_b, send(send_b, [("core", 0)]))
-    part_a = cols(rows(part_a, "z", 0), "y", 0)
-    part_b = rows(cols(part_b, "y", 0), "z", 0)
-    part = halve(part_a, part_b, bit("x_lo", 0), ("x_lo", 0))
-    part = rows(rows(part, "z", 1), "z", 2)
-    part = rows(part, "x_hi", 0)
+    a, got_a = halve(*halves(part_a, 0), "z")
+    b, got_b = halve(*halves(part_b, 1), "y")
+    got_a, got_b = tails[0](got_a, got_b)
+    a, got_a = halve(*halves(plus(a, got_a), 1), "y")
+    b, got_b = halve(*halves(plus(b, got_b), 0), "z")
+    got_a, got_b = tails[1](got_a, got_b)
+    both = jnp.stack([plus(a, got_a).reshape(2, -1, a.shape[1]), plus(b, got_b).reshape(2, -1, a.shape[1])])
+    held, *got = quarter(both.reshape(-1, a.shape[1]), ("x_lo", 0), ("z", 1))
+    got = tails[2](*got)
+    part = total(held, *got)
+    held, *got = quarter(part, ("z", 2), ("x_hi", 0))
+    got = tails[3](*got)
+    part = total(held, *got)
     part = plus(part, send(part, [("y", 1)]))
     by_y = send(part, [("y", 0)])
     by_x = send(part, [("x_lo", 0)])
     by_both = send(part, [("y", 0), ("x_lo", 0)])
-    odd_y, odd_x = bit("y", 0), bit("x_lo", 0)
+    odd_y, odd_x = bit("y"), bit("x_lo")
 
     def ordered(mine, other):
         return jnp.concatenate([jnp.where(odd_y, other, mine), jnp.where(odd_y, mine, other)], axis=1)
@@ -537,20 +478,34 @@
     grid_block = grid_lat.reshape(lat_rows * lon_cols, width)
     cot_block = cotangent.reshape(lat_rows * lon_cols, width)
     received = swap(pick(send_rows, mesh_lat))
-    base, node = early(edge_dst, grid_block, edge_feat, w_edge1, w_node1)
     result, dnpre, sg, own_grad, *rest = main(
-        edge_src, edge_dst, mesh_lat, received, edge_gain, node_gain, base, node, edge_feat, grid_block, cot_block, w_edge1, w_edge2, w_node1, w_node2
+        edge_src, edge_dst, mesh_lat, received, edge_gain, node_gain, edge_feat, grid_block, cot_block, w_edge1, w_edge2, w_node1, w_node2
     )
-    grad_w = reduce_weights(*rest[4:])
-    returned = swap(rest[:4])
-    grad_grid = grid_grads(sg, w_edge1, dnpre, w_node1, cot_block)
-    grad_mesh = mesh_grads(send_rows, own_grad, returned)
+    done = {}
+
+    def after_first(*got):
+        done["grid"], *got = lax.optimization_barrier((grid_grads(sg, w_edge1, dnpre, w_node1, cot_block), *got))
+        return got
+
+    def after_second(*got):
+        return got
+
+    def after_third(*got):
+        *parts, first = lax.optimization_barrier((*rest[:4], got[0]))
+        done["returned"] = swap(parts)
+        return (first, *got[1:])
+
+    def after_fourth(*got):
+        done["mesh"], *got = lax.optimization_barrier((mesh_grads(send_rows, own_grad, done["returned"]), *got))
+        return got
+
+    grad_w = reduce_weights(*rest[4:], (after_first, after_second, after_third, after_fourth))
     total_edges = edge_feat.shape[0] * lax.axis_size("band") * lax.axis_size("sector")
     grad_w = grad_w * (1.0 / math.sqrt(total_edges))
     return (
         result.reshape(lat_rows, lon_cols, width),
-        grad_grid.reshape(lat_rows, lon_cols, width),
-        grad_mesh,
+        done["grid"].reshape(lat_rows, lon_cols, width),
+        done["mesh"],
         grad_w,
     )
 

time: 95.6 us -> 88.7 us (0.928)
  waiting for transfers between devices: 27.3 us -> 17.9 us
  starting transfers between devices: 34.6 us -> 42.5 us
  Pallas kernels: 28.7 us -> 23.6 us
    ppermute x14 -> x16, waiting for transfers between devices: 27.2 us -> 14.4 us  [send(): return lax.ppermute(values, ('band', 'sector'), sorted(pairs))]
    pallas_call x1 -> x0, Pallas kernels: 5.96 us -> none  [early(): pl.pallas_call(early_kernel, out_shape=[jax.ShapeDtypeStruct((edges, widt...]
    ppermute x14 -> x16, starting transfers between devices: 30.3 us -> 36.2 us  [send(): return lax.ppermute(values, ('band', 'sector'), sorted(pairs))]
    ppermute x2, starting transfers between devices: 2.05 us -> 4.73 us  [swap(): lax.ppermute(parts[1], 'sector', pairs(1, sectors, sectors))]
    ppermute x2, waiting for transfers between devices: 0.01 us -> 2.21 us  [swap(): lax.ppermute(parts[2], 'band', pairs(0, bands - 1, bands))]
    ppermute x2, waiting for transfers between devices: 0.01 us -> 1.23 us  [swap(): lax.ppermute(parts[1], 'sector', pairs(1, sectors, sectors))]
  transfers between devices with their start and end apart: 22 -> 24, of which waited for: 10 -> 11; matrix products, arithmetic and copies ran while one was open for 2% -> 2% of each run, Pallas kernels for 12% -> 6%
where the time goes in v3:
time: 88.7 us; the launch traced here: 88.5 us
  starting transfers between devices  42.5 us (48%)
  Pallas kernels  23.6 us (27%)
  waiting for transfers between devices  17.9 us (20%)
  other arithmetic  2.32 us (3%)
  local copies, waits for them, and re-layouts  1.21 us (1%)
  between operations  0.92 us (1%)
    ppermute x16, starting transfers between devices, send(): return lax.ppermute(values, ('band', 'sector'), sorted(pairs))  36.2 us
    pallas_call x1, Pallas kernels, main(): pl.pallas_call(main_kernel, out_shape=[sds((points, width), BF16), sds((p...  16.8 us
    ppermute x16, waiting for transfers between devices, send(): return lax.ppermute(values, ('band', 'sector'), sorted(pairs))  14.4 us
    ppermute x2, starting transfers between devices, swap(): lax.ppermute(parts[1], 'sector', pairs(1, sectors, sectors))  4.73 us
    pallas_call x1, Pallas kernels, grid_grads(): pl.pallas_call(grid_kernel, out_shape=jax.ShapeDtypeStruct((points, width...  3.21 us
    ppermute x2, waiting for transfers between devices, swap(): lax.ppermute(parts[2], 'band', pairs(0, bands - 1, bands))  2.21 us
    pallas_call x1, Pallas kernels, mesh_grads(): pl.pallas_call(mesh_kernel, out_shape=jax.ShapeDtypeStruct(own.shape, BF1...  1.8 us
    pallas_call x1, Pallas kernels, pick(): pl.pallas_call(pick_kernel, out_shape=[part] * 4, in_specs=[VM, VM], out_...  1.79 us
  transfers between devices with their start and end apart: 24, of which 11 were waited for; matrix products, arithmetic and copies ran while one was open for 2% of the time, Pallas kernels for 6%

profile of v3, /device:TPU:32, one launch (start us, length us, event | category | flops | bytes accessed | tf_op | source)
XLA Modules:
  0.0 88.5 jit_solution(13603488398573435121)
XLA Ops:
  0.6 1.8 %pick.1 = (bf16[32,512]{1,0:T(8,128)(2,1)}, bf16[32,512]{1,0:T(8,128)(2,1)}, bf16[32,512]{1,0:T(8,128)(2,1)}, bf16[32,512]{1,0:T(8,128)(2,1)}) custom-call(s32[1,128]{1,0:T(1,128)} %bitcast.12, bf16[128,512]{1,0:T(8,128)(2,1)} %mesh_ref.3), custom_call_target="tpu_custom_call" | custom-call | flops 16777216 | bytes 262144 | tf_op jit(solution)/shard_map/pick/pallas_call | solution.py:93
  2.4 2.0 %collective-permute-start.1 = (bf16[32,512]{1,0:T(8,128)(2,1)}, bf16[32,512]{1,0:T(8,128)(2,1)S(1)}, u32[]{:S(2)}, u32[]{:S(2)}) collective-permute-start(bf16[32,512]{1,0:T(8,128)(2,1)} %get-tuple-element.33), channel_id=1, source_target_pairs={{1,2},{3,4},{5,6},{7,8},{9,10},{11,12},{13,14},{15,16},{17,18},{19... | collective-permute-start | bytes 98312 | tf_op jit(solution)/shard_map/ppermute | solution.py:372
  6.3 2.2 %collective-permute-done.2.r2_ref = bf16[32,512]{1,0:T(8,128)(2,1)S(1)} collective-permute-done((bf16[32,512]{1,0:T(8,128)(2,1)}, bf16[32,512]{1,0:T(8,128)(2,1)S(1)}, u32[]{:S(2)}, u32[]{:S(2)}) %collective-permute-start.2) | collective-permute-done | bytes 32800 | tf_op jit(solution)/shard_map/ppermute | solution.py:373
  9.1 16.8 %main.1 = (bf16[512,512]{1,0:T(8,128)(2,1)}, bf16[512,512]{1,0:T(8,128)(2,1)}, bf16[512,512]{1,0:T(8,128)(2,1)}, f32[128,512]{1,0:T(8,128)}, bf16[32,512]{1,0:T(...) custom-call(s32[12,128]{1,0:T(8,128)} %bitcast.15, ...), custom_call_target="tpu_custom_call" | custom-call | flops 8858370048 | bytes 11010048 | tf_op jit(solution)/shard_map/main/pallas_call | solution.py:261
  26.7 1.4 %collective-permute-done.6 = bf16[768,256]{1,0:T(8,128)(2,1)S(1)} collective-permute-done((bf16[768,256]{1,0:T(8,128)(2,1)}, bf16[768,256]{1,0:T(8,128)(2,1)S(1)}, u32[]{:S(2)}, u32[]{:S(2)}) %collective-permute-start.6) | collective-permute-done | bytes 393248 | tf_op jit(solution)/shard_map/ppermute | solution.py:400
  29.3 4.0 %collective-permute-start.7 = (bf16[768,128]{1,0:T(8,128)(2,1)S(1)}, bf16[768,128]{1,0:T(8,128)(2,1)S(1)}, u32[]{:S(2)}, u32[]{:S(2)}) collective-permute-start(bf16[768,128]{1,0:T(8,128)(2,1)S(1)} %broadcast_select_fusion), channel_id=1, source_target_pairs={{0,32},{1,33},{2,34},{3,35},{4,36},{5,37},{6,38},{7,39},{8,40},{9,... | collective-permute-start | bytes 589832 | tf_op jit(solution)/shard_map/ppermute | solution.py:400
  33.4 7.1 %collective-permute-start.5 = (bf16[384,256]{1,0:T(8,128)(2,1)S(1)}, bf16[384,256]{1,0:T(8,128)(2,1)S(1)}, u32[]{:S(2)}, u32[]{:S(2)}) collective-permute-start(bf16[384,256]{1,0:T(8,128)(2,1)S(1)} %broadcast_select_fusion.1), channel_id=1, source_target_pairs={{0,2},{1,3},{2,0},{3,1},{4,6},{5,7},{6,4},{7,5},{8,10},{9,11},{10,... | collective-permute-start | bytes 589832 | tf_op jit(solution)/shard_map/ppermute | solution.py:400
  40.5 3.2 %grid_grads.1 = bf16[512,512]{1,0:T(8,128)(2,1)} custom-call(bf16[512,512]{1,0:T(8,128)(2,1)} %get-tuple-element.37.sg_ref, bf16[1536,512]{1,0:T(8,128)(2,1)} %w1_ref.1, bf16[512,512]{1,0:T(8,128)(2,1)} %get-tuple-element.38.dnpre_ref, bf16[1024,512]{1,0:T(8,128)(2,1)} %n1_ref.1, bf16[512,512]{1,0:T(8,128)(2,1)} %bitcast.10), custom_call_target="tpu_custom_call" | custom-call | flops 536870912 | bytes 3145728 | tf_op jit(solution)/shard_map/grid_grads/pallas_call | solution.py:328
  43.7 1.7 %collective-permute-done.5 = bf16[384,256]{1,0:T(8,128)(2,1)S(1)} collective-permute-done((bf16[384,256]{1,0:T(8,128)(2,1)S(1)}, bf16[384,256]{1,0:T(8,128)(2,1)S(1)}, u32[]{:S(2)}, u32[]{:S(2)}) %collective-permute-start.5) | collective-permute-done | bytes 196640 | tf_op jit(solution)/shard_map/ppermute | solution.py:400
  46.0 1.8 %collective-permute-start.8 = (bf16[384,128]{1,0:T(8,128)(2,1)S(1)}, bf16[384,128]{1,0:T(8,128)(2,1)S(1)}, u32[]{:S(2)}, u32[]{:S(2)}) collective-permute-start(bf16[384,128]{1,0:T(8,128)(2,1)S(1)} %broadcast_select_fusion.3), channel_id=1, source_target_pairs={{0,2},{1,3},{2,0},{3,1},{4,6},{5,7},{6,4},{7,5},{8,10},{9,11},{10,... | collective-permute-start | bytes 294920 | tf_op jit(solution)/shard_map/ppermute | solution.py:400
  47.8 2.4 %collective-permute-done.9 = bf16[384,128]{1,0:T(8,128)(2,1)S(1)} collective-permute-done((bf16[384,128]{1,0:T(8,128)(2,1)S(1)}, bf16[384,128]{1,0:T(8,128)(2,1)S(1)}, u32[]{:S(2)}, u32[]{:S(2)}) %collective-permute-start.9) | collective-permute-done | bytes 98336 | tf_op jit(solution)/shard_map/ppermute | solution.py:400
  50.8 3.7 %collective-permute-start.10 = (bf16[192,128]{1,0:T(8,128)(2,1)S(1)}, bf16[192,128]{1,0:T(8,128)(2,1)S(1)}, u32[]{:S(2)}, u32[]{:S(2)}) collective-permute-start(bf16[192,128]{1,0:T(8,128)(2,1)S(1)} %get-tuple-element.62), channel_id=1, source_target_pairs={{0,128},{1,129},{2,130},{3,131},{4,132},{5,133},{6,134},{7,135},{8... | collective-permute-start | bytes 147464 | tf_op jit(solution)/shard_map/ppermute | solution.py:400
  54.5 1.6 %collective-permute-start.16 = (bf16[192,128]{1,0:T(8,128)(2,1)S(1)}, bf16[192,128]{1,0:T(8,128)(2,1)S(1)}, u32[]{:S(2)}, u32[]{:S(2)}) collective-permute-start(bf16[192,128]{1,0:T(8,128)(2,1)S(1)} %get-tuple-element.61), channel_id=1, source_target_pairs={{0,134},{1,135},{2,132},{3,133},{4,130},{5,131},{6,128},{7,129},{8... | collective-permute-start | bytes 147464 | tf_op jit(solution)/shard_map/ppermute | solution.py:400
  56.9 2.8 %collective-permute-start.12 = (bf16[32,512]{1,0:T(8,128)(2,1)S(1)}, bf16[32,512]{1,0:T(8,128)(2,1)S(1)}, u32[]{:S(2)}, u32[]{:S(2)}) collective-permute-start(bf16[32,512]{1,0:T(8,128)(2,1)S(1)} %copy-done.7), channel_id=1, source_target_pairs={{1,2},{3,4},{5,6},{7,8},{9,10},{11,12},{13,14},{15,16},{17,18},{19... | collective-permute-start | bytes 98312 | tf_op jit(solution)/shard_map/ppermute | solution.py:372
  61.7 2.7 %collective-permute-start.18 = (bf16[48,128]{1,0:T(8,128)(2,1)S(1)}, bf16[48,128]{1,0:T(8,128)(2,1)S(1)}, u32[]{:S(2)}, u32[]{:S(2)}) collective-permute-start(bf16[48,128]{1,0:T(8,128)(2,1)S(1)} %get-tuple-element.66), channel_id=1, source_target_pairs={{0,16},{1,17},{2,18},{3,19},{4,20},{5,21},{6,22},{7,23},{8,24},{9,... | collective-permute-start | bytes 36872 | tf_op jit(solution)/shard_map/ppermute | solution.py:400
  64.4 4.4 %collective-permute-start.19 = (bf16[48,128]{1,0:T(8,128)(2,1)S(1)}, bf16[48,128]{1,0:T(8,128)(2,1)S(1)}, u32[]{:S(2)}, u32[]{:S(2)}) collective-permute-start(bf16[48,128]{1,0:T(8,128)(2,1)S(1)} %get-tuple-element.65), channel_id=1, source_target_pairs={{0,30},{1,31},{2,28},{3,29},{4,26},{5,27},{6,24},{7,25},{8,22},{9,... | collective-permute-start | bytes 36872 | tf_op jit(solution)/shard_map/ppermute | solution.py:400
  69.5 1.8 %mesh_grads.1 = bf16[128,512]{1,0:T(8,128)(2,1)} custom-call(s32[1,128]{1,0:T(1,128)} %bitcast.13, f32[128,512]{1,0:T(8,128)} %get-tuple-element.44.own_ref, bf16[32,512]{1,0:T(8,128)(2,1)} %copy-done.1, bf16[32,512]{1,0:T(8,128)(2,1)} %copy-done.2, bf16[32,512]{1,0:T(8,128)(2,1)} %copy-done.3, bf16[32,512]{1,0:T(8,128)(2,1)} %copy-done.4), custom_call_target="tpu_custom_call" | custom-call | flops 16777216 | bytes 524288 | tf_op jit(solution)/shard_map/mesh_grads/pallas_call | solution.py:352
  71.3 2.2 %collective-permute-done.19 = bf16[48,128]{1,0:T(8,128)(2,1)S(1)} collective-permute-done((bf16[48,128]{1,0:T(8,128)(2,1)S(1)}, bf16[48,128]{1,0:T(8,128)(2,1)S(1)}, u32[]{:S(2)}, u32[]{:S(2)}) %collective-permute-start.19) | collective-permute-done | bytes 12320 | tf_op jit(solution)/shard_map/ppermute | solution.py:400
  73.5 4.5 %collective-permute-start.20 = (bf16[48,128]{1,0:T(8,128)(2,1)S(1)}, bf16[48,128]{1,0:T(8,128)(2,1)S(1)}, u32[]{:S(2)}, u32[]{:S(2)}) collective-permute-start(bf16[48,128]{1,0:T(8,128)(2,1)S(1)} %add_convert_fusion.8), channel_id=1, source_target_pairs={{0,96},{1,97},{2,98},{3,99},{4,100},{5,101},{6,102},{7,103},{8,104... | collective-permute-start | bytes 36872 | tf_op jit(solution)/shard_map/ppermute | solution.py:400
  78.1 1.7 %collective-permute-done.20 = bf16[48,128]{1,0:T(8,128)(2,1)S(1)} collective-permute-done((bf16[48,128]{1,0:T(8,128)(2,1)S(1)}, bf16[48,128]{1,0:T(8,128)(2,1)S(1)}, u32[]{:S(2)}, u32[]{:S(2)}) %collective-permute-start.20) | collective-permute-done | bytes 12320 | tf_op jit(solution)/shard_map/ppermute | solution.py:400
  79.7 1.3 %collective-permute-start.23 = (bf16[48,128]{1,0:T(8,128)(2,1)S(1)}, bf16[48,128]{1,0:T(8,128)(2,1)S(1)}, u32[]{:S(2)}, u32[]{:S(2)}) collective-permute-start(bf16[48,128]{1,0:T(8,128)(2,1)S(1)} %add_convert_fusion.7), channel_id=1, source_target_pairs={{0,32},{1,33},{2,34},{3,35},{4,36},{5,37},{6,38},{7,39},{8,40},{9,... | collective-permute-start | bytes 36872 | tf_op jit(solution)/shard_map/ppermute | solution.py:400
  81.1 3.0 %collective-permute-start.21 = (bf16[48,128]{1,0:T(8,128)(2,1)S(1)}, bf16[48,128]{1,0:T(8,128)(2,1)S(1)}, u32[]{:S(2)}, u32[]{:S(2)}) collective-permute-start(bf16[48,128]{1,0:T(8,128)(2,1)S(1)} %add_convert_fusion.7), channel_id=1, source_target_pairs={{0,160},{1,161},{2,162},{3,163},{4,164},{5,165},{6,166},{7,167},{8... | collective-permute-start | bytes 36872 | tf_op jit(solution)/shard_map/ppermute | solution.py:400
  84.1 1.7 %collective-permute-done.21 = bf16[48,128]{1,0:T(8,128)(2,1)S(1)} collective-permute-done((bf16[48,128]{1,0:T(8,128)(2,1)S(1)}, bf16[48,128]{1,0:T(8,128)(2,1)S(1)}, u32[]{:S(2)}, u32[]{:S(2)}) %collective-permute-start.21) | collective-permute-done | bytes 12320 | tf_op jit(solution)/shard_map/ppermute | solution.py:400
  85.8 2.0 %collective-permute-done.22 = bf16[48,128]{1,0:T(8,128)(2,1)S(1)} collective-permute-done((bf16[48,128]{1,0:T(8,128)(2,1)S(1)}, bf16[48,128]{1,0:T(8,128)(2,1)S(1)}, u32[]{:S(2)}, u32[]{:S(2)}) %collective-permute-start.22) | collective-permute-done | bytes 12320 | tf_op jit(solution)/shard_map/ppermute | solution.py:400
  (73 shorter events, 9.8 us)
Async XLA Ops:
  2.4 2.6 %collective-permute-start = (bf16[32,512]{1,0:T(8,128)(2,1)}, bf16[32,512]{1,0:T(8,128)(2,1)S(1)}, u32[]{:S(2)}, u32[]{:S(2)}) collective-permute-start(bf16[32,512]{1,0:T(8,128)(2,1)} %get-tuple-element.32), channel_id=1, source_target_pairs={{0,1},{2,3},{4,5},{6,7},{8,9},{10,11},{12,13},{14,15},{16,17},{18,... | collective-permute-start | bytes 98312 | tf_op jit(solution)/shard_map/ppermute | solution.py:371
  2.4 3.9 %collective-permute-start.1 = (bf16[32,512]{1,0:T(8,128)(2,1)}, bf16[32,512]{1,0:T(8,128)(2,1)S(1)}, u32[]{:S(2)}, u32[]{:S(2)}) collective-permute-start(bf16[32,512]{1,0:T(8,128)(2,1)} %get-tuple-element.33), channel_id=1, source_target_pairs={{1,2},{3,4},{5,6},{7,8},{9,10},{11,12},{13,14},{15,16},{17,18},{19... | collective-permute-start | bytes 98312 | tf_op jit(solution)/shard_map/ppermute | solution.py:372
  4.4 4.1 %collective-permute-start.2 = (bf16[32,512]{1,0:T(8,128)(2,1)}, bf16[32,512]{1,0:T(8,128)(2,1)S(1)}, u32[]{:S(2)}, u32[]{:S(2)}) collective-permute-start(bf16[32,512]{1,0:T(8,128)(2,1)} %get-tuple-element.34), channel_id=1, source_target_pairs={{0,32},{64,96},{128,160},{192,224},{32,0},{96,64},{160,128},{224,1... | collective-permute-start | bytes 98312 | tf_op jit(solution)/shard_map/ppermute | solution.py:373
  4.4 4.1 %collective-permute-start.3 = (bf16[32,512]{1,0:T(8,128)(2,1)}, bf16[32,512]{1,0:T(8,128)(2,1)S(1)}, u32[]{:S(2)}, u32[]{:S(2)}) collective-permute-start(bf16[32,512]{1,0:T(8,128)(2,1)} %get-tuple-element.35), channel_id=1, source_target_pairs={{32,64},{96,128},{160,192},{64,32},{128,96},{192,160},{33,65},{97,... | collective-permute-start | bytes 98312 | tf_op jit(solution)/shard_map/ppermute | solution.py:374
  26.0 2.2 %collective-permute-start.6 = (bf16[768,256]{1,0:T(8,128)(2,1)}, bf16[768,256]{1,0:T(8,128)(2,1)S(1)}, u32[]{:S(2)}, u32[]{:S(2)}) collective-permute-start(bf16[768,256]{1,0:T(8,128)(2,1)} %get-tuple-element.42), channel_id=1, source_target_pairs={{0,1},{1,0},{2,3},{3,2},{4,5},{5,4},{6,7},{7,6},{8,9},{9,8},{10,11... | collective-permute-start | bytes 1179656 | tf_op jit(solution)/shard_map/ppermute | solution.py:400
  26.3 7.0 %collective-permute-start.4 = (bf16[768,256]{1,0:T(8,128)(2,1)}, bf16[768,256]{1,0:T(8,128)(2,1)S(1)}, u32[]{:S(2)}, u32[]{:S(2)}) collective-permute-start(bf16[768,256]{1,0:T(8,128)(2,1)} %get-tuple-element.40), channel_id=1, source_target_pairs={{0,1},{1,0},{2,3},{3,2},{4,5},{5,4},{6,7},{7,6},{8,9},{9,8},{10,11... | collective-permute-start | bytes 1179656 | tf_op jit(solution)/shard_map/ppermute | solution.py:400
  29.3 14.4 %collective-permute-start.7 = (bf16[768,128]{1,0:T(8,128)(2,1)S(1)}, bf16[768,128]{1,0:T(8,128)(2,1)S(1)}, u32[]{:S(2)}, u32[]{:S(2)}) collective-permute-start(bf16[768,128]{1,0:T(8,128)(2,1)S(1)} %broadcast_select_fusion), channel_id=1, source_target_pairs={{0,32},{1,33},{2,34},{3,35},{4,36},{5,37},{6,38},{7,39},{8,40},{9,... | collective-permute-start | bytes 589832 | tf_op jit(solution)/shard_map/ppermute | solution.py:400
  33.4 12.0 %collective-permute-start.5 = (bf16[384,256]{1,0:T(8,128)(2,1)S(1)}, bf16[384,256]{1,0:T(8,128)(2,1)S(1)}, u32[]{:S(2)}, u32[]{:S(2)}) collective-permute-start(bf16[384,256]{1,0:T(8,128)(2,1)S(1)} %broadcast_select_fusion.1), channel_id=1, source_target_pairs={{0,2},{1,3},{2,0},{3,1},{4,6},{5,7},{6,4},{7,5},{8,10},{9,11},{10,... | collective-permute-start | bytes 589832 | tf_op jit(solution)/shard_map/ppermute | solution.py:400
  45.5 4.7 %collective-permute-start.9 = (bf16[384,128]{1,0:T(8,128)(2,1)S(1)}, bf16[384,128]{1,0:T(8,128)(2,1)S(1)}, u32[]{:S(2)}, u32[]{:S(2)}) collective-permute-start(bf16[384,128]{1,0:T(8,128)(2,1)S(1)} %broadcast_select_fusion.2), channel_id=1, source_target_pairs={{0,32},{1,33},{2,34},{3,35},{4,36},{5,37},{6,38},{7,39},{8,40},{9,... | collective-permute-start | bytes 294920 | tf_op jit(solution)/shard_map/ppermute | solution.py:400
  46.0 4.7 %collective-permute-start.8 = (bf16[384,128]{1,0:T(8,128)(2,1)S(1)}, bf16[384,128]{1,0:T(8,128)(2,1)S(1)}, u32[]{:S(2)}, u32[]{:S(2)}) collective-permute-start(bf16[384,128]{1,0:T(8,128)(2,1)S(1)} %broadcast_select_fusion.3), channel_id=1, source_target_pairs={{0,2},{1,3},{2,0},{3,1},{4,6},{5,7},{6,4},{7,5},{8,10},{9,11},{10,... | collective-permute-start | bytes 294920 | tf_op jit(solution)/shard_map/ppermute | solution.py:400
  50.8 6.1 %collective-permute-start.10 = (bf16[192,128]{1,0:T(8,128)(2,1)S(1)}, bf16[192,128]{1,0:T(8,128)(2,1)S(1)}, u32[]{:S(2)}, u32[]{:S(2)}) collective-permute-start(bf16[192,128]{1,0:T(8,128)(2,1)S(1)} %get-tuple-element.62), channel_id=1, source_target_pairs={{0,128},{1,129},{2,130},{3,131},{4,132},{5,133},{6,134},{7,135},{8... | collective-permute-start | bytes 147464 | tf_op jit(solution)/shard_map/ppermute | solution.py:400
  54.5 5.5 %collective-permute-start.15 = (bf16[192,128]{1,0:T(8,128)(2,1)S(1)}, bf16[192,128]{1,0:T(8,128)(2,1)S(1)}, u32[]{:S(2)}, u32[]{:S(2)}) collective-permute-start(bf16[192,128]{1,0:T(8,128)(2,1)S(1)} %get-tuple-element.60), channel_id=1, source_target_pairs={{0,6},{1,7},{2,4},{3,5},{4,2},{5,3},{6,0},{7,1},{8,14},{9,15},{10,... | collective-permute-start | bytes 147464 | tf_op jit(solution)/shard_map/ppermute | solution.py:400
  54.5 6.2 %collective-permute-start.16 = (bf16[192,128]{1,0:T(8,128)(2,1)S(1)}, bf16[192,128]{1,0:T(8,128)(2,1)S(1)}, u32[]{:S(2)}, u32[]{:S(2)}) collective-permute-start(bf16[192,128]{1,0:T(8,128)(2,1)S(1)} %get-tuple-element.61), channel_id=1, source_target_pairs={{0,134},{1,135},{2,132},{3,133},{4,130},{5,131},{6,128},{7,129},{8... | collective-permute-start | bytes 147464 | tf_op jit(solution)/shard_map/ppermute | solution.py:400
  56.9 4.8 %collective-permute-start.11 = (bf16[32,512]{1,0:T(8,128)(2,1)S(1)}, bf16[32,512]{1,0:T(8,128)(2,1)S(1)}, u32[]{:S(2)}, u32[]{:S(2)}) collective-permute-start(bf16[32,512]{1,0:T(8,128)(2,1)S(1)} %copy-done.8), channel_id=1, source_target_pairs={{0,1},{2,3},{4,5},{6,7},{8,9},{10,11},{12,13},{14,15},{16,17},{18,... | collective-permute-start | bytes 98312 | tf_op jit(solution)/shard_map/ppermute | solution.py:371
  56.9 7.5 %collective-permute-start.12 = (bf16[32,512]{1,0:T(8,128)(2,1)S(1)}, bf16[32,512]{1,0:T(8,128)(2,1)S(1)}, u32[]{:S(2)}, u32[]{:S(2)}) collective-permute-start(bf16[32,512]{1,0:T(8,128)(2,1)S(1)} %copy-done.7), channel_id=1, source_target_pairs={{1,2},{3,4},{5,6},{7,8},{9,10},{11,12},{13,14},{15,16},{17,18},{19... | collective-permute-start | bytes 98312 | tf_op jit(solution)/shard_map/ppermute | solution.py:372
  59.7 9.2 %collective-permute-start.13 = (bf16[32,512]{1,0:T(8,128)(2,1)S(1)}, bf16[32,512]{1,0:T(8,128)(2,1)S(1)}, u32[]{:S(2)}, u32[]{:S(2)}) collective-permute-start(bf16[32,512]{1,0:T(8,128)(2,1)S(1)} %copy-done.6), channel_id=1, source_target_pairs={{0,32},{64,96},{128,160},{192,224},{32,0},{96,64},{160,128},{224,1... | collective-permute-start | bytes 98312 | tf_op jit(solution)/shard_map/ppermute | solution.py:373
  60.0 8.9 %collective-permute-start.14 = (bf16[32,512]{1,0:T(8,128)(2,1)S(1)}, bf16[32,512]{1,0:T(8,128)(2,1)S(1)}, u32[]{:S(2)}, u32[]{:S(2)}) collective-permute-start(bf16[32,512]{1,0:T(8,128)(2,1)S(1)} %copy-done.5), channel_id=1, source_target_pairs={{32,64},{96,128},{160,192},{64,32},{128,96},{192,160},{33,65},{97,... | collective-permute-start | bytes 98312 | tf_op jit(solution)/shard_map/ppermute | solution.py:374
  60.8 10.5 %collective-permute-start.17 = (bf16[48,128]{1,0:T(8,128)(2,1)S(1)}, bf16[48,128]{1,0:T(8,128)(2,1)S(1)}, u32[]{:S(2)}, u32[]{:S(2)}) collective-permute-start(bf16[48,128]{1,0:T(8,128)(2,1)S(1)} %get-tuple-element.67), channel_id=1, source_target_pairs={{0,14},{1,15},{2,12},{3,13},{4,10},{5,11},{6,8},{7,9},{8,6},{9,7},... | collective-permute-start | bytes 36872 | tf_op jit(solution)/shard_map/ppermute | solution.py:400
  61.7 9.6 %collective-permute-start.18 = (bf16[48,128]{1,0:T(8,128)(2,1)S(1)}, bf16[48,128]{1,0:T(8,128)(2,1)S(1)}, u32[]{:S(2)}, u32[]{:S(2)}) collective-permute-start(bf16[48,128]{1,0:T(8,128)(2,1)S(1)} %get-tuple-element.66), channel_id=1, source_target_pairs={{0,16},{1,17},{2,18},{3,19},{4,20},{5,21},{6,22},{7,23},{8,24},{9,... | collective-permute-start | bytes 36872 | tf_op jit(solution)/shard_map/ppermute | solution.py:400
  64.4 9.1 %collective-permute-start.19 = (bf16[48,128]{1,0:T(8,128)(2,1)S(1)}, bf16[48,128]{1,0:T(8,128)(2,1)S(1)}, u32[]{:S(2)}, u32[]{:S(2)}) collective-permute-start(bf16[48,128]{1,0:T(8,128)(2,1)S(1)} %get-tuple-element.65), channel_id=1, source_target_pairs={{0,30},{1,31},{2,28},{3,29},{4,26},{5,27},{6,24},{7,25},{8,22},{9,... | collective-permute-start | bytes 36872 | tf_op jit(solution)/shard_map/ppermute | solution.py:400
  73.5 6.2 %collective-permute-start.20 = (bf16[48,128]{1,0:T(8,128)(2,1)S(1)}, bf16[48,128]{1,0:T(8,128)(2,1)S(1)}, u32[]{:S(2)}, u32[]{:S(2)}) collective-permute-start(bf16[48,128]{1,0:T(8,128)(2,1)S(1)} %add_convert_fusion.8), channel_id=1, source_target_pairs={{0,96},{1,97},{2,98},{3,99},{4,100},{5,101},{6,102},{7,103},{8,104... | collective-permute-start | bytes 36872 | tf_op jit(solution)/shard_map/ppermute | solution.py:400
  79.7 4.4 %collective-permute-start.23 = (bf16[48,128]{1,0:T(8,128)(2,1)S(1)}, bf16[48,128]{1,0:T(8,128)(2,1)S(1)}, u32[]{:S(2)}, u32[]{:S(2)}) collective-permute-start(bf16[48,128]{1,0:T(8,128)(2,1)S(1)} %add_convert_fusion.7), channel_id=1, source_target_pairs={{0,32},{1,33},{2,34},{3,35},{4,36},{5,37},{6,38},{7,39},{8,40},{9,... | collective-permute-start | bytes 36872 | tf_op jit(solution)/shard_map/ppermute | solution.py:400
  81.1 4.7 %collective-permute-start.21 = (bf16[48,128]{1,0:T(8,128)(2,1)S(1)}, bf16[48,128]{1,0:T(8,128)(2,1)S(1)}, u32[]{:S(2)}, u32[]{:S(2)}) collective-permute-start(bf16[48,128]{1,0:T(8,128)(2,1)S(1)} %add_convert_fusion.7), channel_id=1, source_target_pairs={{0,160},{1,161},{2,162},{3,163},{4,164},{5,165},{6,166},{7,167},{8... | collective-permute-start | bytes 36872 | tf_op jit(solution)/shard_map/ppermute | solution.py:400
  84.1 3.7 %collective-permute-start.22 = (bf16[48,128]{1,0:T(8,128)(2,1)S(1)}, bf16[48,128]{1,0:T(8,128)(2,1)S(1)}, u32[]{:S(2)}, u32[]{:S(2)}) collective-permute-start(bf16[48,128]{1,0:T(8,128)(2,1)S(1)} %add_convert_fusion.7), channel_id=1, source_target_pairs={{0,128},{1,129},{2,130},{3,131},{4,132},{5,133},{6,134},{7,135},{8... | collective-permute-start | bytes 36872 | tf_op jit(solution)/shard_map/ppermute | solution.py:400
  (13 other events, 85.8 us)

commit v4 on v3

v4 whole, which is shorter than its diff:
```python
import math

import jax
import jax.numpy as jnp
from jax import lax
from jax.experimental import pallas as pl
from jax.experimental.pallas import tpu as pltpu
from jax.sharding import PartitionSpec as P

EPSILON = 1e-05
BF16 = jnp.bfloat16
F32 = jnp.float32
ANY = pl.BlockSpec(memory_space=pl.ANY)
VM = pl.BlockSpec(memory_space=pltpu.VMEM)


def mm(a, b):
    return lax.dot_general(a, b, (((1,), (0,)), ((), ())), preferred_element_type=F32)


def mm_nt(a, b):
    return lax.dot_general(a, b, (((1,), (1,)), ((), ())), preferred_element_type=F32)


def mm_tn(a, b):
    return lax.dot_general(a, b, (((0,), (0,)), ((), ())), preferred_element_type=F32)


def onehot_rows(index_row, rows):
    n = index_row.shape[1]
    return (lax.broadcasted_iota(jnp.int32, (rows, n), 0) == index_row).astype(BF16)


def onehot_cols(index_col, cols):
    n = index_col.shape[0]
    return (lax.broadcasted_iota(jnp.int32, (n, cols), 1) == index_col).astype(BF16)


LANES = 128


def fill_rows(index_ref, hot_ref):
    for j in range(index_ref.shape[0]):
        hot_ref[:, j * LANES : (j + 1) * LANES] = onehot_rows(index_ref[j : j + 1, :], hot_ref.shape[0])


def fill_cols(index_ref, hot_ref):
    turned = jnp.transpose(index_ref[...])
    for j in range(index_ref.shape[0]):
        hot_ref[j * LANES : (j + 1) * LANES, :] = onehot_cols(turned[:, j : j + 1], hot_ref.shape[1])


def swish_parts(pre):
    sig = 0.5 * jnp.tanh(0.5 * pre) + 0.5
    value = pre * sig
    return value, sig + value * (1.0 - sig)


def norm_parts(raw):
    width = raw.shape[1]
    centred = raw - jnp.sum(raw, axis=1, keepdims=True) * (1.0 / width)
    spread = jnp.sum(centred * centred, axis=1, keepdims=True) * (1.0 / width)
    scale = lax.rsqrt(spread + EPSILON)
    return centred * scale, scale


def norm_back(grad, unit, scale):
    width = grad.shape[1]
    first = jnp.sum(grad, axis=1, keepdims=True) * (1.0 / width)
    second = jnp.sum(grad * unit, axis=1, keepdims=True) * (1.0 / width)
    return (grad - first - unit * second) * scale


def parity(axis):
    return lax.axis_index(axis) % 2


def pick_kernel(send_ref, mesh_ref, *refs):
    outs, picked = refs[:4], refs[4]
    hot = onehot_rows(send_ref[...], mesh_ref.shape[0])
    picked[...] = mm_tn(hot, mesh_ref[...]).astype(BF16)
    margin = outs[0].shape[0]
    for pair, axis in enumerate(("sector", "band")):
        odd = parity(axis)
        for turn in range(2):
            group = 2 * pair + (1 - odd if turn == 0 else odd)
            outs[2 * pair + turn][...] = picked[pl.ds(pl.multiple_of(group * margin, margin), margin), :]


def pick(send_rows, mesh_lat):
    n, width = send_rows.shape[0], mesh_lat.shape[1]
    part = jax.ShapeDtypeStruct((n // 4, width), BF16)
    return pl.pallas_call(
        pick_kernel,
        out_shape=[part] * 4,
        in_specs=[VM, VM],
        out_specs=[VM] * 4,
        scratch_shapes=[pltpu.VMEM((n, width), BF16)],
        name="pick",
        cost_estimate=pl.CostEstimate(flops=2 * n * n * width, bytes_accessed=2 * n * width * 2, transcendentals=0),
    )(send_rows.reshape(1, n), mesh_lat)


TILE = 512


def gray(value):
    return value ^ (value >> 1)


def z_code(z):
    return z ^ (3 * (z >> 2))


def piece_order():
    pieces = []
    for block in range(16):
        code = (block >> 3) | ((block >> 2) & 1) << 1 | ((block >> 1) & 1) << 2
        z = next(i for i in range(8) if z_code(i) == code)
        pieces.append((block & 1) * 8 + z)
    return pieces


NODE_TILE = 512


def main_kernel(*refs):
    (src_hbm, dst_hbm, mesh_hbm, r0_hbm, r1_hbm, r2_hbm, r3_hbm, eg_hbm, ng_hbm), refs = refs[:9], refs[9:]
    (edge_hbm, grid_hbm, cot_hbm, w1_hbm, w2_hbm, n1_hbm, n2_hbm), refs = refs[:7], refs[7:]
    (out_hbm, gg_hbm, own_hbm, far_s_hbm, near_b_hbm, far_b_hbm, sa_hbm, sb_hbm, ka_hbm, kb_hbm), refs = refs[:10], refs[10:]
    (src, dst, parts, eg, ng, edge, grid, cot, w1, w2, n1, n2), refs = refs[:12], refs[12:]
    (out, gg, own_grad, far_s, near_b, far_b, send_a, send_b, keep_a, keep_b), refs = refs[:10], refs[10:]
    table, prod, prod_g, hot_s, hot_d, hot_st, hot_dt, slope, unit, scale, msg, gp, d_pre, gw, borrowed, sems, out_sems = refs

    width = w2.shape[0]
    edges, points, rows_table = edge.shape[0], grid.shape[0], table.shape[0]
    own, margin = mesh_hbm.shape[0], r0_hbm.shape[0]
    tiles = [slice(t * TILE, (t + 1) * TILE) for t in range(edges // TILE)]
    nodes = [slice(t * NODE_TILE, (t + 1) * NODE_TILE) for t in range(points // NODE_TILE)]
    received = [parts.at[pl.ds(i * margin, margin), :] for i in range(4)]
    pairs = (
        (dst_hbm, dst),
        (src_hbm, src),
        (grid_hbm, grid),
        (w1_hbm, w1),
        (edge_hbm, edge),
        (mesh_hbm, table.at[pl.ds(0, own), :]),
        (r0_hbm, received[0]),
        (r1_hbm, received[1]),
        (r2_hbm, received[2]),
        (r3_hbm, received[3]),
        (w2_hbm, w2),
        (eg_hbm, eg),
        (n1_hbm, n1),
        (ng_hbm, ng),
        (n2_hbm, n2),
        (cot_hbm, cot),
    )
    copies = [pltpu.make_async_copy(source, target, sems.at[i]) for i, (source, target) in enumerate(pairs)]
    for copy in copies:
        copy.start()

    results = (
        (out, out_hbm),
        (send_a, sa_hbm),
        (send_b, sb_hbm),
        (keep_a, ka_hbm),
        (keep_b, kb_hbm),
        (near_b, near_b_hbm),
        (far_s, far_s_hbm),
        (far_b, far_b_hbm),
        (own_grad, own_hbm),
        (gg, gg_hbm),
    )
    stores = [pltpu.make_async_copy(source, target, out_sems.at[i]) for i, (source, target) in enumerate(results)]

    copies[0].wait()
    fill_cols(dst, hot_d)
    fill_rows(dst, hot_dt)
    copies[1].wait()
    fill_cols(src, hot_s)
    fill_rows(src, hot_st)
    starts = []
    for pair, axis in enumerate(("sector", "band")):
        odd = parity(axis)
        for slot in (1 - odd, odd):
            starts.append(pl.multiple_of((2 * pair + slot) * margin, margin))
    copies[2].wait()
    copies[3].wait()
    w_edge, w_mesh, w_grid = (w1.at[pl.ds(i * width, width), :] for i in range(3))
    prod_g[...] = mm(grid[...], w_grid[...]).astype(BF16)
    for copy in copies[5:10]:
        copy.wait()
    for start, part in zip(starts, received):
        table[pl.ds(own + start, margin), :] = part[...]
    prod[...] = mm(table[...], w_mesh[...]).astype(BF16)
    copies[4].wait()
    copies[10].wait()
    copies[11].wait()
    edge_gain = eg[...]
    for rows in tiles:
        pre = mm(edge[rows, :], w_edge[...]) + mm(hot_s[rows, :], prod[...]) + mm(hot_d[rows, :], prod_g[...])
        hidden, steep = swish_parts(pre)
        slope[rows, :] = steep
        normed, inv = norm_parts(mm(hidden.astype(BF16), w2[...]))
        unit[rows, :] = normed
        scale[rows, :] = inv
        msg[rows, :] = (normed * edge_gain).astype(BF16)
    for copy in copies[12:]:
        copy.wait()
    node_gain = ng[...]
    n1_agg, n1_grid = (n1.at[pl.ds(i * width, width), :] for i in range(2))
    d_agg = []
    for rows in nodes:
        agg = mm(hot_dt[rows, :], msg[...]).astype(BF16)
        node_hidden, node_slope = swish_parts(mm(agg, n1_agg[...]) + mm(grid[rows, :], n1_grid[...]))
        node_unit, node_inv = norm_parts(mm(node_hidden.astype(BF16), n2[...]))
        out[rows, :] = (grid[rows, :].astype(F32) + node_unit * node_gain).astype(BF16)
        d_raw = norm_back(cot[rows, :].astype(F32) * node_gain, node_unit, node_inv)
        d_hidden = mm_nt(d_raw.astype(BF16), n2[...]).astype(BF16).astype(F32)
        d_pre[rows, :] = (d_hidden * node_slope).astype(BF16)
        d_agg.append(mm_nt(d_pre[rows, :], n1_agg[...]).astype(BF16))
    stores[0].start()
    d_agg = jnp.concatenate(d_agg, axis=0)
    for rows in tiles:
        d_msg = mm(hot_d[rows, :], d_agg)
        d_edge = norm_back(d_msg * edge_gain, unit[rows, :], scale[rows, :])
        d_hid = mm_nt(d_edge.astype(BF16), w2[...]).astype(BF16).astype(F32)
        gp[rows, :] = (d_hid * slope[rows, :]).astype(BF16)
    sm = mm(hot_st[...], gp[...]).astype(BF16)
    sg = mm(hot_dt[...], gp[...]).astype(BF16)
    gw[width : 2 * width, :] = mm_tn(table[...], sm).astype(BF16)
    grad_table = mm_nt(sm, w_mesh[...])
    gw[2 * width : 3 * width, :] = mm_tn(grid[...], sg).astype(BF16)
    gw[0:width, :] = mm_tn(edge[...], gp[...]).astype(BF16)
    core = parity("sector")
    half, quarter = width // 2, width // 4
    own_grad[...] = grad_table[0:own]
    borrowed[...] = grad_table[own:].astype(BF16)
    near_s_rows, far_s_rows, near_b_rows, far_b_rows = (borrowed[pl.ds(start, margin), :] for start in starts)
    kept = keep_a.shape[0]
    for i in range(2):
        send_a[kept + i * margin : kept + (i + 1) * margin, :] = near_s_rows[:, i * half : (i + 1) * half]
    for i in range(4):
        near_b[i * margin : (i + 1) * margin, :] = near_b_rows[:, i * quarter : (i + 1) * quarter]
    far_s[...] = far_s_rows
    far_b[...] = far_b_rows
    piece = gw.shape[0] // (2 * len(piece_order()))
    for i, j in enumerate(piece_order()):
        rows = slice(i * piece, (i + 1) * piece)
        mine = pl.ds(pl.multiple_of((2 * j + core) * piece, piece), piece)
        other = pl.ds(pl.multiple_of((2 * j + 1 - core) * piece, piece), piece)
        send_a[rows, :] = gw[other, 0:half]
        send_b[rows, :] = gw[other, half:width]
        keep_a[rows, :] = gw[mine, 0:half]
        keep_b[rows, :] = gw[mine, half:width]
    for store in stores[1:9]:
        store.start()
    gg[...] = (cot[...].astype(F32) + mm_nt(d_pre[...], n1_grid[...]) + mm_nt(sg, w_grid[...])).astype(BF16)
    stores[9].start()
    for store in stores:
        store.wait()


def main(edge_src, edge_dst, mesh_lat, received, edge_gain, node_gain, edge_feat, grid_block, cot_block, w1, w2, n1, n2):
    edges, width = edge_feat.shape
    points, own = grid_block.shape[0], mesh_lat.shape[0]
    margin = received[0].shape[0]
    table = own + 4 * margin
    half, quarter, kept = width // 2, width // 4, 3 * width // 2
    operands = (
        edge_src.reshape(edges // LANES, LANES),
        edge_dst.reshape(edges // LANES, LANES),
        mesh_lat,
        *received,
        edge_gain.reshape(1, width),
        node_gain.reshape(1, width),
        edge_feat,
        grid_block,
        cot_block,
        w1,
        w2,
        n1,
        n2,
    )
    outs = [
        ((points, width), BF16),
        ((points, width), BF16),
        ((own, width), F32),
        ((margin, width), BF16),
        ((4 * margin, quarter), BF16),
        ((margin, width), BF16),
        ((kept + 2 * margin, half), BF16),
        ((kept, half), BF16),
        ((kept, half), BF16),
        ((kept, half), BF16),
    ]
    local = [pltpu.VMEM(x.shape, x.dtype) for x in operands]
    scratch = [
        ((table, width), BF16),
        ((table, width), BF16),
        ((points, width), BF16),
        ((edges, table), BF16),
        ((edges, points), BF16),
        ((table, edges), BF16),
        ((points, edges), BF16),
        ((edges, width), F32),
        ((edges, width), F32),
        ((edges, 1), F32),
        ((edges, width), BF16),
        ((edges, width), BF16),
        ((points, width), BF16),
        ((3 * width, width), BF16),
        ((4 * margin, width), BF16),
    ]
    return pl.pallas_call(
        main_kernel,
        out_shape=[jax.ShapeDtypeStruct(*shape) for shape in outs],
        in_specs=[ANY] * len(operands),
        out_specs=[ANY] * len(outs),
        scratch_shapes=local[:2]
        + [pltpu.VMEM((4 * margin, width), BF16)]
        + local[7:]
        + [pltpu.VMEM(*shape) for shape in outs + scratch]
        + [pltpu.SemaphoreType.DMA((len(operands),)), pltpu.SemaphoreType.DMA((len(outs),))],
        compiler_params=pltpu.CompilerParams(vmem_limit_bytes=58 << 20),
        name="main",
        cost_estimate=pl.CostEstimate(
            flops=24 * edges * width * width,
            bytes_accessed=12 * edges * width,
            transcendentals=edges * width,
        ),
    )(*operands)


def mesh_kernel(send_ref, own_ref, near_s_ref, far_s_ref, near_b_ref, far_b_ref, out_ref, back):
    margin = far_s_ref.shape[0]
    width = far_s_ref.shape[1]
    for pair, (near, far) in enumerate(((near_s_ref, far_s_ref), (near_b_ref, far_b_ref))):
        odd = parity("band" if pair else "sector")
        first = pl.ds(pl.multiple_of((2 * pair + 1 - odd) * margin, margin), margin)
        second = pl.ds(pl.multiple_of((2 * pair + odd) * margin, margin), margin)
        for i in range(width // near.shape[1]):
            back[first, i * near.shape[1] : (i + 1) * near.shape[1]] = near[i * margin : (i + 1) * margin, :]
        back[second, :] = far[...]
    hot = onehot_rows(send_ref[...], own_ref.shape[0])
    out_ref[...] = (own_ref[...] + mm(hot, back[...])).astype(BF16)


def mesh_grads(send_rows, own, returned):
    n = send_rows.shape[0]
    return pl.pallas_call(
        mesh_kernel,
        out_shape=jax.ShapeDtypeStruct(own.shape, BF16),
        in_specs=[VM] * 6,
        out_specs=VM,
        scratch_shapes=[pltpu.VMEM((n, own.shape[1]), BF16)],
        name="mesh_grads",
        cost_estimate=pl.CostEstimate(flops=2 * n * n * own.shape[1], bytes_accessed=1 << 19, transcendentals=0),
    )(send_rows.reshape(1, n), own, *returned)


def trade(part, axis, turn):
    devices = lax.axis_size(axis)
    last = devices if axis == "sector" else devices - 1
    ups = [(i, (i + 1) % devices) for i in range(turn, last, 2)]
    return lax.ppermute(part, axis, ups + [(j, i) for i, j in ups])


def swap(parts):
    return [trade(parts[2 * pair + turn], axis, turn) for pair, axis in enumerate(("sector", "band")) for turn in range(2)]


def coordinates(band, sector):
    return {
        "x_lo": band // 4,
        "y": gray(band % 4),
        "x_hi": sector // 16,
        "z": z_code(sector % 16 // 2),
        "core": sector % 2,
    }


def send(values, flips):
    place = {}
    for band in range(lax.axis_size("band")):
        for sector in range(lax.axis_size("sector")):
            place[tuple(coordinates(band, sector).values())] = band * lax.axis_size("sector") + sector
    names = list(coordinates(0, 0))
    pairs = []
    for spot, source in place.items():
        target = list(spot)
        for name, bit in flips:
            target[names.index(name)] ^= 1 << bit
        pairs.append((source, place[tuple(target)]))
    return lax.ppermute(values, ("band", "sector"), sorted(pairs))


def total(*terms):
    return sum(term.astype(F32) for term in terms).astype(BF16)


def plus(a, b):
    return total(a, b)


def reduce_weights(near_b, send_a, send_b, keep_a, keep_b, tails):
    here = coordinates(lax.axis_index("band"), lax.axis_index("sector"))

    def bit(name, k=0):
        return ((here[name] >> k) & 1) == 1

    def halve(low, high, name, k=0):
        mine = bit(name, k)
        return jnp.where(mine, high, low), send(jnp.where(mine, low, high), [(name, k)])

    def quarter(values, first, second):
        parts = values.reshape(2, 2, values.shape[0] // 4, values.shape[1])
        one, two = bit(*first), bit(*second)

        def part(swap_one, swap_two):
            low, high = (jnp.where(two != swap_two, row[1], row[0]) for row in parts)
            return jnp.where(one != swap_one, high, low)

        return part(False, False), send(part(True, False), [first]), send(part(False, True), [second]), send(part(True, True), [first, second])

    def halves(values, axis):
        return jnp.split(values, 2, axis=axis)

    got_a = send(send_a, [("core", 0)])
    near_s = got_a[keep_a.shape[0] :]
    part_a = plus(keep_a, got_a[: keep_a.shape[0]])
    part_b = plus(keep_b, send(send_b, [("core", 0)]))
    a, got_a = halve(*halves(part_a, 0), "z")
    left, right = halves(part_b, 1)
    mine = bit("y")
    b = jnp.where(mine, right, left)
    got_b = send(jnp.concatenate([jnp.where(mine, left, right), near_b], axis=0), [("y", 0)])
    got_b, near_b = got_b[: b.shape[0]], got_b[b.shape[0] :]
    got_a, got_b = tails[0](part_b, got_a, got_b, near_s, near_b)
    a, got_a = halve(*halves(plus(a, got_a), 1), "y")
    b, got_b = halve(*halves(plus(b, got_b), 0), "z")
    got_a, got_b = tails[1](got_a, got_b)
    both = jnp.stack([plus(a, got_a).reshape(2, -1, a.shape[1]), plus(b, got_b).reshape(2, -1, a.shape[1])])
    held, *got = quarter(both.reshape(-1, a.shape[1]), ("x_lo", 0), ("z", 1))
    got = tails[2](*got)
    part = total(held, *got)
    held, *got = quarter(part, ("z", 2), ("x_hi", 0))
    got = tails[3](*got)
    part = total(held, *got)
    part = plus(part, send(part, [("y", 1)]))
    by_y = send(part, [("y", 0)])
    by_x = send(part, [("x_lo", 0)])
    by_both = send(part, [("y", 0), ("x_lo", 0)])
    odd_y, odd_x = bit("y"), bit("x_lo")

    def ordered(mine, other):
        return jnp.concatenate([jnp.where(odd_y, other, mine), jnp.where(odd_y, mine, other)], axis=1)

    near, far = ordered(part, by_y), ordered(by_x, by_both)
    return jnp.concatenate([jnp.where(odd_x, far, near), jnp.where(odd_x, near, far)], axis=1).astype(F32)


def shards(
    grid_lat,
    mesh_lat,
    edge_feat,
    edge_src,
    edge_dst,
    send_rows,
    w_edge1,
    w_edge2,
    edge_gain,
    w_node1,
    w_node2,
    node_gain,
    cotangent,
):
    lat_rows, lon_cols, width = grid_lat.shape
    grid_block = grid_lat.reshape(lat_rows * lon_cols, width)
    cot_block = cotangent.reshape(lat_rows * lon_cols, width)
    received = swap(pick(send_rows, mesh_lat))
    result, grad_grid, own_grad, far_s, near_b, far_b, *sums = main(
        edge_src, edge_dst, mesh_lat, received, edge_gain, node_gain, edge_feat, grid_block, cot_block, w_edge1, w_edge2, w_node1, w_node2
    )
    done = {}

    def after_first(part, got_a, got_b, near_s, near_b):
        far, _ = lax.optimization_barrier((far_s, part))
        far = trade(far, "sector", 1)
        done["near"] = near_s, near_b
        done["far_s"], *got = lax.optimization_barrier((far, got_a, got_b))
        done["first"] = got[0]
        return got

    def after_second(got_a, got_b):
        far, _ = lax.optimization_barrier((far_b, done["first"]))
        far = trade(far, "band", 1)
        done["far_b"], *got = lax.optimization_barrier((far, got_a, got_b))
        return got

    def after_third(*got):
        return got

    def after_fourth(*got):
        near_s, near_b = done["near"]
        grads = mesh_grads(send_rows, own_grad, (near_s, done["far_s"], near_b, done["far_b"]))
        done["mesh"], *got = lax.optimization_barrier((grads, *got))
        return got

    grad_w = reduce_weights(near_b, *sums, (after_first, after_second, after_third, after_fourth))
    total_edges = edge_feat.shape[0] * lax.axis_size("band") * lax.axis_size("sector")
    grad_w = grad_w * (1.0 / math.sqrt(total_edges))
    return (
        result.reshape(lat_rows, lon_cols, width),
        grad_grid.reshape(lat_rows, lon_cols, width),
        done["mesh"],
        grad_w,
    )


def solution(mesh):
    rows = P(("band", "sector"), None)
    flat = P(("band", "sector"))
    grid = P("band", "sector", None)
    in_specs = (grid, rows, rows, flat, flat, flat, P(), P(), P(), P(), P(), P(), grid)
    out_specs = (grid, grid, rows, P("sector", None))
    return jax.shard_map(shards, mesh=mesh, in_specs=in_specs, out_specs=out_specs, check_vma=False)
```

time: 88.7 us -> 89.6 us (1.010)
  Pallas kernels: 23.6 us -> 20.6 us
  waiting for transfers between devices: 17.9 us -> 20.5 us
    ppermute x8 -> x6, waiting for transfers between devices: 3.45 us -> 8.23 us  [trade(): return lax.ppermute(part, axis, ups + [(j, i) for i, j in ups])]
    ppermute x8 -> x6, starting transfers between devices: 6.35 us -> 3.26 us  [trade(): return lax.ppermute(part, axis, ups + [(j, i) for i, j in ups])]
    pallas_call x2 -> x1, Pallas kernels: 20 us -> 17 us  [main(): pl.pallas_call(main_kernel, out_shape=[jax.ShapeDtypeStruct(*shape) for s...]
    ppermute x16, starting transfers between devices: 36.2 us -> 39.1 us  [send(): return lax.ppermute(values, ('band', 'sector'), sorted(pairs))]
    ppermute x16, waiting for transfers between devices: 14.4 us -> 12.2 us  [send(): return lax.ppermute(values, ('band', 'sector'), sorted(pairs))]
    slice x0 -> x3, local copies, waits for them, and re-layouts: none -> 1.24 us  [the longest x2 0.62 us: reduce_weights(): got_b, near_b = (got_b[:b.shape[0]], got_b[b.shape[0]:])]
  transfers between devices with their start and end apart: 24 -> 22, of which waited for: 11 -> 14; matrix products, arithmetic and copies ran while one was open for 2% -> 3% of each run, Pallas kernels for 6% -> 2%
where the time goes in v4:
time: 89.6 us; the launch traced here: 88.6 us
  starting transfers between devices  42.4 us (47%)
  Pallas kernels  20.6 us (23%)
  waiting for transfers between devices  20.5 us (23%)
  other arithmetic  2.32 us (3%)
  local copies, waits for them, and re-layouts  1.87 us (2%)
  between operations  0.97 us (1%)
    ppermute x16, starting transfers between devices, send(): return lax.ppermute(values, ('band', 'sector'), sorted(pairs))  39.1 us
    pallas_call x1, Pallas kernels, main(): pl.pallas_call(main_kernel, out_shape=[jax.ShapeDtypeStruct(*shape) for s...  17 us
    ppermute x16, waiting for transfers between devices, send(): return lax.ppermute(values, ('band', 'sector'), sorted(pairs))  12.2 us
    ppermute x6, waiting for transfers between devices, trade(): return lax.ppermute(part, axis, ups + [(j, i) for i, j in ups])  8.23 us
    ppermute x6, starting transfers between devices, trade(): return lax.ppermute(part, axis, ups + [(j, i) for i, j in ups])  3.26 us
    pallas_call x1, Pallas kernels, mesh_grads(): pl.pallas_call(mesh_kernel, out_shape=jax.ShapeDtypeStruct(own.shape, BF1...  1.81 us
  transfers between devices with their start and end apart: 22, of which 14 were waited for; matrix products, arithmetic and copies ran while one was open for 3% of the time, Pallas kernels for 2%

profile of v4, /device:TPU:32, one launch (start us, length us, event | category | flops | bytes accessed | tf_op | source)
XLA Modules:
  0.0 88.6 jit_solution(4290328554464502844)
XLA Ops:
  0.6 1.8 %pick.1 = (bf16[32,512]{1,0:T(8,128)(2,1)}, bf16[32,512]{1,0:T(8,128)(2,1)}, bf16[32,512]{1,0:T(8,128)(2,1)}, bf16[32,512]{1,0:T(8,128)(2,1)}) custom-call(s32[1,128]{1,0:T(1,128)} %bitcast.9, bf16[128,512]{1,0:T(8,128)(2,1)} %refs_2_.1), custom_call_target="tpu_custom_call" | custom-call | flops 16777216 | bytes 262144 | tf_op jit(solution)/shard_map/pick/pallas_call | solution.py:93
  2.4 2.0 %collective-permute-start.1 = (bf16[32,512]{1,0:T(8,128)(2,1)}, bf16[32,512]{1,0:T(8,128)(2,1)S(1)}, u32[]{:S(2)}, u32[]{:S(2)}) collective-permute-start(bf16[32,512]{1,0:T(8,128)(2,1)} %get-tuple-element.31), channel_id=1, source_target_pairs={{1,2},{3,4},{5,6},{7,8},{9,10},{11,12},{13,14},{15,16},{17,18},{19... | collective-permute-start | bytes 98312 | tf_op jit(solution)/shard_map/ppermute | solution.py:367
  5.1 1.2 %collective-permute-done.1.refs_4_ = bf16[32,512]{1,0:T(8,128)(2,1)S(1)} collective-permute-done((bf16[32,512]{1,0:T(8,128)(2,1)}, bf16[32,512]{1,0:T(8,128)(2,1)S(1)}, u32[]{:S(2)}, u32[]{:S(2)}) %collective-permute-start.1) | collective-permute-done | bytes 32800 | tf_op jit(solution)/shard_map/ppermute | solution.py:367
  6.3 2.2 %collective-permute-done.2.refs_5_ = bf16[32,512]{1,0:T(8,128)(2,1)S(1)} collective-permute-done((bf16[32,512]{1,0:T(8,128)(2,1)}, bf16[32,512]{1,0:T(8,128)(2,1)S(1)}, u32[]{:S(2)}, u32[]{:S(2)}) %collective-permute-start.2) | collective-permute-done | bytes 32800 | tf_op jit(solution)/shard_map/ppermute | solution.py:367
  9.1 17.0 %main.1 = (bf16[512,512]{1,0:T(8,128)(2,1)}, bf16[512,512]{1,0:T(8,128)(2,1)}, f32[128,512]{1,0:T(8,128)}, bf16[32,512]{1,0:T(8,128)(2,1)}, bf16[128,128]{1,0:T(...) custom-call(s32[12,128]{1,0:T(8,128)} %bitcast.13, ...), custom_call_target="tpu_custom_call" | custom-call | flops 9663676416 | bytes 9437184 | tf_op jit(solution)/shard_map/main/pallas_call | solution.py:316
  26.8 1.4 %collective-permute-done.5 = bf16[768,256]{1,0:T(8,128)(2,1)S(1)} collective-permute-done((bf16[768,256]{1,0:T(8,128)(2,1)}, bf16[768,256]{1,0:T(8,128)(2,1)S(1)}, u32[]{:S(2)}, u32[]{:S(2)}) %collective-permute-start.5) | collective-permute-done | bytes 393248 | tf_op jit(solution)/shard_map/ppermute | solution.py:396
  28.2 1.1 %add_convert_fusion.1 = bf16[768,256]{1,0:T(8,128)(2,1)S(1)} fusion(bf16[768,256]{1,0:T(8,128)(2,1)S(1)} %collective-permute-done.5, bf16[768,256]{1,0:T(8,128)(2,1)} %get-tuple-element.39), kind=kLoop, calls=%fused_computation.1 | loop fusion | flops 786432 | bytes 1179648 | tf_op jit(solution)/shard_map/convert_element_type | solution.py:400
  29.3 4.0 %collective-permute-start.8 = (bf16[896,128]{1,0:T(8,128)(2,1)S(1)}, bf16[896,128]{1,0:T(8,128)(2,1)S(1)}, u32[]{:S(2)}, u32[]{:S(2)}) collective-permute-start(bf16[896,128]{1,0:T(8,128)(2,1)S(1)} %pad_maximum_fusion), channel_id=1, source_target_pairs={{0,32},{1,33},{2,34},{3,35},{4,36},{5,37},{6,38},{7,39},{8,40},{9,... | collective-permute-start | bytes 688136 | tf_op jit(solution)/shard_map/ppermute | solution.py:396
  33.5 7.1 %collective-permute-start.7 = (bf16[384,256]{1,0:T(8,128)(2,1)S(1)}, bf16[384,256]{1,0:T(8,128)(2,1)S(1)}, u32[]{:S(2)}, u32[]{:S(2)}) collective-permute-start(bf16[384,256]{1,0:T(8,128)(2,1)S(1)} %broadcast_select_fusion.1), channel_id=1, source_target_pairs={{0,2},{1,3},{2,0},{3,1},{4,6},{5,7},{6,4},{7,5},{8,10},{9,11},{10,... | collective-permute-start | bytes 589832 | tf_op jit(solution)/shard_map/ppermute | solution.py:396
  40.6 4.8 %collective-permute-done.6.far_s_ref = bf16[32,512]{1,0:T(8,128)(2,1)S(1)} collective-permute-done((bf16[32,512]{1,0:T(8,128)(2,1)S(1)}, bf16[32,512]{1,0:T(8,128)(2,1)S(1)}, u32[]{:S(2)}, u32[]{:S(2)}) %collective-permute-start.6) | collective-permute-done | bytes 32800 | tf_op jit(solution)/shard_map/ppermute | solution.py:367
  46.4 1.9 %collective-permute-start.11 = (bf16[384,128]{1,0:T(8,128)(2,1)S(1)}, bf16[384,128]{1,0:T(8,128)(2,1)S(1)}, u32[]{:S(2)}, u32[]{:S(2)}) collective-permute-start(bf16[384,128]{1,0:T(8,128)(2,1)S(1)} %broadcast_select_fusion.2), channel_id=1, source_target_pairs={{0,2},{1,3},{2,0},{3,1},{4,6},{5,7},{6,4},{7,5},{8,10},{9,11},{10,... | collective-permute-start | bytes 294920 | tf_op jit(solution)/shard_map/ppermute | solution.py:396
  49.0 1.7 %collective-permute-done.10 = bf16[384,128]{1,0:T(8,128)(2,1)S(1)} collective-permute-done((bf16[384,128]{1,0:T(8,128)(2,1)S(1)}, bf16[384,128]{1,0:T(8,128)(2,1)S(1)}, u32[]{:S(2)}, u32[]{:S(2)}) %collective-permute-start.10) | collective-permute-done | bytes 98336 | tf_op jit(solution)/shard_map/ppermute | solution.py:396
  51.2 8.8 %collective-permute-start.12 = (bf16[192,128]{1,0:T(8,128)(2,1)S(1)}, bf16[192,128]{1,0:T(8,128)(2,1)S(1)}, u32[]{:S(2)}, u32[]{:S(2)}) collective-permute-start(bf16[192,128]{1,0:T(8,128)(2,1)S(1)} %get-tuple-element.56), channel_id=1, source_target_pairs={{0,128},{1,129},{2,130},{3,131},{4,132},{5,133},{6,134},{7,135},{8... | collective-permute-start | bytes 147464 | tf_op jit(solution)/shard_map/ppermute | solution.py:396
  59.9 2.5 %collective-permute-start.14 = (bf16[192,128]{1,0:T(8,128)(2,1)S(1)}, bf16[192,128]{1,0:T(8,128)(2,1)S(1)}, u32[]{:S(2)}, u32[]{:S(2)}) collective-permute-start(bf16[192,128]{1,0:T(8,128)(2,1)S(1)} %get-tuple-element.58), channel_id=1, source_target_pairs={{0,132},{1,133},{2,134},{3,135},{4,128},{5,129},{6,130},{7,131},{8... | collective-permute-start | bytes 147464 | tf_op jit(solution)/shard_map/ppermute | solution.py:396
  62.4 2.5 %collective-permute-done.13 = bf16[192,128]{1,0:T(8,128)(2,1)S(1)} collective-permute-done((bf16[192,128]{1,0:T(8,128)(2,1)S(1)}, bf16[192,128]{1,0:T(8,128)(2,1)S(1)}, u32[]{:S(2)}, u32[]{:S(2)}) %collective-permute-start.13) | collective-permute-done | bytes 49184 | tf_op jit(solution)/shard_map/ppermute | solution.py:396
  64.9 0.9 %collective-permute-done.14 = bf16[192,128]{1,0:T(8,128)(2,1)S(1)} collective-permute-done((bf16[192,128]{1,0:T(8,128)(2,1)S(1)}, bf16[192,128]{1,0:T(8,128)(2,1)S(1)}, u32[]{:S(2)}, u32[]{:S(2)}) %collective-permute-start.14) | collective-permute-done | bytes 49184 | tf_op jit(solution)/shard_map/ppermute | solution.py:396
  65.9 4.0 %collective-permute-start.17 = (bf16[48,128]{1,0:T(8,128)(2,1)S(1)}, bf16[48,128]{1,0:T(8,128)(2,1)S(1)}, u32[]{:S(2)}, u32[]{:S(2)}) collective-permute-start(bf16[48,128]{1,0:T(8,128)(2,1)S(1)} %get-tuple-element.61), channel_id=1, source_target_pairs={{0,30},{1,31},{2,28},{3,29},{4,26},{5,27},{6,24},{7,25},{8,22},{9,... | collective-permute-start | bytes 36872 | tf_op jit(solution)/shard_map/ppermute | solution.py:396
  70.7 3.3 %collective-permute-start.15 = (bf16[48,128]{1,0:T(8,128)(2,1)S(1)}, bf16[48,128]{1,0:T(8,128)(2,1)S(1)}, u32[]{:S(2)}, u32[]{:S(2)}) collective-permute-start(bf16[48,128]{1,0:T(8,128)(2,1)S(1)} %get-tuple-element.63), channel_id=1, source_target_pairs={{0,14},{1,15},{2,12},{3,13},{4,10},{5,11},{6,8},{7,9},{8,6},{9,7},... | collective-permute-start | bytes 36872 | tf_op jit(solution)/shard_map/ppermute | solution.py:396
  75.2 1.8 %mesh_grads.1 = bf16[128,512]{1,0:T(8,128)(2,1)} custom-call(s32[1,128]{1,0:T(1,128)} %bitcast.10, f32[128,512]{1,0:T(8,128)} %get-tuple-element.36.own_ref, bf16[64,256]{1,0:T(8,128)(2,1)} %slice.86.near_s_ref, bf16[32,512]{1,0:T(8,128)(2,1)} %copy-done.2, bf16[128,128]{1,0:T(8,128)(2,1)} %slice.89.near_b_ref, bf16[32,512]{1,0:T(8,128)(2,1)} %copy-done.3), custom_call_target="tpu_custom_call" | custom-call | flops 16777216 | bytes 524288 | tf_op jit(solution)/shard_map/mesh_grads/pallas_call | solution.py:352
  77.4 2.4 %collective-permute-start.18 = (bf16[48,128]{1,0:T(8,128)(2,1)S(1)}, bf16[48,128]{1,0:T(8,128)(2,1)S(1)}, u32[]{:S(2)}, u32[]{:S(2)}) collective-permute-start(bf16[48,128]{1,0:T(8,128)(2,1)S(1)} %add_convert_fusion.8), channel_id=1, source_target_pairs={{0,96},{1,97},{2,98},{3,99},{4,100},{5,101},{6,102},{7,103},{8,104... | collective-permute-start | bytes 36872 | tf_op jit(solution)/shard_map/ppermute | solution.py:396
  79.8 2.6 %collective-permute-done.18 = bf16[48,128]{1,0:T(8,128)(2,1)S(1)} collective-permute-done((bf16[48,128]{1,0:T(8,128)(2,1)S(1)}, bf16[48,128]{1,0:T(8,128)(2,1)S(1)}, u32[]{:S(2)}, u32[]{:S(2)}) %collective-permute-start.18) | collective-permute-done | bytes 12320 | tf_op jit(solution)/shard_map/ppermute | solution.py:396
  82.5 0.8 collective-permute-start.20
  83.4 2.6 %collective-permute-start.19 = (bf16[48,128]{1,0:T(8,128)(2,1)S(1)}, bf16[48,128]{1,0:T(8,128)(2,1)S(1)}, u32[]{:S(2)}, u32[]{:S(2)}) collective-permute-start(bf16[48,128]{1,0:T(8,128)(2,1)S(1)} %add_convert_fusion.7), channel_id=1, source_target_pairs={{0,160},{1,161},{2,162},{3,163},{4,164},{5,165},{6,166},{7,167},{8... | collective-permute-start | bytes 36872 | tf_op jit(solution)/shard_map/ppermute | solution.py:396
  86.3 1.6 %collective-permute-done.19 = bf16[48,128]{1,0:T(8,128)(2,1)S(1)} collective-permute-done((bf16[48,128]{1,0:T(8,128)(2,1)S(1)}, bf16[48,128]{1,0:T(8,128)(2,1)S(1)}, u32[]{:S(2)}, u32[]{:S(2)}) %collective-permute-start.19) | collective-permute-done | bytes 12320 | tf_op jit(solution)/shard_map/ppermute | solution.py:396
  (65 shorter events, 7.7 us)
Async XLA Ops:
  2.4 2.6 %collective-permute-start = (bf16[32,512]{1,0:T(8,128)(2,1)}, bf16[32,512]{1,0:T(8,128)(2,1)S(1)}, u32[]{:S(2)}, u32[]{:S(2)}) collective-permute-start(bf16[32,512]{1,0:T(8,128)(2,1)} %get-tuple-element.30), channel_id=1, source_target_pairs={{0,1},{2,3},{4,5},{6,7},{8,9},{10,11},{12,13},{14,15},{16,17},{18,... | collective-permute-start | bytes 98312 | tf_op jit(solution)/shard_map/ppermute | solution.py:367
  2.4 3.9 %collective-permute-start.1 = (bf16[32,512]{1,0:T(8,128)(2,1)}, bf16[32,512]{1,0:T(8,128)(2,1)S(1)}, u32[]{:S(2)}, u32[]{:S(2)}) collective-permute-start(bf16[32,512]{1,0:T(8,128)(2,1)} %get-tuple-element.31), channel_id=1, source_target_pairs={{1,2},{3,4},{5,6},{7,8},{9,10},{11,12},{13,14},{15,16},{17,18},{19... | collective-permute-start | bytes 98312 | tf_op jit(solution)/shard_map/ppermute | solution.py:367
  4.4 4.1 %collective-permute-start.2 = (bf16[32,512]{1,0:T(8,128)(2,1)}, bf16[32,512]{1,0:T(8,128)(2,1)S(1)}, u32[]{:S(2)}, u32[]{:S(2)}) collective-permute-start(bf16[32,512]{1,0:T(8,128)(2,1)} %get-tuple-element.32), channel_id=1, source_target_pairs={{0,32},{64,96},{128,160},{192,224},{32,0},{96,64},{160,128},{224,1... | collective-permute-start | bytes 98312 | tf_op jit(solution)/shard_map/ppermute | solution.py:367
  4.4 4.1 %collective-permute-start.3 = (bf16[32,512]{1,0:T(8,128)(2,1)}, bf16[32,512]{1,0:T(8,128)(2,1)S(1)}, u32[]{:S(2)}, u32[]{:S(2)}) collective-permute-start(bf16[32,512]{1,0:T(8,128)(2,1)} %get-tuple-element.33), channel_id=1, source_target_pairs={{32,64},{96,128},{160,192},{64,32},{128,96},{192,160},{33,65},{97,... | collective-permute-start | bytes 98312 | tf_op jit(solution)/shard_map/ppermute | solution.py:367
  26.2 2.0 %collective-permute-start.5 = (bf16[768,256]{1,0:T(8,128)(2,1)}, bf16[768,256]{1,0:T(8,128)(2,1)S(1)}, u32[]{:S(2)}, u32[]{:S(2)}) collective-permute-start(bf16[768,256]{1,0:T(8,128)(2,1)} %get-tuple-element.40), channel_id=1, source_target_pairs={{0,1},{1,0},{2,3},{3,2},{4,5},{5,4},{6,7},{7,6},{8,9},{9,8},{10,11... | collective-permute-start | bytes 1179656 | tf_op jit(solution)/shard_map/ppermute | solution.py:396
  26.3 7.0 %collective-permute-start.4 = (bf16[832,256]{1,0:T(8,128)(2,1)}, bf16[832,256]{1,0:T(8,128)(2,1)S(1)}, u32[]{:S(2)}, u32[]{:S(2)}) collective-permute-start(bf16[832,256]{1,0:T(8,128)(2,1)} %get-tuple-element.37), channel_id=1, source_target_pairs={{0,1},{1,0},{2,3},{3,2},{4,5},{5,4},{6,7},{7,6},{8,9},{9,8},{10,11... | collective-permute-start | bytes 1277960 | tf_op jit(solution)/shard_map/ppermute | solution.py:396
  29.3 11.2 %collective-permute-start.8 = (bf16[896,128]{1,0:T(8,128)(2,1)S(1)}, bf16[896,128]{1,0:T(8,128)(2,1)S(1)}, u32[]{:S(2)}, u32[]{:S(2)}) collective-permute-start(bf16[896,128]{1,0:T(8,128)(2,1)S(1)} %pad_maximum_fusion), channel_id=1, source_target_pairs={{0,32},{1,33},{2,34},{3,35},{4,36},{5,37},{6,38},{7,39},{8,40},{9,... | collective-permute-start | bytes 688136 | tf_op jit(solution)/shard_map/ppermute | solution.py:396
  33.4 14.9 %copy-start.4 = (bf16[32,512]{1,0:T(8,128)(2,1)S(1)}, bf16[32,512]{1,0:T(8,128)(2,1)}, u32[]{:S(2)}) copy-start(bf16[32,512]{1,0:T(8,128)(2,1)} %get-tuple-element.47) | copy-start | bytes 98308
  33.5 12.3 %collective-permute-start.7 = (bf16[384,256]{1,0:T(8,128)(2,1)S(1)}, bf16[384,256]{1,0:T(8,128)(2,1)S(1)}, u32[]{:S(2)}, u32[]{:S(2)}) collective-permute-start(bf16[384,256]{1,0:T(8,128)(2,1)S(1)} %broadcast_select_fusion.1), channel_id=1, source_target_pairs={{0,2},{1,3},{2,0},{3,1},{4,6},{5,7},{6,4},{7,5},{8,10},{9,11},{10,... | collective-permute-start | bytes 589832 | tf_op jit(solution)/shard_map/ppermute | solution.py:396
  40.5 4.8 %collective-permute-start.6 = (bf16[32,512]{1,0:T(8,128)(2,1)S(1)}, bf16[32,512]{1,0:T(8,128)(2,1)S(1)}, u32[]{:S(2)}, u32[]{:S(2)}) collective-permute-start(bf16[32,512]{1,0:T(8,128)(2,1)S(1)} %copy-done.5), channel_id=1, source_target_pairs={{1,2},{3,4},{5,6},{7,8},{9,10},{11,12},{13,14},{15,16},{17,18},{19... | collective-permute-start | bytes 98312 | tf_op jit(solution)/shard_map/ppermute | solution.py:367
  46.0 4.7 %collective-permute-start.10 = (bf16[384,128]{1,0:T(8,128)(2,1)S(1)}, bf16[384,128]{1,0:T(8,128)(2,1)S(1)}, u32[]{:S(2)}, u32[]{:S(2)}) collective-permute-start(bf16[384,128]{1,0:T(8,128)(2,1)S(1)} %broadcast_select_fusion.3), channel_id=1, source_target_pairs={{0,32},{1,33},{2,34},{3,35},{4,36},{5,37},{6,38},{7,39},{8,40},{9,... | collective-permute-start | bytes 294920 | tf_op jit(solution)/shard_map/ppermute | solution.py:396
  46.4 4.6 %collective-permute-start.11 = (bf16[384,128]{1,0:T(8,128)(2,1)S(1)}, bf16[384,128]{1,0:T(8,128)(2,1)S(1)}, u32[]{:S(2)}, u32[]{:S(2)}) collective-permute-start(bf16[384,128]{1,0:T(8,128)(2,1)S(1)} %broadcast_select_fusion.2), channel_id=1, source_target_pairs={{0,2},{1,3},{2,0},{3,1},{4,6},{5,7},{6,4},{7,5},{8,10},{9,11},{10,... | collective-permute-start | bytes 294920 | tf_op jit(solution)/shard_map/ppermute | solution.py:396
  48.3 0.7 collective-permute-start.9
  49.0 26.2 %copy-start.3 = (bf16[32,512]{1,0:T(8,128)(2,1)}, bf16[32,512]{1,0:T(8,128)(2,1)S(1)}, u32[]{:S(2)}) copy-start(bf16[32,512]{1,0:T(8,128)(2,1)S(1)} %collective-permute-done.9.far_b_ref) | copy-start | bytes 98308
  51.2 11.2 %collective-permute-start.12 = (bf16[192,128]{1,0:T(8,128)(2,1)S(1)}, bf16[192,128]{1,0:T(8,128)(2,1)S(1)}, u32[]{:S(2)}, u32[]{:S(2)}) collective-permute-start(bf16[192,128]{1,0:T(8,128)(2,1)S(1)} %get-tuple-element.56), channel_id=1, source_target_pairs={{0,128},{1,129},{2,130},{3,131},{4,132},{5,133},{6,134},{7,135},{8... | collective-permute-start | bytes 147464 | tf_op jit(solution)/shard_map/ppermute | solution.py:396
  59.9 5.0 %collective-permute-start.13 = (bf16[192,128]{1,0:T(8,128)(2,1)S(1)}, bf16[192,128]{1,0:T(8,128)(2,1)S(1)}, u32[]{:S(2)}, u32[]{:S(2)}) collective-permute-start(bf16[192,128]{1,0:T(8,128)(2,1)S(1)} %get-tuple-element.57), channel_id=1, source_target_pairs={{0,4},{1,5},{2,6},{3,7},{4,0},{5,1},{6,2},{7,3},{8,12},{9,13},{10,... | collective-permute-start | bytes 147464 | tf_op jit(solution)/shard_map/ppermute | solution.py:396
  59.9 5.9 %collective-permute-start.14 = (bf16[192,128]{1,0:T(8,128)(2,1)S(1)}, bf16[192,128]{1,0:T(8,128)(2,1)S(1)}, u32[]{:S(2)}, u32[]{:S(2)}) collective-permute-start(bf16[192,128]{1,0:T(8,128)(2,1)S(1)} %get-tuple-element.58), channel_id=1, source_target_pairs={{0,132},{1,133},{2,134},{3,135},{4,128},{5,129},{6,130},{7,131},{8... | collective-permute-start | bytes 147464 | tf_op jit(solution)/shard_map/ppermute | solution.py:396
  65.9 11.1 %collective-permute-start.17 = (bf16[48,128]{1,0:T(8,128)(2,1)S(1)}, bf16[48,128]{1,0:T(8,128)(2,1)S(1)}, u32[]{:S(2)}, u32[]{:S(2)}) collective-permute-start(bf16[48,128]{1,0:T(8,128)(2,1)S(1)} %get-tuple-element.61), channel_id=1, source_target_pairs={{0,30},{1,31},{2,28},{3,29},{4,26},{5,27},{6,24},{7,25},{8,22},{9,... | collective-permute-start | bytes 36872 | tf_op jit(solution)/shard_map/ppermute | solution.py:396
  69.9 7.1 %collective-permute-start.16 = (bf16[48,128]{1,0:T(8,128)(2,1)S(1)}, bf16[48,128]{1,0:T(8,128)(2,1)S(1)}, u32[]{:S(2)}, u32[]{:S(2)}) collective-permute-start(bf16[48,128]{1,0:T(8,128)(2,1)S(1)} %get-tuple-element.62), channel_id=1, source_target_pairs={{0,16},{1,17},{2,18},{3,19},{4,20},{5,21},{6,22},{7,23},{8,24},{9,... | collective-permute-start | bytes 36872 | tf_op jit(solution)/shard_map/ppermute | solution.py:396
  70.7 6.7 %collective-permute-start.15 = (bf16[48,128]{1,0:T(8,128)(2,1)S(1)}, bf16[48,128]{1,0:T(8,128)(2,1)S(1)}, u32[]{:S(2)}, u32[]{:S(2)}) collective-permute-start(bf16[48,128]{1,0:T(8,128)(2,1)S(1)} %get-tuple-element.63), channel_id=1, source_target_pairs={{0,14},{1,15},{2,12},{3,13},{4,10},{5,11},{6,8},{7,9},{8,6},{9,7},... | collective-permute-start | bytes 36872 | tf_op jit(solution)/shard_map/ppermute | solution.py:396
  77.4 5.0 %collective-permute-start.18 = (bf16[48,128]{1,0:T(8,128)(2,1)S(1)}, bf16[48,128]{1,0:T(8,128)(2,1)S(1)}, u32[]{:S(2)}, u32[]{:S(2)}) collective-permute-start(bf16[48,128]{1,0:T(8,128)(2,1)S(1)} %add_convert_fusion.8), channel_id=1, source_target_pairs={{0,96},{1,97},{2,98},{3,99},{4,100},{5,101},{6,102},{7,103},{8,104... | collective-permute-start | bytes 36872 | tf_op jit(solution)/shard_map/ppermute | solution.py:396
  82.4 3.8 %collective-permute-start.21 = (bf16[48,128]{1,0:T(8,128)(2,1)S(1)}, bf16[48,128]{1,0:T(8,128)(2,1)S(1)}, u32[]{:S(2)}, u32[]{:S(2)}) collective-permute-start(bf16[48,128]{1,0:T(8,128)(2,1)S(1)} %add_convert_fusion.7), channel_id=1, source_target_pairs={{0,32},{1,33},{2,34},{3,35},{4,36},{5,37},{6,38},{7,39},{8,40},{9,... | collective-permute-start | bytes 36872 | tf_op jit(solution)/shard_map/ppermute | solution.py:396
  82.5 3.8 %collective-permute-start.20 = (bf16[48,128]{1,0:T(8,128)(2,1)S(1)}, bf16[48,128]{1,0:T(8,128)(2,1)S(1)}, u32[]{:S(2)}, u32[]{:S(2)}) collective-permute-start(bf16[48,128]{1,0:T(8,128)(2,1)S(1)} %add_convert_fusion.7), channel_id=1, source_target_pairs={{0,128},{1,129},{2,130},{3,131},{4,132},{5,133},{6,134},{7,135},{8... | collective-permute-start | bytes 36872 | tf_op jit(solution)/shard_map/ppermute | solution.py:396
  83.4 4.6 %collective-permute-start.19 = (bf16[48,128]{1,0:T(8,128)(2,1)S(1)}, bf16[48,128]{1,0:T(8,128)(2,1)S(1)}, u32[]{:S(2)}, u32[]{:S(2)}) collective-permute-start(bf16[48,128]{1,0:T(8,128)(2,1)S(1)} %add_convert_fusion.7), channel_id=1, source_target_pairs={{0,160},{1,161},{2,162},{3,163},{4,164},{5,165},{6,166},{7,167},{8... | collective-permute-start | bytes 36872 | tf_op jit(solution)/shard_map/ppermute | solution.py:396
  (8 other events, 34.4 us)

commit v5 on v4

--- a/solution.py
+++ b/solution.py
@@ -102,6 +102,7 @@
 
 
 TILE = 512
+VMEM_LIMIT = 58 << 20
 
 
 def gray(value):
@@ -198,6 +199,8 @@
     copies[10].wait()
     copies[11].wait()
     edge_gain = eg[...]
+    for copy in copies[12:]:
+        copy.wait()
     for rows in tiles:
         pre = mm(edge[rows, :], w_edge[...]) + mm(hot_s[rows, :], prod[...]) + mm(hot_d[rows, :], prod_g[...])
         hidden, steep = swish_parts(pre)
@@ -206,8 +209,6 @@
         unit[rows, :] = normed
         scale[rows, :] = inv
         msg[rows, :] = (normed * edge_gain).astype(BF16)
-    for copy in copies[12:]:
-        copy.wait()
     node_gain = ng[...]
     n1_agg, n1_grid = (n1.at[pl.ds(i * width, width), :] for i in range(2))
     d_agg = []
@@ -323,7 +324,7 @@
         + local[7:]
         + [pltpu.VMEM(*shape) for shape in outs + scratch]
         + [pltpu.SemaphoreType.DMA((len(operands),)), pltpu.SemaphoreType.DMA((len(outs),))],
-        compiler_params=pltpu.CompilerParams(vmem_limit_bytes=58 << 20),
+        compiler_params=pltpu.CompilerParams(vmem_limit_bytes=VMEM_LIMIT),
         name="main",
         cost_estimate=pl.CostEstimate(
             flops=24 * edges * width * width,
@@ -348,16 +349,24 @@
 
 
 def mesh_grads(send_rows, own, returned):
-    n = send_rows.shape[0]
+    n, width = send_rows.shape[0], own.shape[1]
+
+    def tail(array):
+        rows = n // 4 * width // array.shape[1]
+        return pl.BlockSpec((rows, array.shape[1]), lambda i: (array.shape[0] // rows - 1, 0))
+
+    whole = lambda array: pl.BlockSpec(array.shape, lambda i: (0, 0))
+    send_row = send_rows.reshape(1, n)
     return pl.pallas_call(
         mesh_kernel,
         out_shape=jax.ShapeDtypeStruct(own.shape, BF16),
-        in_specs=[VM] * 6,
-        out_specs=VM,
-        scratch_shapes=[pltpu.VMEM((n, own.shape[1]), BF16)],
+        grid=(1,),
+        in_specs=[whole(send_row), whole(own)] + [tail(array) for array in returned],
+        out_specs=whole(own),
+        scratch_shapes=[pltpu.VMEM((n, width), BF16)],
         name="mesh_grads",
-        cost_estimate=pl.CostEstimate(flops=2 * n * n * own.shape[1], bytes_accessed=1 << 19, transcendentals=0),
-    )(send_rows.reshape(1, n), own, *returned)
+        cost_estimate=pl.CostEstimate(flops=2 * n * n * width, bytes_accessed=1 << 19, transcendentals=0),
+    )(send_row, own, *returned)
 
 
 def trade(part, axis, turn):
@@ -427,16 +436,15 @@
     def halves(values, axis):
         return jnp.split(values, 2, axis=axis)
 
-    got_a = send(send_a, [("core", 0)])
-    near_s = got_a[keep_a.shape[0] :]
+    near_s = got_a = send(send_a, [("core", 0)])
     part_a = plus(keep_a, got_a[: keep_a.shape[0]])
     part_b = plus(keep_b, send(send_b, [("core", 0)]))
     a, got_a = halve(*halves(part_a, 0), "z")
     left, right = halves(part_b, 1)
     mine = bit("y")
     b = jnp.where(mine, right, left)
-    got_b = send(jnp.concatenate([jnp.where(mine, left, right), near_b], axis=0), [("y", 0)])
-    got_b, near_b = got_b[: b.shape[0]], got_b[b.shape[0] :]
+    near_b = got_b = send(jnp.concatenate([jnp.where(mine, left, right), near_b], axis=0), [("y", 0)])
+    got_b = got_b[: b.shape[0]]
     got_a, got_b = tails[0](part_b, got_a, got_b, near_s, near_b)
     a, got_a = halve(*halves(plus(a, got_a), 1), "y")
     b, got_b = halve(*halves(plus(b, got_b), 0), "z")
@@ -487,19 +495,19 @@
 
     def after_first(part, got_a, got_b, near_s, near_b):
         far, _ = lax.optimization_barrier((far_s, part))
-        far = trade(far, "sector", 1)
+        done["far_s"] = trade(far, "sector", 1)
         done["near"] = near_s, near_b
-        done["far_s"], *got = lax.optimization_barrier((far, got_a, got_b))
-        done["first"] = got[0]
+        done["first"] = got_a
+        return got_a, got_b
+
+    def after_second(*got):
+        far, _ = lax.optimization_barrier((far_b, done["first"]))
+        done["far_b"] = trade(far, "band", 1)
+        done["far_s"], *got = lax.optimization_barrier((done["far_s"], *got))
         return got
 
-    def after_second(got_a, got_b):
-        far, _ = lax.optimization_barrier((far_b, done["first"]))
-        far = trade(far, "band", 1)
-        done["far_b"], *got = lax.optimization_barrier((far, got_a, got_b))
-        return got
-
     def after_third(*got):
+        done["far_b"], *got = lax.optimization_barrier((done["far_b"], *got))
         return got
 
     def after_fourth(*got):

time: 89.6 us -> 89.3 us (level)
  the two profiles are of different devices: /device:TPU:32 before, /device:TPU:8 now
where the time goes in v5:
time: 89.3 us; the launch traced here: 89.1 us
  starting transfers between devices  39.2 us (44%)
  waiting for transfers between devices  25.9 us (29%)
  Pallas kernels  20 us (22%)
  other arithmetic  2.33 us (3%)
  between operations  1.06 us (1%)
    ppermute x16, starting transfers between devices, send(): return lax.ppermute(values, ('band', 'sector'), sorted(pairs))  21.1 us
    ppermute x6, starting transfers between devices, trade(): return lax.ppermute(part, axis, ups + [(j, i) for i, j in ups])  18.1 us
    pallas_call x1, Pallas kernels, main(): pl.pallas_call(main_kernel, out_shape=[jax.ShapeDtypeStruct(*shape) for s...  16.4 us
    ppermute x16, waiting for transfers between devices, send(): return lax.ppermute(values, ('band', 'sector'), sorted(pairs))  15.1 us
    ppermute x6, waiting for transfers between devices, trade(): return lax.ppermute(part, axis, ups + [(j, i) for i, j in ups])  10.8 us
    pallas_call x1, Pallas kernels, mesh_grads(): pl.pallas_call(mesh_kernel, out_shape=jax.ShapeDtypeStruct(own.shape, BF1...  1.81 us
    pallas_call x1, Pallas kernels, pick(): pl.pallas_call(pick_kernel, out_shape=[part] * 4, in_specs=[VM, VM], out_...  1.79 us
  transfers between devices with their start and end apart: 22, of which 8 were waited for; matrix products, arithmetic and copies ran while one was open for 2% of the time, Pallas kernels for 2%

profile of v5, /device:TPU:8, one launch (start us, length us, event | category | flops | bytes accessed | tf_op | source)
XLA Modules:
  0.0 89.1 jit_solution(7972729997308069897)
XLA Ops:
  0.6 1.8 %pick.1 = (bf16[32,512]{1,0:T(8,128)(2,1)}, bf16[32,512]{1,0:T(8,128)(2,1)}, bf16[32,512]{1,0:T(8,128)(2,1)}, bf16[32,512]{1,0:T(8,128)(2,1)}) custom-call(s32[1,128]{1,0:T(1,128)} %bitcast.9, bf16[128,512]{1,0:T(8,128)(2,1)} %refs_2_.1), custom_call_target="tpu_custom_call" | custom-call | flops 16777216 | bytes 262144 | tf_op jit(solution)/shard_map/pick/pallas_call | solution.py:93
  2.4 8.4 %collective-permute-start.1 = (bf16[32,512]{1,0:T(8,128)(2,1)}, bf16[32,512]{1,0:T(8,128)(2,1)S(1)}, u32[]{:S(2)}, u32[]{:S(2)}) collective-permute-start(bf16[32,512]{1,0:T(8,128)(2,1)} %get-tuple-element.32), channel_id=1, source_target_pairs={{1,2},{3,4},{5,6},{7,8},{9,10},{11,12},{13,14},{15,16},{17,18},{19... | collective-permute-start | bytes 98312 | tf_op jit(solution)/shard_map/ppermute | solution.py:376
  11.3 4.3 %collective-permute-start.3 = (bf16[32,512]{1,0:T(8,128)(2,1)}, bf16[32,512]{1,0:T(8,128)(2,1)S(1)}, u32[]{:S(2)}, u32[]{:S(2)}) collective-permute-start(bf16[32,512]{1,0:T(8,128)(2,1)} %get-tuple-element.34), channel_id=1, source_target_pairs={{32,64},{96,128},{160,192},{64,32},{128,96},{192,160},{33,65},{97,... | collective-permute-start | bytes 98312 | tf_op jit(solution)/shard_map/ppermute | solution.py:376
  15.7 2.0 %collective-permute-done.3.refs_6_ = bf16[32,512]{1,0:T(8,128)(2,1)S(1)} collective-permute-done((bf16[32,512]{1,0:T(8,128)(2,1)}, bf16[32,512]{1,0:T(8,128)(2,1)S(1)}, u32[]{:S(2)}, u32[]{:S(2)}) %collective-permute-start.3) | collective-permute-done | bytes 32800 | tf_op jit(solution)/shard_map/ppermute | solution.py:376
  17.7 0.6 copy-done.11
  18.3 16.4 %main.1 = (bf16[512,512]{1,0:T(8,128)(2,1)}, bf16[512,512]{1,0:T(8,128)(2,1)}, f32[128,512]{1,0:T(8,128)}, bf16[32,512]{1,0:T(8,128)(2,1)}, bf16[128,128]{1,0:T(...) custom-call(s32[12,128]{1,0:T(8,128)} %bitcast.13, ...), custom_call_target="tpu_custom_call" | custom-call | flops 9663676416 | bytes 9437184 | tf_op jit(solution)/shard_map/main/pallas_call | solution.py:317
  35.3 1.4 %collective-permute-done.5 = bf16[768,256]{1,0:T(8,128)(2,1)S(1)} collective-permute-done((bf16[768,256]{1,0:T(8,128)(2,1)}, bf16[768,256]{1,0:T(8,128)(2,1)S(1)}, u32[]{:S(2)}, u32[]{:S(2)}) %collective-permute-start.5) | collective-permute-done | bytes 393248 | tf_op jit(solution)/shard_map/ppermute | solution.py:405
  36.7 1.1 %add_convert_fusion.1 = bf16[768,256]{1,0:T(8,128)(2,1)S(1)} fusion(bf16[768,256]{1,0:T(8,128)(2,1)S(1)} %collective-permute-done.5, bf16[768,256]{1,0:T(8,128)(2,1)} %get-tuple-element.40), kind=kLoop, calls=%fused_computation.1 | loop fusion | flops 786432 | bytes 1179648 | tf_op jit(solution)/shard_map/convert_element_type | solution.py:409
  38.3 7.3 %collective-permute-done.9.near_b_ref = bf16[896,128]{1,0:T(8,128)(2,1)S(1)} collective-permute-done((bf16[896,128]{1,0:T(8,128)(2,1)S(1)}, bf16[896,128]{1,0:T(8,128)(2,1)S(1)}, u32[]{:S(2)}, u32[]{:S(2)}) %collective-permute-start.9) | collective-permute-done | bytes 229408 | tf_op jit(solution)/shard_map/ppermute | solution.py:405
  46.0 1.1 %collective-permute-start.8 = (bf16[384,128]{1,0:T(8,128)(2,1)S(1)}, bf16[384,128]{1,0:T(8,128)(2,1)S(1)}, u32[]{:S(2)}, u32[]{:S(2)}) collective-permute-start(bf16[384,128]{1,0:T(8,128)(2,1)S(1)} %broadcast_select_fusion.3), channel_id=1, source_target_pairs={{0,32},{1,33},{2,34},{3,35},{4,36},{5,37},{6,38},{7,39},{8,40},{9,... | collective-permute-start | bytes 294920 | tf_op jit(solution)/shard_map/ppermute | solution.py:405
  47.1 7.0 %collective-permute-done.6.far_s_ref = bf16[32,512]{1,0:T(8,128)(2,1)S(1)} collective-permute-done((bf16[32,512]{1,0:T(8,128)(2,1)S(1)}, bf16[32,512]{1,0:T(8,128)(2,1)S(1)}, u32[]{:S(2)}, u32[]{:S(2)}) %collective-permute-start.6) | collective-permute-done | bytes 32800 | tf_op jit(solution)/shard_map/ppermute | solution.py:376
  54.3 5.2 %collective-permute-start.13 = (bf16[192,128]{1,0:T(8,128)(2,1)S(1)}, bf16[192,128]{1,0:T(8,128)(2,1)S(1)}, u32[]{:S(2)}, u32[]{:S(2)}) collective-permute-start(bf16[192,128]{1,0:T(8,128)(2,1)S(1)} %get-tuple-element.59), channel_id=1, source_target_pairs={{0,4},{1,5},{2,6},{3,7},{4,0},{5,1},{6,2},{7,3},{8,12},{9,13},{10,... | collective-permute-start | bytes 147464 | tf_op jit(solution)/shard_map/ppermute | solution.py:405
  59.5 4.9 %collective-permute-start.11 = (bf16[32,512]{1,0:T(8,128)(2,1)S(1)}, bf16[32,512]{1,0:T(8,128)(2,1)S(1)}, u32[]{:S(2)}, u32[]{:S(2)}) collective-permute-start(bf16[32,512]{1,0:T(8,128)(2,1)S(1)} %copy-done.6), channel_id=1, source_target_pairs={{32,64},{96,128},{160,192},{64,32},{128,96},{192,160},{33,65},{97,... | collective-permute-start | bytes 98312 | tf_op jit(solution)/shard_map/ppermute | solution.py:376
  64.4 1.9 %collective-permute-done.11.far_b_ref = bf16[32,512]{1,0:T(8,128)(2,1)S(1)} collective-permute-done((bf16[32,512]{1,0:T(8,128)(2,1)S(1)}, bf16[32,512]{1,0:T(8,128)(2,1)S(1)}, u32[]{:S(2)}, u32[]{:S(2)}) %collective-permute-start.11) | collective-permute-done | bytes 32800 | tf_op jit(solution)/shard_map/ppermute | solution.py:376
  66.5 1.1 %collective-permute-start.16 = (bf16[48,128]{1,0:T(8,128)(2,1)S(1)}, bf16[48,128]{1,0:T(8,128)(2,1)S(1)}, u32[]{:S(2)}, u32[]{:S(2)}) collective-permute-start(bf16[48,128]{1,0:T(8,128)(2,1)S(1)} %get-tuple-element.64), channel_id=1, source_target_pairs={{0,16},{1,17},{2,18},{3,19},{4,20},{5,21},{6,22},{7,23},{8,24},{9,... | collective-permute-start | bytes 36872 | tf_op jit(solution)/shard_map/ppermute | solution.py:405
  67.6 5.1 %collective-permute-start.15 = (bf16[48,128]{1,0:T(8,128)(2,1)S(1)}, bf16[48,128]{1,0:T(8,128)(2,1)S(1)}, u32[]{:S(2)}, u32[]{:S(2)}) collective-permute-start(bf16[48,128]{1,0:T(8,128)(2,1)S(1)} %get-tuple-element.65), channel_id=1, source_target_pairs={{0,14},{1,15},{2,12},{3,13},{4,10},{5,11},{6,8},{7,9},{8,6},{9,7},... | collective-permute-start | bytes 36872 | tf_op jit(solution)/shard_map/ppermute | solution.py:405
  72.7 1.8 %mesh_grads.1 = bf16[128,512]{1,0:T(8,128)(2,1)} custom-call(s32[1,128]{1,0:T(1,128)} %bitcast.10, f32[128,512]{1,0:T(8,128)} %get-tuple-element.37.own_ref, bf16[832,256]{1,0:T(8,128)(2,1)} %copy-done, bf16[32,512]{1,0:T(8,128)(2,1)} %copy-done.4, bf16[896,128]{1,0:T(8,128)(2,1)} %copy-done.1, bf16[32,512]{1,0:T(8,128)(2,1)} %copy-done.5), custom_call_target="tpu_custom_call" | custom-call | flops 16777216 | bytes 524288 | tf_op jit(solution)/shard_map/mesh_grads/pallas_call | solution.py:360
  74.5 2.1 %collective-permute-start.18 = (bf16[48,128]{1,0:T(8,128)(2,1)S(1)}, bf16[48,128]{1,0:T(8,128)(2,1)S(1)}, u32[]{:S(2)}, u32[]{:S(2)}) collective-permute-start(bf16[48,128]{1,0:T(8,128)(2,1)S(1)} %add_convert_fusion.8), channel_id=1, source_target_pairs={{0,96},{1,97},{2,98},{3,99},{4,100},{5,101},{6,102},{7,103},{8,104... | collective-permute-start | bytes 36872 | tf_op jit(solution)/shard_map/ppermute | solution.py:405
  76.6 1.7 %collective-permute-done.18 = bf16[48,128]{1,0:T(8,128)(2,1)S(1)} collective-permute-done((bf16[48,128]{1,0:T(8,128)(2,1)S(1)}, bf16[48,128]{1,0:T(8,128)(2,1)S(1)}, u32[]{:S(2)}, u32[]{:S(2)}) %collective-permute-start.18) | collective-permute-done | bytes 12320 | tf_op jit(solution)/shard_map/ppermute | solution.py:405
  78.3 3.8 %collective-permute-start.21 = (bf16[48,128]{1,0:T(8,128)(2,1)S(1)}, bf16[48,128]{1,0:T(8,128)(2,1)S(1)}, u32[]{:S(2)}, u32[]{:S(2)}) collective-permute-start(bf16[48,128]{1,0:T(8,128)(2,1)S(1)} %add_convert_fusion.7), channel_id=1, source_target_pairs={{0,32},{1,33},{2,34},{3,35},{4,36},{5,37},{6,38},{7,39},{8,40},{9,... | collective-permute-start | bytes 36872 | tf_op jit(solution)/shard_map/ppermute | solution.py:405
  82.2 1.6 %collective-permute-start.20 = (bf16[48,128]{1,0:T(8,128)(2,1)S(1)}, bf16[48,128]{1,0:T(8,128)(2,1)S(1)}, u32[]{:S(2)}, u32[]{:S(2)}) collective-permute-start(bf16[48,128]{1,0:T(8,128)(2,1)S(1)} %add_convert_fusion.7), channel_id=1, source_target_pairs={{0,128},{1,129},{2,130},{3,131},{4,132},{5,133},{6,134},{7,135},{8... | collective-permute-start | bytes 36872 | tf_op jit(solution)/shard_map/ppermute | solution.py:405
  83.9 2.0 %collective-permute-done.20 = bf16[48,128]{1,0:T(8,128)(2,1)S(1)} collective-permute-done((bf16[48,128]{1,0:T(8,128)(2,1)S(1)}, bf16[48,128]{1,0:T(8,128)(2,1)S(1)}, u32[]{:S(2)}, u32[]{:S(2)}) %collective-permute-start.20) | collective-permute-done | bytes 12320 | tf_op jit(solution)/shard_map/ppermute | solution.py:405
  85.9 2.5 %collective-permute-done.19 = bf16[48,128]{1,0:T(8,128)(2,1)S(1)} collective-permute-done((bf16[48,128]{1,0:T(8,128)(2,1)S(1)}, bf16[48,128]{1,0:T(8,128)(2,1)S(1)}, u32[]{:S(2)}, u32[]{:S(2)}) %collective-permute-start.19) | collective-permute-done | bytes 12320 | tf_op jit(solution)/shard_map/ppermute | solution.py:405
  88.4 0.7 convert_multiply_fusion
  (66 shorter events, 2.2 us)
Async XLA Ops:
  2.4 13.2 %collective-permute-start = (bf16[32,512]{1,0:T(8,128)(2,1)}, bf16[32,512]{1,0:T(8,128)(2,1)S(1)}, u32[]{:S(2)}, u32[]{:S(2)}) collective-permute-start(bf16[32,512]{1,0:T(8,128)(2,1)} %get-tuple-element.31), channel_id=1, source_target_pairs={{0,1},{2,3},{4,5},{6,7},{8,9},{10,11},{12,13},{14,15},{16,17},{18,... | collective-permute-start | bytes 98312 | tf_op jit(solution)/shard_map/ppermute | solution.py:376
  2.4 13.2 %collective-permute-start.1 = (bf16[32,512]{1,0:T(8,128)(2,1)}, bf16[32,512]{1,0:T(8,128)(2,1)S(1)}, u32[]{:S(2)}, u32[]{:S(2)}) collective-permute-start(bf16[32,512]{1,0:T(8,128)(2,1)} %get-tuple-element.32), channel_id=1, source_target_pairs={{1,2},{3,4},{5,6},{7,8},{9,10},{11,12},{13,14},{15,16},{17,18},{19... | collective-permute-start | bytes 98312 | tf_op jit(solution)/shard_map/ppermute | solution.py:376
  10.9 4.8 %collective-permute-start.2 = (bf16[32,512]{1,0:T(8,128)(2,1)}, bf16[32,512]{1,0:T(8,128)(2,1)S(1)}, u32[]{:S(2)}, u32[]{:S(2)}) collective-permute-start(bf16[32,512]{1,0:T(8,128)(2,1)} %get-tuple-element.33), channel_id=1, source_target_pairs={{0,32},{64,96},{128,160},{192,224},{32,0},{96,64},{160,128},{224,1... | collective-permute-start | bytes 98312 | tf_op jit(solution)/shard_map/ppermute | solution.py:376
  11.3 6.4 %collective-permute-start.3 = (bf16[32,512]{1,0:T(8,128)(2,1)}, bf16[32,512]{1,0:T(8,128)(2,1)S(1)}, u32[]{:S(2)}, u32[]{:S(2)}) collective-permute-start(bf16[32,512]{1,0:T(8,128)(2,1)} %get-tuple-element.34), channel_id=1, source_target_pairs={{32,64},{96,128},{160,192},{64,32},{128,96},{192,160},{33,65},{97,... | collective-permute-start | bytes 98312 | tf_op jit(solution)/shard_map/ppermute | solution.py:376
  34.7 2.0 %collective-permute-start.5 = (bf16[768,256]{1,0:T(8,128)(2,1)}, bf16[768,256]{1,0:T(8,128)(2,1)S(1)}, u32[]{:S(2)}, u32[]{:S(2)}) collective-permute-start(bf16[768,256]{1,0:T(8,128)(2,1)} %get-tuple-element.41), channel_id=1, source_target_pairs={{0,1},{1,0},{2,3},{3,2},{4,5},{5,4},{6,7},{7,6},{8,9},{9,8},{10,11... | collective-permute-start | bytes 1179656 | tf_op jit(solution)/shard_map/ppermute | solution.py:405
  34.9 3.1 %collective-permute-start.4 = (bf16[832,256]{1,0:T(8,128)(2,1)}, bf16[832,256]{1,0:T(8,128)(2,1)S(1)}, u32[]{:S(2)}, u32[]{:S(2)}) collective-permute-start(bf16[832,256]{1,0:T(8,128)(2,1)} %get-tuple-element.38), channel_id=1, source_target_pairs={{0,1},{1,0},{2,3},{3,2},{4,5},{5,4},{6,7},{7,6},{8,9},{9,8},{10,11... | collective-permute-start | bytes 1277960 | tf_op jit(solution)/shard_map/ppermute | solution.py:405
  37.9 7.7 %collective-permute-start.9 = (bf16[896,128]{1,0:T(8,128)(2,1)S(1)}, bf16[896,128]{1,0:T(8,128)(2,1)S(1)}, u32[]{:S(2)}, u32[]{:S(2)}) collective-permute-start(bf16[896,128]{1,0:T(8,128)(2,1)S(1)} %pad_maximum_fusion), channel_id=1, source_target_pairs={{0,32},{1,33},{2,34},{3,35},{4,36},{5,37},{6,38},{7,39},{8,40},{9,... | collective-permute-start | bytes 688136 | tf_op jit(solution)/shard_map/ppermute | solution.py:405
  38.2 21.3 %copy-start.6 = (bf16[32,512]{1,0:T(8,128)(2,1)S(1)}, bf16[32,512]{1,0:T(8,128)(2,1)}, u32[]{:S(2)}) copy-start(bf16[32,512]{1,0:T(8,128)(2,1)} %get-tuple-element.47) | copy-start | bytes 98308
  38.2 7.7 %collective-permute-start.7 = (bf16[384,256]{1,0:T(8,128)(2,1)S(1)}, bf16[384,256]{1,0:T(8,128)(2,1)S(1)}, u32[]{:S(2)}, u32[]{:S(2)}) collective-permute-start(bf16[384,256]{1,0:T(8,128)(2,1)S(1)} %broadcast_select_fusion.1), channel_id=1, source_target_pairs={{0,2},{1,3},{2,0},{3,1},{4,6},{5,7},{6,4},{7,5},{8,10},{9,11},{10,... | collective-permute-start | bytes 589832 | tf_op jit(solution)/shard_map/ppermute | solution.py:405
  45.7 8.3 %collective-permute-start.10 = (bf16[384,128]{1,0:T(8,128)(2,1)S(1)}, bf16[384,128]{1,0:T(8,128)(2,1)S(1)}, u32[]{:S(2)}, u32[]{:S(2)}) collective-permute-start(bf16[384,128]{1,0:T(8,128)(2,1)S(1)} %broadcast_select_fusion.2), channel_id=1, source_target_pairs={{0,2},{1,3},{2,0},{3,1},{4,6},{5,7},{6,4},{7,5},{8,10},{9,11},{10,... | collective-permute-start | bytes 294920 | tf_op jit(solution)/shard_map/ppermute | solution.py:405
  46.0 8.1 %collective-permute-start.8 = (bf16[384,128]{1,0:T(8,128)(2,1)S(1)}, bf16[384,128]{1,0:T(8,128)(2,1)S(1)}, u32[]{:S(2)}, u32[]{:S(2)}) collective-permute-start(bf16[384,128]{1,0:T(8,128)(2,1)S(1)} %broadcast_select_fusion.3), channel_id=1, source_target_pairs={{0,32},{1,33},{2,34},{3,35},{4,36},{5,37},{6,38},{7,39},{8,40},{9,... | collective-permute-start | bytes 294920 | tf_op jit(solution)/shard_map/ppermute | solution.py:405
  47.1 7.0 %collective-permute-start.6 = (bf16[32,512]{1,0:T(8,128)(2,1)S(1)}, bf16[32,512]{1,0:T(8,128)(2,1)S(1)}, u32[]{:S(2)}, u32[]{:S(2)}) collective-permute-start(bf16[32,512]{1,0:T(8,128)(2,1)S(1)} %copy-done.7), channel_id=1, source_target_pairs={{1,2},{3,4},{5,6},{7,8},{9,10},{11,12},{13,14},{15,16},{17,18},{19... | collective-permute-start | bytes 98312 | tf_op jit(solution)/shard_map/ppermute | solution.py:376
  54.1 18.6 %copy-start.4 = (bf16[32,512]{1,0:T(8,128)(2,1)}, bf16[32,512]{1,0:T(8,128)(2,1)S(1)}, u32[]{:S(2)}) copy-start(bf16[32,512]{1,0:T(8,128)(2,1)S(1)} %collective-permute-done.6.far_s_ref) | copy-start | bytes 98308
  54.2 12.1 %collective-permute-start.14 = (bf16[192,128]{1,0:T(8,128)(2,1)S(1)}, bf16[192,128]{1,0:T(8,128)(2,1)S(1)}, u32[]{:S(2)}, u32[]{:S(2)}) collective-permute-start(bf16[192,128]{1,0:T(8,128)(2,1)S(1)} %get-tuple-element.58), channel_id=1, source_target_pairs={{0,132},{1,133},{2,134},{3,135},{4,128},{5,129},{6,130},{7,131},{8... | collective-permute-start | bytes 147464 | tf_op jit(solution)/shard_map/ppermute | solution.py:405
  54.3 12.0 %collective-permute-start.13 = (bf16[192,128]{1,0:T(8,128)(2,1)S(1)}, bf16[192,128]{1,0:T(8,128)(2,1)S(1)}, u32[]{:S(2)}, u32[]{:S(2)}) collective-permute-start(bf16[192,128]{1,0:T(8,128)(2,1)S(1)} %get-tuple-element.59), channel_id=1, source_target_pairs={{0,4},{1,5},{2,6},{3,7},{4,0},{5,1},{6,2},{7,3},{8,12},{9,13},{10,... | collective-permute-start | bytes 147464 | tf_op jit(solution)/shard_map/ppermute | solution.py:405
  59.5 6.8 %collective-permute-start.12 = (bf16[192,128]{1,0:T(8,128)(2,1)S(1)}, bf16[192,128]{1,0:T(8,128)(2,1)S(1)}, u32[]{:S(2)}, u32[]{:S(2)}) collective-permute-start(bf16[192,128]{1,0:T(8,128)(2,1)S(1)} %get-tuple-element.60), channel_id=1, source_target_pairs={{0,128},{1,129},{2,130},{3,131},{4,132},{5,133},{6,134},{7,135},{8... | collective-permute-start | bytes 147464 | tf_op jit(solution)/shard_map/ppermute | solution.py:405
  59.5 6.8 %collective-permute-start.11 = (bf16[32,512]{1,0:T(8,128)(2,1)S(1)}, bf16[32,512]{1,0:T(8,128)(2,1)S(1)}, u32[]{:S(2)}, u32[]{:S(2)}) collective-permute-start(bf16[32,512]{1,0:T(8,128)(2,1)S(1)} %copy-done.6), channel_id=1, source_target_pairs={{32,64},{96,128},{160,192},{64,32},{128,96},{192,160},{33,65},{97,... | collective-permute-start | bytes 98312 | tf_op jit(solution)/shard_map/ppermute | solution.py:376
  66.4 8.1 %collective-permute-start.17 = (bf16[48,128]{1,0:T(8,128)(2,1)S(1)}, bf16[48,128]{1,0:T(8,128)(2,1)S(1)}, u32[]{:S(2)}, u32[]{:S(2)}) collective-permute-start(bf16[48,128]{1,0:T(8,128)(2,1)S(1)} %get-tuple-element.63), channel_id=1, source_target_pairs={{0,30},{1,31},{2,28},{3,29},{4,26},{5,27},{6,24},{7,25},{8,22},{9,... | collective-permute-start | bytes 36872 | tf_op jit(solution)/shard_map/ppermute | solution.py:405
  66.5 8.0 %collective-permute-start.16 = (bf16[48,128]{1,0:T(8,128)(2,1)S(1)}, bf16[48,128]{1,0:T(8,128)(2,1)S(1)}, u32[]{:S(2)}, u32[]{:S(2)}) collective-permute-start(bf16[48,128]{1,0:T(8,128)(2,1)S(1)} %get-tuple-element.64), channel_id=1, source_target_pairs={{0,16},{1,17},{2,18},{3,19},{4,20},{5,21},{6,22},{7,23},{8,24},{9,... | collective-permute-start | bytes 36872 | tf_op jit(solution)/shard_map/ppermute | solution.py:405
  67.6 6.9 %collective-permute-start.15 = (bf16[48,128]{1,0:T(8,128)(2,1)S(1)}, bf16[48,128]{1,0:T(8,128)(2,1)S(1)}, u32[]{:S(2)}, u32[]{:S(2)}) collective-permute-start(bf16[48,128]{1,0:T(8,128)(2,1)S(1)} %get-tuple-element.65), channel_id=1, source_target_pairs={{0,14},{1,15},{2,12},{3,13},{4,10},{5,11},{6,8},{7,9},{8,6},{9,7},... | collective-permute-start | bytes 36872 | tf_op jit(solution)/shard_map/ppermute | solution.py:405
  74.5 3.8 %collective-permute-start.18 = (bf16[48,128]{1,0:T(8,128)(2,1)S(1)}, bf16[48,128]{1,0:T(8,128)(2,1)S(1)}, u32[]{:S(2)}, u32[]{:S(2)}) collective-permute-start(bf16[48,128]{1,0:T(8,128)(2,1)S(1)} %add_convert_fusion.8), channel_id=1, source_target_pairs={{0,96},{1,97},{2,98},{3,99},{4,100},{5,101},{6,102},{7,103},{8,104... | collective-permute-start | bytes 36872 | tf_op jit(solution)/shard_map/ppermute | solution.py:405
  78.3 5.5 %collective-permute-start.21 = (bf16[48,128]{1,0:T(8,128)(2,1)S(1)}, bf16[48,128]{1,0:T(8,128)(2,1)S(1)}, u32[]{:S(2)}, u32[]{:S(2)}) collective-permute-start(bf16[48,128]{1,0:T(8,128)(2,1)S(1)} %add_convert_fusion.7), channel_id=1, source_target_pairs={{0,32},{1,33},{2,34},{3,35},{4,36},{5,37},{6,38},{7,39},{8,40},{9,... | collective-permute-start | bytes 36872 | tf_op jit(solution)/shard_map/ppermute | solution.py:405
  82.2 3.7 %collective-permute-start.20 = (bf16[48,128]{1,0:T(8,128)(2,1)S(1)}, bf16[48,128]{1,0:T(8,128)(2,1)S(1)}, u32[]{:S(2)}, u32[]{:S(2)}) collective-permute-start(bf16[48,128]{1,0:T(8,128)(2,1)S(1)} %add_convert_fusion.7), channel_id=1, source_target_pairs={{0,128},{1,129},{2,130},{3,131},{4,132},{5,133},{6,134},{7,135},{8... | collective-permute-start | bytes 36872 | tf_op jit(solution)/shard_map/ppermute | solution.py:405
  83.8 4.6 %collective-permute-start.19 = (bf16[48,128]{1,0:T(8,128)(2,1)S(1)}, bf16[48,128]{1,0:T(8,128)(2,1)S(1)}, u32[]{:S(2)}, u32[]{:S(2)}) collective-permute-start(bf16[48,128]{1,0:T(8,128)(2,1)S(1)} %add_convert_fusion.7), channel_id=1, source_target_pairs={{0,160},{1,161},{2,162},{3,163},{4,164},{5,165},{6,166},{7,167},{8... | collective-permute-start | bytes 36872 | tf_op jit(solution)/shard_map/ppermute | solution.py:405
  (10 other events, 45.2 us)

commit v6 on v5

--- a/solution.py
+++ b/solution.py
@@ -10,6 +10,7 @@
 EPSILON = 1e-05
 BF16 = jnp.bfloat16
 F32 = jnp.float32
+HBM = pl.BlockSpec(memory_space=pltpu.HBM)
 ANY = pl.BlockSpec(memory_space=pl.ANY)
 VM = pl.BlockSpec(memory_space=pltpu.VMEM)
 
@@ -96,13 +97,14 @@
         in_specs=[VM, VM],
         out_specs=[VM] * 4,
         scratch_shapes=[pltpu.VMEM((n, width), BF16)],
+        compiler_params=pltpu.CompilerParams(vmem_limit_bytes=8 << 20),
         name="pick",
         cost_estimate=pl.CostEstimate(flops=2 * n * n * width, bytes_accessed=2 * n * width * 2, transcendentals=0),
-    )(send_rows.reshape(1, n), mesh_lat)
+    )(*(pltpu.with_memory_space_constraint(x, pltpu.HBM) for x in (send_rows.reshape(1, n), mesh_lat)))
 
 
 TILE = 512
-VMEM_LIMIT = 58 << 20
+VMEM_LIMIT = 44 << 20
 
 
 def gray(value):
@@ -317,8 +319,8 @@
     return pl.pallas_call(
         main_kernel,
         out_shape=[jax.ShapeDtypeStruct(*shape) for shape in outs],
-        in_specs=[ANY] * len(operands),
-        out_specs=[ANY] * len(outs),
+        in_specs=[HBM] * 3 + [ANY] * 4 + [HBM] * (len(operands) - 7),
+        out_specs=[HBM] * 3 + [ANY] * (len(outs) - 3),
         scratch_shapes=local[:2]
         + [pltpu.VMEM((4 * margin, width), BF16)]
         + local[7:]
@@ -331,7 +333,7 @@
             bytes_accessed=12 * edges * width,
             transcendentals=edges * width,
         ),
-    )(*operands)
+    )(*[x if 3 <= i < 7 else pltpu.with_memory_space_constraint(x, pltpu.HBM) for i, x in enumerate(operands)])
 
 
 def mesh_kernel(send_ref, own_ref, near_s_ref, far_s_ref, near_b_ref, far_b_ref, out_ref, back):
@@ -364,6 +366,7 @@
         in_specs=[whole(send_row), whole(own)] + [tail(array) for array in returned],
         out_specs=whole(own),
         scratch_shapes=[pltpu.VMEM((n, width), BF16)],
+        compiler_params=pltpu.CompilerParams(vmem_limit_bytes=8 << 20),
         name="mesh_grads",
         cost_estimate=pl.CostEstimate(flops=2 * n * n * width, bytes_accessed=1 << 19, transcendentals=0),
     )(send_row, own, *returned)
@@ -451,10 +454,8 @@
     got_a, got_b = tails[1](got_a, got_b)
     both = jnp.stack([plus(a, got_a).reshape(2, -1, a.shape[1]), plus(b, got_b).reshape(2, -1, a.shape[1])])
     held, *got = quarter(both.reshape(-1, a.shape[1]), ("x_lo", 0), ("z", 1))
-    got = tails[2](*got)
     part = total(held, *got)
     held, *got = quarter(part, ("z", 2), ("x_hi", 0))
-    got = tails[3](*got)
     part = total(held, *got)
     part = plus(part, send(part, [("y", 1)]))
     by_y = send(part, [("y", 0)])
@@ -494,29 +495,16 @@
     done = {}
 
     def after_first(part, got_a, got_b, near_s, near_b):
-        far, _ = lax.optimization_barrier((far_s, part))
-        done["far_s"] = trade(far, "sector", 1)
-        done["near"] = near_s, near_b
-        done["first"] = got_a
-        return got_a, got_b
+        far, other, _ = lax.optimization_barrier((far_s, far_b, part))
+        far, other, *got = lax.optimization_barrier((trade(far, "sector", 1), trade(other, "band", 1), got_a, got_b))
+        done["back"] = near_s, far, near_b, other
+        return got
 
     def after_second(*got):
-        far, _ = lax.optimization_barrier((far_b, done["first"]))
-        done["far_b"] = trade(far, "band", 1)
-        done["far_s"], *got = lax.optimization_barrier((done["far_s"], *got))
+        done["mesh"], *got = lax.optimization_barrier((mesh_grads(send_rows, own_grad, done["back"]), *got))
         return got
 
-    def after_third(*got):
-        done["far_b"], *got = lax.optimization_barrier((done["far_b"], *got))
-        return got
-
-    def after_fourth(*got):
-        near_s, near_b = done["near"]
-        grads = mesh_grads(send_rows, own_grad, (near_s, done["far_s"], near_b, done["far_b"]))
-        done["mesh"], *got = lax.optimization_barrier((grads, *got))
-        return got
-
-    grad_w = reduce_weights(near_b, *sums, (after_first, after_second, after_third, after_fourth))
+    grad_w = reduce_weights(near_b, *sums, (after_first, after_second))
     total_edges = edge_feat.shape[0] * lax.axis_size("band") * lax.axis_size("sector")
     grad_w = grad_w * (1.0 / math.sqrt(total_edges))
     return (

time: 89.3 us -> 82.7 us (0.926)
  the two profiles are of different devices: /device:TPU:8 before, /device:TPU:32 now
where the time goes in v6:
time: 82.7 us; the launch traced here: 82.5 us
  starting transfers between devices  37.4 us (45%)
  waiting for transfers between devices  23.4 us (28%)
  Pallas kernels  19.4 us (23%)
  other arithmetic  1.32 us (2%)
  between operations  0.86 us (1%)
    ppermute x16, starting transfers between devices, send(): return lax.ppermute(values, ('band', 'sector'), sorted(pairs))  34.1 us
    pallas_call x1, Pallas kernels, main(): pl.pallas_call(main_kernel, out_shape=[jax.ShapeDtypeStruct(*shape) for s...  17.4 us
    ppermute x16, waiting for transfers between devices, send(): return lax.ppermute(values, ('band', 'sector'), sorted(pairs))  16.1 us
    ppermute x6, waiting for transfers between devices, trade(): return lax.ppermute(part, axis, ups + [(j, i) for i, j in ups])  7.37 us
    ppermute x6, starting transfers between devices, trade(): return lax.ppermute(part, axis, ups + [(j, i) for i, j in ups])  3.35 us
  transfers between devices with their start and end apart: 22, of which 16 were waited for; matrix products, arithmetic and copies ran while one was open for 0% of the time, Pallas kernels for 1%

profile of v6, /device:TPU:32, one launch (start us, length us, event | category | flops | bytes accessed | tf_op | source)
XLA Modules:
  0.0 82.5 jit_solution(8101096078513343760)
XLA Ops:
  0.6 1.2 %pick.1 = (bf16[32,512]{1,0:T(8,128)(2,1)S(1)}, bf16[32,512]{1,0:T(8,128)(2,1)S(1)}, bf16[32,512]{1,0:T(8,128)(2,1)S(1)}, bf16[32,512]{1,0:T(8,128)(2,1)S(1)}) custom-call(s32[1,128]{1,0:T(1,128)} %bitcast.9, bf16[128,512]{1,0:T(8,128)(2,1)} %refs_2_.1), custom_call_target="tpu_custom_call" | custom-call | flops 16777216 | bytes 262144 | tf_op jit(solution)/shard_map/pick/pallas_call | solution.py:94
  1.9 1.9 %collective-permute-start.1 = (bf16[32,512]{1,0:T(8,128)(2,1)S(1)}, bf16[32,512]{1,0:T(8,128)(2,1)S(1)}, u32[]{:S(2)}, u32[]{:S(2)}) collective-permute-start(bf16[32,512]{1,0:T(8,128)(2,1)S(1)} %get-tuple-element.28), channel_id=1, source_target_pairs={{1,2},{3,4},{5,6},{7,8},{9,10},{11,12},{13,14},{15,16},{17,18},{19... | collective-permute-start | bytes 98312 | tf_op jit(solution)/shard_map/ppermute | solution.py:379
  5.4 2.3 %collective-permute-done.2.refs_5_ = bf16[32,512]{1,0:T(8,128)(2,1)S(1)} collective-permute-done((bf16[32,512]{1,0:T(8,128)(2,1)S(1)}, bf16[32,512]{1,0:T(8,128)(2,1)S(1)}, u32[]{:S(2)}, u32[]{:S(2)}) %collective-permute-start.2) | collective-permute-done | bytes 32800 | tf_op jit(solution)/shard_map/ppermute | solution.py:379
  7.8 17.4 %main.1 = (bf16[512,512]{1,0:T(8,128)(2,1)}, bf16[512,512]{1,0:T(8,128)(2,1)}, f32[128,512]{1,0:T(8,128)S(1)}, bf16[32,512]{1,0:T(8,128)(2,1)S(1)}, bf16[128,128...) custom-call(s32[12,128]{1,0:T(8,128)} %bitcast.13, ...), custom_call_target="tpu_custom_call" | custom-call | flops 9663676416 | bytes 9437184 | tf_op jit(solution)/shard_map/main/pallas_call | solution.py:319
  25.8 1.2 %collective-permute-done.5 = bf16[768,256]{1,0:T(8,128)(2,1)S(1)} collective-permute-done((bf16[768,256]{1,0:T(8,128)(2,1)S(1)}, bf16[768,256]{1,0:T(8,128)(2,1)S(1)}, u32[]{:S(2)}, u32[]{:S(2)}) %collective-permute-start.5) | collective-permute-done | bytes 393248 | tf_op jit(solution)/shard_map/ppermute | solution.py:408
  27.1 4.0 %collective-permute-start.9 = (bf16[896,128]{1,0:T(8,128)(2,1)S(1)}, bf16[896,128]{1,0:T(8,128)(2,1)S(1)}, u32[]{:S(2)}, u32[]{:S(2)}) collective-permute-start(bf16[896,128]{1,0:T(8,128)(2,1)S(1)} %pad_maximum_fusion), channel_id=1, source_target_pairs={{0,32},{1,33},{2,34},{3,35},{4,36},{5,37},{6,38},{7,39},{8,40},{9,... | collective-permute-start | bytes 688136 | tf_op jit(solution)/shard_map/ppermute | solution.py:408
  31.3 7.0 %collective-permute-start.8 = (bf16[384,256]{1,0:T(8,128)(2,1)S(1)}, bf16[384,256]{1,0:T(8,128)(2,1)S(1)}, u32[]{:S(2)}, u32[]{:S(2)}) collective-permute-start(bf16[384,256]{1,0:T(8,128)(2,1)S(1)} %broadcast_select_fusion.1), channel_id=1, source_target_pairs={{0,2},{1,3},{2,0},{3,1},{4,6},{5,7},{6,4},{7,5},{8,10},{9,11},{10,... | collective-permute-start | bytes 589832 | tf_op jit(solution)/shard_map/ppermute | solution.py:408
  39.0 4.1 %collective-permute-done.6.far_s_ref = bf16[32,512]{1,0:T(8,128)(2,1)S(1)} collective-permute-done((bf16[32,512]{1,0:T(8,128)(2,1)S(1)}, bf16[32,512]{1,0:T(8,128)(2,1)S(1)}, u32[]{:S(2)}, u32[]{:S(2)}) %collective-permute-start.6) | collective-permute-done | bytes 32800 | tf_op jit(solution)/shard_map/ppermute | solution.py:379
  43.7 3.5 %collective-permute-start.10 = (bf16[384,128]{1,0:T(8,128)(2,1)S(1)}, bf16[384,128]{1,0:T(8,128)(2,1)S(1)}, u32[]{:S(2)}, u32[]{:S(2)}) collective-permute-start(bf16[384,128]{1,0:T(8,128)(2,1)S(1)} %broadcast_select_fusion.3), channel_id=1, source_target_pairs={{0,32},{1,33},{2,34},{3,35},{4,36},{5,37},{6,38},{7,39},{8,40},{9,... | collective-permute-start | bytes 294920 | tf_op jit(solution)/shard_map/ppermute | solution.py:408
  47.3 1.4 %collective-permute-start.11 = (bf16[384,128]{1,0:T(8,128)(2,1)S(1)}, bf16[384,128]{1,0:T(8,128)(2,1)S(1)}, u32[]{:S(2)}, u32[]{:S(2)}) collective-permute-start(bf16[384,128]{1,0:T(8,128)(2,1)S(1)} %broadcast_select_fusion.2), channel_id=1, source_target_pairs={{0,2},{1,3},{2,0},{3,1},{4,6},{5,7},{6,4},{7,5},{8,10},{9,11},{10,... | collective-permute-start | bytes 294920 | tf_op jit(solution)/shard_map/ppermute | solution.py:408
  49.8 2.2 %collective-permute-done.11 = bf16[384,128]{1,0:T(8,128)(2,1)S(1)} collective-permute-done((bf16[384,128]{1,0:T(8,128)(2,1)S(1)}, bf16[384,128]{1,0:T(8,128)(2,1)S(1)}, u32[]{:S(2)}, u32[]{:S(2)}) %collective-permute-start.11) | collective-permute-done | bytes 98336 | tf_op jit(solution)/shard_map/ppermute | solution.py:408
  52.1 1.9 %collective-permute-start.14 = (bf16[192,128]{1,0:T(8,128)(2,1)S(1)}, bf16[192,128]{1,0:T(8,128)(2,1)S(1)}, u32[]{:S(2)}, u32[]{:S(2)}) collective-permute-start(bf16[192,128]{1,0:T(8,128)(2,1)S(1)} %get-tuple-element.52), channel_id=1, source_target_pairs={{0,132},{1,133},{2,134},{3,135},{4,128},{5,129},{6,130},{7,131},{8... | collective-permute-start | bytes 147464 | tf_op jit(solution)/shard_map/ppermute | solution.py:408
  54.1 2.0 %collective-permute-start.13 = (bf16[192,128]{1,0:T(8,128)(2,1)S(1)}, bf16[192,128]{1,0:T(8,128)(2,1)S(1)}, u32[]{:S(2)}, u32[]{:S(2)}) collective-permute-start(bf16[192,128]{1,0:T(8,128)(2,1)S(1)} %get-tuple-element.51), channel_id=1, source_target_pairs={{0,4},{1,5},{2,6},{3,7},{4,0},{5,1},{6,2},{7,3},{8,12},{9,13},{10,... | collective-permute-start | bytes 147464 | tf_op jit(solution)/shard_map/ppermute | solution.py:408
  56.6 1.6 %collective-permute-done.14 = bf16[192,128]{1,0:T(8,128)(2,1)S(1)} collective-permute-done((bf16[192,128]{1,0:T(8,128)(2,1)S(1)}, bf16[192,128]{1,0:T(8,128)(2,1)S(1)}, u32[]{:S(2)}, u32[]{:S(2)}) %collective-permute-start.14) | collective-permute-done | bytes 49184 | tf_op jit(solution)/shard_map/ppermute | solution.py:408
  59.0 1.1 %collective-permute-done.12 = bf16[192,128]{1,0:T(8,128)(2,1)S(1)} collective-permute-done((bf16[192,128]{1,0:T(8,128)(2,1)S(1)}, bf16[192,128]{1,0:T(8,128)(2,1)S(1)}, u32[]{:S(2)}, u32[]{:S(2)}) %collective-permute-start.12) | collective-permute-done | bytes 49184 | tf_op jit(solution)/shard_map/ppermute | solution.py:408
  60.2 3.1 %collective-permute-start.17 = (bf16[48,128]{1,0:T(8,128)(2,1)S(1)}, bf16[48,128]{1,0:T(8,128)(2,1)S(1)}, u32[]{:S(2)}, u32[]{:S(2)}) collective-permute-start(bf16[48,128]{1,0:T(8,128)(2,1)S(1)} %get-tuple-element.57), channel_id=1, source_target_pairs={{0,30},{1,31},{2,28},{3,29},{4,26},{5,27},{6,24},{7,25},{8,22},{9,... | collective-permute-start | bytes 36872 | tf_op jit(solution)/shard_map/ppermute | solution.py:408
  64.1 4.2 %collective-permute-start.15 = (bf16[48,128]{1,0:T(8,128)(2,1)S(1)}, bf16[48,128]{1,0:T(8,128)(2,1)S(1)}, u32[]{:S(2)}, u32[]{:S(2)}) collective-permute-start(bf16[48,128]{1,0:T(8,128)(2,1)S(1)} %get-tuple-element.55), channel_id=1, source_target_pairs={{0,14},{1,15},{2,12},{3,13},{4,10},{5,11},{6,8},{7,9},{8,6},{9,7},... | collective-permute-start | bytes 36872 | tf_op jit(solution)/shard_map/ppermute | solution.py:408
  68.3 1.1 %collective-permute-done.17 = bf16[48,128]{1,0:T(8,128)(2,1)S(1)} collective-permute-done((bf16[48,128]{1,0:T(8,128)(2,1)S(1)}, bf16[48,128]{1,0:T(8,128)(2,1)S(1)}, u32[]{:S(2)}, u32[]{:S(2)}) %collective-permute-start.17) | collective-permute-done | bytes 12320 | tf_op jit(solution)/shard_map/ppermute | solution.py:408
  69.4 1.4 %collective-permute-done.15 = bf16[48,128]{1,0:T(8,128)(2,1)S(1)} collective-permute-done((bf16[48,128]{1,0:T(8,128)(2,1)S(1)}, bf16[48,128]{1,0:T(8,128)(2,1)S(1)}, u32[]{:S(2)}, u32[]{:S(2)}) %collective-permute-start.15) | collective-permute-done | bytes 12320 | tf_op jit(solution)/shard_map/ppermute | solution.py:408
  70.8 1.5 %collective-permute-start.18 = (bf16[48,128]{1,0:T(8,128)(2,1)S(1)}, bf16[48,128]{1,0:T(8,128)(2,1)S(1)}, u32[]{:S(2)}, u32[]{:S(2)}) collective-permute-start(bf16[48,128]{1,0:T(8,128)(2,1)S(1)} %add_convert_fusion.8), channel_id=1, source_target_pairs={{0,96},{1,97},{2,98},{3,99},{4,100},{5,101},{6,102},{7,103},{8,104... | collective-permute-start | bytes 36872 | tf_op jit(solution)/shard_map/ppermute | solution.py:408
  72.3 3.5 %collective-permute-done.18 = bf16[48,128]{1,0:T(8,128)(2,1)S(1)} collective-permute-done((bf16[48,128]{1,0:T(8,128)(2,1)S(1)}, bf16[48,128]{1,0:T(8,128)(2,1)S(1)}, u32[]{:S(2)}, u32[]{:S(2)}) %collective-permute-start.18) | collective-permute-done | bytes 12320 | tf_op jit(solution)/shard_map/ppermute | solution.py:408
  75.8 1.2 %collective-permute-start.21 = (bf16[48,128]{1,0:T(8,128)(2,1)S(1)}, bf16[48,128]{1,0:T(8,128)(2,1)S(1)}, u32[]{:S(2)}, u32[]{:S(2)}) collective-permute-start(bf16[48,128]{1,0:T(8,128)(2,1)S(1)} %add_convert_fusion.7), channel_id=1, source_target_pairs={{0,32},{1,33},{2,34},{3,35},{4,36},{5,37},{6,38},{7,39},{8,40},{9,... | collective-permute-start | bytes 36872 | tf_op jit(solution)/shard_map/ppermute | solution.py:408
  78.1 1.3 %collective-permute-start.20 = (bf16[48,128]{1,0:T(8,128)(2,1)S(1)}, bf16[48,128]{1,0:T(8,128)(2,1)S(1)}, u32[]{:S(2)}, u32[]{:S(2)}) collective-permute-start(bf16[48,128]{1,0:T(8,128)(2,1)S(1)} %add_convert_fusion.7), channel_id=1, source_target_pairs={{0,128},{1,129},{2,130},{3,131},{4,132},{5,133},{6,134},{7,135},{8... | collective-permute-start | bytes 36872 | tf_op jit(solution)/shard_map/ppermute | solution.py:408
  79.6 2.0 %collective-permute-done.19 = bf16[48,128]{1,0:T(8,128)(2,1)S(1)} collective-permute-done((bf16[48,128]{1,0:T(8,128)(2,1)S(1)}, bf16[48,128]{1,0:T(8,128)(2,1)S(1)}, u32[]{:S(2)}, u32[]{:S(2)}) %collective-permute-start.19) | collective-permute-done | bytes 12320 | tf_op jit(solution)/shard_map/ppermute | solution.py:408
  (45 shorter events, 9.4 us)
Async XLA Ops:
  1.8 2.7 %collective-permute-start = (bf16[32,512]{1,0:T(8,128)(2,1)S(1)}, bf16[32,512]{1,0:T(8,128)(2,1)S(1)}, u32[]{:S(2)}, u32[]{:S(2)}) collective-permute-start(bf16[32,512]{1,0:T(8,128)(2,1)S(1)} %get-tuple-element.27), channel_id=1, source_target_pairs={{0,1},{2,3},{4,5},{6,7},{8,9},{10,11},{12,13},{14,15},{16,17},{18,... | collective-permute-start | bytes 98312 | tf_op jit(solution)/shard_map/ppermute | solution.py:379
  1.9 3.5 %collective-permute-start.1 = (bf16[32,512]{1,0:T(8,128)(2,1)S(1)}, bf16[32,512]{1,0:T(8,128)(2,1)S(1)}, u32[]{:S(2)}, u32[]{:S(2)}) collective-permute-start(bf16[32,512]{1,0:T(8,128)(2,1)S(1)} %get-tuple-element.28), channel_id=1, source_target_pairs={{1,2},{3,4},{5,6},{7,8},{9,10},{11,12},{13,14},{15,16},{17,18},{19... | collective-permute-start | bytes 98312 | tf_op jit(solution)/shard_map/ppermute | solution.py:379
  3.8 3.9 %collective-permute-start.2 = (bf16[32,512]{1,0:T(8,128)(2,1)S(1)}, bf16[32,512]{1,0:T(8,128)(2,1)S(1)}, u32[]{:S(2)}, u32[]{:S(2)}) collective-permute-start(bf16[32,512]{1,0:T(8,128)(2,1)S(1)} %get-tuple-element.29), channel_id=1, source_target_pairs={{0,32},{64,96},{128,160},{192,224},{32,0},{96,64},{160,128},{224,1... | collective-permute-start | bytes 98312 | tf_op jit(solution)/shard_map/ppermute | solution.py:379
  3.8 3.9 %collective-permute-start.3 = (bf16[32,512]{1,0:T(8,128)(2,1)S(1)}, bf16[32,512]{1,0:T(8,128)(2,1)S(1)}, u32[]{:S(2)}, u32[]{:S(2)}) collective-permute-start(bf16[32,512]{1,0:T(8,128)(2,1)S(1)} %get-tuple-element.30), channel_id=1, source_target_pairs={{32,64},{96,128},{160,192},{64,32},{128,96},{192,160},{33,65},{97,... | collective-permute-start | bytes 98312 | tf_op jit(solution)/shard_map/ppermute | solution.py:379
  25.2 1.8 %collective-permute-start.5 = (bf16[768,256]{1,0:T(8,128)(2,1)S(1)}, bf16[768,256]{1,0:T(8,128)(2,1)S(1)}, u32[]{:S(2)}, u32[]{:S(2)}) collective-permute-start(bf16[768,256]{1,0:T(8,128)(2,1)S(1)} %get-tuple-element.38), channel_id=1, source_target_pairs={{0,1},{1,0},{2,3},{3,2},{4,5},{5,4},{6,7},{7,6},{8,9},{9,8},{10,11... | collective-permute-start | bytes 1179656 | tf_op jit(solution)/shard_map/ppermute | solution.py:408
  25.3 5.8 %collective-permute-start.4 = (bf16[832,256]{1,0:T(8,128)(2,1)S(1)}, bf16[832,256]{1,0:T(8,128)(2,1)S(1)}, u32[]{:S(2)}, u32[]{:S(2)}) collective-permute-start(bf16[832,256]{1,0:T(8,128)(2,1)S(1)} %get-tuple-element.34), channel_id=1, source_target_pairs={{0,1},{1,0},{2,3},{3,2},{4,5},{5,4},{6,7},{7,6},{8,9},{9,8},{10,11... | collective-permute-start | bytes 1277960 | tf_op jit(solution)/shard_map/ppermute | solution.py:408
  27.1 11.9 %collective-permute-start.9 = (bf16[896,128]{1,0:T(8,128)(2,1)S(1)}, bf16[896,128]{1,0:T(8,128)(2,1)S(1)}, u32[]{:S(2)}, u32[]{:S(2)}) collective-permute-start(bf16[896,128]{1,0:T(8,128)(2,1)S(1)} %pad_maximum_fusion), channel_id=1, source_target_pairs={{0,32},{1,33},{2,34},{3,35},{4,36},{5,37},{6,38},{7,39},{8,40},{9,... | collective-permute-start | bytes 688136 | tf_op jit(solution)/shard_map/ppermute | solution.py:408
  31.2 17.4 %copy-start = (s32[128]{0:T(128)S(1)}, s32[128]{0:T(128)}, u32[]{:S(2)}) copy-start(s32[128]{0:T(128)} %param.18) | copy-start | bytes 1540
  31.3 12.3 %collective-permute-start.8 = (bf16[384,256]{1,0:T(8,128)(2,1)S(1)}, bf16[384,256]{1,0:T(8,128)(2,1)S(1)}, u32[]{:S(2)}, u32[]{:S(2)}) collective-permute-start(bf16[384,256]{1,0:T(8,128)(2,1)S(1)} %broadcast_select_fusion.1), channel_id=1, source_target_pairs={{0,2},{1,3},{2,0},{3,1},{4,6},{5,7},{6,4},{7,5},{8,10},{9,11},{10,... | collective-permute-start | bytes 589832 | tf_op jit(solution)/shard_map/ppermute | solution.py:408
  38.3 4.8 %collective-permute-start.6 = (bf16[32,512]{1,0:T(8,128)(2,1)S(1)}, bf16[32,512]{1,0:T(8,128)(2,1)S(1)}, u32[]{:S(2)}, u32[]{:S(2)}) collective-permute-start(bf16[32,512]{1,0:T(8,128)(2,1)S(1)} %get-tuple-element.39), channel_id=1, source_target_pairs={{1,2},{3,4},{5,6},{7,8},{9,10},{11,12},{13,14},{15,16},{17,18},{19... | collective-permute-start | bytes 98312 | tf_op jit(solution)/shard_map/ppermute | solution.py:379
  38.3 4.8 %collective-permute-start.7 = (bf16[32,512]{1,0:T(8,128)(2,1)S(1)}, bf16[32,512]{1,0:T(8,128)(2,1)S(1)}, u32[]{:S(2)}, u32[]{:S(2)}) collective-permute-start(bf16[32,512]{1,0:T(8,128)(2,1)S(1)} %get-tuple-element.40), channel_id=1, source_target_pairs={{32,64},{96,128},{160,192},{64,32},{128,96},{192,160},{33,65},{97,... | collective-permute-start | bytes 98312 | tf_op jit(solution)/shard_map/ppermute | solution.py:379
  43.7 6.1 %collective-permute-start.10 = (bf16[384,128]{1,0:T(8,128)(2,1)S(1)}, bf16[384,128]{1,0:T(8,128)(2,1)S(1)}, u32[]{:S(2)}, u32[]{:S(2)}) collective-permute-start(bf16[384,128]{1,0:T(8,128)(2,1)S(1)} %broadcast_select_fusion.3), channel_id=1, source_target_pairs={{0,32},{1,33},{2,34},{3,35},{4,36},{5,37},{6,38},{7,39},{8,40},{9,... | collective-permute-start | bytes 294920 | tf_op jit(solution)/shard_map/ppermute | solution.py:408
  47.3 4.7 %collective-permute-start.11 = (bf16[384,128]{1,0:T(8,128)(2,1)S(1)}, bf16[384,128]{1,0:T(8,128)(2,1)S(1)}, u32[]{:S(2)}, u32[]{:S(2)}) collective-permute-start(bf16[384,128]{1,0:T(8,128)(2,1)S(1)} %broadcast_select_fusion.2), channel_id=1, source_target_pairs={{0,2},{1,3},{2,0},{3,1},{4,6},{5,7},{6,4},{7,5},{8,10},{9,11},{10,... | collective-permute-start | bytes 294920 | tf_op jit(solution)/shard_map/ppermute | solution.py:408
  52.1 6.1 %collective-permute-start.14 = (bf16[192,128]{1,0:T(8,128)(2,1)S(1)}, bf16[192,128]{1,0:T(8,128)(2,1)S(1)}, u32[]{:S(2)}, u32[]{:S(2)}) collective-permute-start(bf16[192,128]{1,0:T(8,128)(2,1)S(1)} %get-tuple-element.52), channel_id=1, source_target_pairs={{0,132},{1,133},{2,134},{3,135},{4,128},{5,129},{6,130},{7,131},{8... | collective-permute-start | bytes 147464 | tf_op jit(solution)/shard_map/ppermute | solution.py:408
  54.1 5.0 %collective-permute-start.13 = (bf16[192,128]{1,0:T(8,128)(2,1)S(1)}, bf16[192,128]{1,0:T(8,128)(2,1)S(1)}, u32[]{:S(2)}, u32[]{:S(2)}) collective-permute-start(bf16[192,128]{1,0:T(8,128)(2,1)S(1)} %get-tuple-element.51), channel_id=1, source_target_pairs={{0,4},{1,5},{2,6},{3,7},{4,0},{5,1},{6,2},{7,3},{8,12},{9,13},{10,... | collective-permute-start | bytes 147464 | tf_op jit(solution)/shard_map/ppermute | solution.py:408
  56.1 4.1 %collective-permute-start.12 = (bf16[192,128]{1,0:T(8,128)(2,1)S(1)}, bf16[192,128]{1,0:T(8,128)(2,1)S(1)}, u32[]{:S(2)}, u32[]{:S(2)}) collective-permute-start(bf16[192,128]{1,0:T(8,128)(2,1)S(1)} %get-tuple-element.50), channel_id=1, source_target_pairs={{0,128},{1,129},{2,130},{3,131},{4,132},{5,133},{6,134},{7,135},{8... | collective-permute-start | bytes 147464 | tf_op jit(solution)/shard_map/ppermute | solution.py:408
  60.2 9.2 %collective-permute-start.17 = (bf16[48,128]{1,0:T(8,128)(2,1)S(1)}, bf16[48,128]{1,0:T(8,128)(2,1)S(1)}, u32[]{:S(2)}, u32[]{:S(2)}) collective-permute-start(bf16[48,128]{1,0:T(8,128)(2,1)S(1)} %get-tuple-element.57), channel_id=1, source_target_pairs={{0,30},{1,31},{2,28},{3,29},{4,26},{5,27},{6,24},{7,25},{8,22},{9,... | collective-permute-start | bytes 36872 | tf_op jit(solution)/shard_map/ppermute | solution.py:408
  63.3 6.1 %collective-permute-start.16 = (bf16[48,128]{1,0:T(8,128)(2,1)S(1)}, bf16[48,128]{1,0:T(8,128)(2,1)S(1)}, u32[]{:S(2)}, u32[]{:S(2)}) collective-permute-start(bf16[48,128]{1,0:T(8,128)(2,1)S(1)} %get-tuple-element.56), channel_id=1, source_target_pairs={{0,16},{1,17},{2,18},{3,19},{4,20},{5,21},{6,22},{7,23},{8,24},{9,... | collective-permute-start | bytes 36872 | tf_op jit(solution)/shard_map/ppermute | solution.py:408
  64.1 6.7 %collective-permute-start.15 = (bf16[48,128]{1,0:T(8,128)(2,1)S(1)}, bf16[48,128]{1,0:T(8,128)(2,1)S(1)}, u32[]{:S(2)}, u32[]{:S(2)}) collective-permute-start(bf16[48,128]{1,0:T(8,128)(2,1)S(1)} %get-tuple-element.55), channel_id=1, source_target_pairs={{0,14},{1,15},{2,12},{3,13},{4,10},{5,11},{6,8},{7,9},{8,6},{9,7},... | collective-permute-start | bytes 36872 | tf_op jit(solution)/shard_map/ppermute | solution.py:408
  70.8 5.0 %collective-permute-start.18 = (bf16[48,128]{1,0:T(8,128)(2,1)S(1)}, bf16[48,128]{1,0:T(8,128)(2,1)S(1)}, u32[]{:S(2)}, u32[]{:S(2)}) collective-permute-start(bf16[48,128]{1,0:T(8,128)(2,1)S(1)} %add_convert_fusion.8), channel_id=1, source_target_pairs={{0,96},{1,97},{2,98},{3,99},{4,100},{5,101},{6,102},{7,103},{8,104... | collective-permute-start | bytes 36872 | tf_op jit(solution)/shard_map/ppermute | solution.py:408
  75.8 3.8 %collective-permute-start.21 = (bf16[48,128]{1,0:T(8,128)(2,1)S(1)}, bf16[48,128]{1,0:T(8,128)(2,1)S(1)}, u32[]{:S(2)}, u32[]{:S(2)}) collective-permute-start(bf16[48,128]{1,0:T(8,128)(2,1)S(1)} %add_convert_fusion.7), channel_id=1, source_target_pairs={{0,32},{1,33},{2,34},{3,35},{4,36},{5,37},{6,38},{7,39},{8,40},{9,... | collective-permute-start | bytes 36872 | tf_op jit(solution)/shard_map/ppermute | solution.py:408
  77.0 4.6 %collective-permute-start.19 = (bf16[48,128]{1,0:T(8,128)(2,1)S(1)}, bf16[48,128]{1,0:T(8,128)(2,1)S(1)}, u32[]{:S(2)}, u32[]{:S(2)}) collective-permute-start(bf16[48,128]{1,0:T(8,128)(2,1)S(1)} %add_convert_fusion.7), channel_id=1, source_target_pairs={{0,160},{1,161},{2,162},{3,163},{4,164},{5,165},{6,166},{7,167},{8... | collective-permute-start | bytes 36872 | tf_op jit(solution)/shard_map/ppermute | solution.py:408
  78.1 3.7 %collective-permute-start.20 = (bf16[48,128]{1,0:T(8,128)(2,1)S(1)}, bf16[48,128]{1,0:T(8,128)(2,1)S(1)}, u32[]{:S(2)}, u32[]{:S(2)}) collective-permute-start(bf16[48,128]{1,0:T(8,128)(2,1)S(1)} %add_convert_fusion.7), channel_id=1, source_target_pairs={{0,128},{1,129},{2,130},{3,131},{4,132},{5,133},{6,134},{7,135},{8... | collective-permute-start | bytes 36872 | tf_op jit(solution)/shard_map/ppermute | solution.py:408

commit v7 on v6

--- a/solution.py
+++ b/solution.py
@@ -223,7 +223,6 @@
         d_hidden = mm_nt(d_raw.astype(BF16), n2[...]).astype(BF16).astype(F32)
         d_pre[rows, :] = (d_hidden * node_slope).astype(BF16)
         d_agg.append(mm_nt(d_pre[rows, :], n1_agg[...]).astype(BF16))
-    stores[0].start()
     d_agg = jnp.concatenate(d_agg, axis=0)
     for rows in tiles:
         d_msg = mm(hot_d[rows, :], d_agg)
@@ -232,10 +231,8 @@
         gp[rows, :] = (d_hid * slope[rows, :]).astype(BF16)
     sm = mm(hot_st[...], gp[...]).astype(BF16)
     sg = mm(hot_dt[...], gp[...]).astype(BF16)
-    gw[width : 2 * width, :] = mm_tn(table[...], sm).astype(BF16)
     grad_table = mm_nt(sm, w_mesh[...])
-    gw[2 * width : 3 * width, :] = mm_tn(grid[...], sg).astype(BF16)
-    gw[0:width, :] = mm_tn(edge[...], gp[...]).astype(BF16)
+    gg[...] = (cot[...].astype(F32) + mm_nt(d_pre[...], n1_grid[...]) + mm_nt(sg, w_grid[...])).astype(BF16)
     core = parity("sector")
     half, quarter = width // 2, width // 4
     own_grad[...] = grad_table[0:own]
@@ -248,6 +245,12 @@
         near_b[i * margin : (i + 1) * margin, :] = near_b_rows[:, i * quarter : (i + 1) * quarter]
     far_s[...] = far_s_rows
     far_b[...] = far_b_rows
+    early = [stores[0], *stores[5:]]
+    for store in early:
+        store.start()
+    gw[width : 2 * width, :] = mm_tn(table[...], sm).astype(BF16)
+    gw[2 * width : 3 * width, :] = mm_tn(grid[...], sg).astype(BF16)
+    gw[0:width, :] = mm_tn(edge[...], gp[...]).astype(BF16)
     piece = gw.shape[0] // (2 * len(piece_order()))
     for i, j in enumerate(piece_order()):
         rows = slice(i * piece, (i + 1) * piece)
@@ -257,10 +260,8 @@
         send_b[rows, :] = gw[other, half:width]
         keep_a[rows, :] = gw[mine, 0:half]
         keep_b[rows, :] = gw[mine, half:width]
-    for store in stores[1:9]:
+    for store in stores[1:5]:
         store.start()
-    gg[...] = (cot[...].astype(F32) + mm_nt(d_pre[...], n1_grid[...]) + mm_nt(sg, w_grid[...])).astype(BF16)
-    stores[9].start()
     for store in stores:
         store.wait()
 

time: 82.7 us -> 81.8 us (0.989)
  Pallas kernels: 19.4 us -> 18.4 us
    pallas_call x1, Pallas kernels: 17.4 us -> 16.4 us  [main(): pl.pallas_call(main_kernel, out_shape=[jax.ShapeDtypeStruct(*shape) for s...]
where the time goes in v7:
time: 81.8 us; the launch traced here: 81.6 us
  starting transfers between devices  37.6 us (46%)
  waiting for transfers between devices  23.4 us (29%)
  Pallas kernels  18.4 us (22%)
  other arithmetic  1.32 us (2%)
  between operations  0.86 us (1%)
    ppermute x16, starting transfers between devices, send(): return lax.ppermute(values, ('band', 'sector'), sorted(pairs))  34.3 us
    pallas_call x1, Pallas kernels, main(): pl.pallas_call(main_kernel, out_shape=[jax.ShapeDtypeStruct(*shape) for s...  16.4 us
    ppermute x16, waiting for transfers between devices, send(): return lax.ppermute(values, ('band', 'sector'), sorted(pairs))  16 us
    ppermute x6, waiting for transfers between devices, trade(): return lax.ppermute(part, axis, ups + [(j, i) for i, j in ups])  7.37 us
    ppermute x6, starting transfers between devices, trade(): return lax.ppermute(part, axis, ups + [(j, i) for i, j in ups])  3.35 us
  transfers between devices with their start and end apart: 22, of which 16 were waited for; matrix products, arithmetic and copies ran while one was open for 0% of the time, Pallas kernels for 1%

profile of v7, /device:TPU:32, one launch (start us, length us, event | category | flops | bytes accessed | tf_op | source)
XLA Modules:
  0.0 81.6 jit_solution(13322767290541732612)
XLA Ops:
  0.6 1.2 %pick.1 = (bf16[32,512]{1,0:T(8,128)(2,1)S(1)}, bf16[32,512]{1,0:T(8,128)(2,1)S(1)}, bf16[32,512]{1,0:T(8,128)(2,1)S(1)}, bf16[32,512]{1,0:T(8,128)(2,1)S(1)}) custom-call(s32[1,128]{1,0:T(1,128)} %bitcast.9, bf16[128,512]{1,0:T(8,128)(2,1)} %refs_2_.1), custom_call_target="tpu_custom_call" | custom-call | flops 16777216 | bytes 262144 | tf_op jit(solution)/shard_map/pick/pallas_call | solution.py:94
  1.9 1.9 %collective-permute-start.1 = (bf16[32,512]{1,0:T(8,128)(2,1)S(1)}, bf16[32,512]{1,0:T(8,128)(2,1)S(1)}, u32[]{:S(2)}, u32[]{:S(2)}) collective-permute-start(bf16[32,512]{1,0:T(8,128)(2,1)S(1)} %get-tuple-element.28), channel_id=1, source_target_pairs={{1,2},{3,4},{5,6},{7,8},{9,10},{11,12},{13,14},{15,16},{17,18},{19... | collective-permute-start | bytes 98312 | tf_op jit(solution)/shard_map/ppermute | solution.py:380
  5.4 2.3 %collective-permute-done.2.refs_5_ = bf16[32,512]{1,0:T(8,128)(2,1)S(1)} collective-permute-done((bf16[32,512]{1,0:T(8,128)(2,1)S(1)}, bf16[32,512]{1,0:T(8,128)(2,1)S(1)}, u32[]{:S(2)}, u32[]{:S(2)}) %collective-permute-start.2) | collective-permute-done | bytes 32800 | tf_op jit(solution)/shard_map/ppermute | solution.py:380
  7.8 16.4 %main.1 = (bf16[512,512]{1,0:T(8,128)(2,1)}, bf16[512,512]{1,0:T(8,128)(2,1)}, f32[128,512]{1,0:T(8,128)S(1)}, bf16[32,512]{1,0:T(8,128)(2,1)S(1)}, bf16[128,128...) custom-call(s32[12,128]{1,0:T(8,128)} %bitcast.13, ...), custom_call_target="tpu_custom_call" | custom-call | flops 9663676416 | bytes 9437184 | tf_op jit(solution)/shard_map/main/pallas_call | solution.py:320
  24.9 1.2 %collective-permute-done.5 = bf16[768,256]{1,0:T(8,128)(2,1)S(1)} collective-permute-done((bf16[768,256]{1,0:T(8,128)(2,1)S(1)}, bf16[768,256]{1,0:T(8,128)(2,1)S(1)}, u32[]{:S(2)}, u32[]{:S(2)}) %collective-permute-start.5) | collective-permute-done | bytes 393248 | tf_op jit(solution)/shard_map/ppermute | solution.py:409
  26.3 4.0 %collective-permute-start.9 = (bf16[896,128]{1,0:T(8,128)(2,1)S(1)}, bf16[896,128]{1,0:T(8,128)(2,1)S(1)}, u32[]{:S(2)}, u32[]{:S(2)}) collective-permute-start(bf16[896,128]{1,0:T(8,128)(2,1)S(1)} %pad_maximum_fusion), channel_id=1, source_target_pairs={{0,32},{1,33},{2,34},{3,35},{4,36},{5,37},{6,38},{7,39},{8,40},{9,... | collective-permute-start | bytes 688136 | tf_op jit(solution)/shard_map/ppermute | solution.py:409
  30.4 7.1 %collective-permute-start.8 = (bf16[384,256]{1,0:T(8,128)(2,1)S(1)}, bf16[384,256]{1,0:T(8,128)(2,1)S(1)}, u32[]{:S(2)}, u32[]{:S(2)}) collective-permute-start(bf16[384,256]{1,0:T(8,128)(2,1)S(1)} %broadcast_select_fusion.1), channel_id=1, source_target_pairs={{0,2},{1,3},{2,0},{3,1},{4,6},{5,7},{6,4},{7,5},{8,10},{9,11},{10,... | collective-permute-start | bytes 589832 | tf_op jit(solution)/shard_map/ppermute | solution.py:409
  38.2 4.1 %collective-permute-done.6.far_s_ref = bf16[32,512]{1,0:T(8,128)(2,1)S(1)} collective-permute-done((bf16[32,512]{1,0:T(8,128)(2,1)S(1)}, bf16[32,512]{1,0:T(8,128)(2,1)S(1)}, u32[]{:S(2)}, u32[]{:S(2)}) %collective-permute-start.6) | collective-permute-done | bytes 32800 | tf_op jit(solution)/shard_map/ppermute | solution.py:380
  42.9 3.5 %collective-permute-start.10 = (bf16[384,128]{1,0:T(8,128)(2,1)S(1)}, bf16[384,128]{1,0:T(8,128)(2,1)S(1)}, u32[]{:S(2)}, u32[]{:S(2)}) collective-permute-start(bf16[384,128]{1,0:T(8,128)(2,1)S(1)} %broadcast_select_fusion.3), channel_id=1, source_target_pairs={{0,32},{1,33},{2,34},{3,35},{4,36},{5,37},{6,38},{7,39},{8,40},{9,... | collective-permute-start | bytes 294920 | tf_op jit(solution)/shard_map/ppermute | solution.py:409
  46.4 1.4 %collective-permute-start.11 = (bf16[384,128]{1,0:T(8,128)(2,1)S(1)}, bf16[384,128]{1,0:T(8,128)(2,1)S(1)}, u32[]{:S(2)}, u32[]{:S(2)}) collective-permute-start(bf16[384,128]{1,0:T(8,128)(2,1)S(1)} %broadcast_select_fusion.2), channel_id=1, source_target_pairs={{0,2},{1,3},{2,0},{3,1},{4,6},{5,7},{6,4},{7,5},{8,10},{9,11},{10,... | collective-permute-start | bytes 294920 | tf_op jit(solution)/shard_map/ppermute | solution.py:409
  48.9 2.2 %collective-permute-done.11 = bf16[384,128]{1,0:T(8,128)(2,1)S(1)} collective-permute-done((bf16[384,128]{1,0:T(8,128)(2,1)S(1)}, bf16[384,128]{1,0:T(8,128)(2,1)S(1)}, u32[]{:S(2)}, u32[]{:S(2)}) %collective-permute-start.11) | collective-permute-done | bytes 98336 | tf_op jit(solution)/shard_map/ppermute | solution.py:409
  51.3 1.9 %collective-permute-start.14 = (bf16[192,128]{1,0:T(8,128)(2,1)S(1)}, bf16[192,128]{1,0:T(8,128)(2,1)S(1)}, u32[]{:S(2)}, u32[]{:S(2)}) collective-permute-start(bf16[192,128]{1,0:T(8,128)(2,1)S(1)} %get-tuple-element.52), channel_id=1, source_target_pairs={{0,132},{1,133},{2,134},{3,135},{4,128},{5,129},{6,130},{7,131},{8... | collective-permute-start | bytes 147464 | tf_op jit(solution)/shard_map/ppermute | solution.py:409
  53.2 2.0 %collective-permute-start.13 = (bf16[192,128]{1,0:T(8,128)(2,1)S(1)}, bf16[192,128]{1,0:T(8,128)(2,1)S(1)}, u32[]{:S(2)}, u32[]{:S(2)}) collective-permute-start(bf16[192,128]{1,0:T(8,128)(2,1)S(1)} %get-tuple-element.51), channel_id=1, source_target_pairs={{0,4},{1,5},{2,6},{3,7},{4,0},{5,1},{6,2},{7,3},{8,12},{9,13},{10,... | collective-permute-start | bytes 147464 | tf_op jit(solution)/shard_map/ppermute | solution.py:409
  55.7 1.6 %collective-permute-done.14 = bf16[192,128]{1,0:T(8,128)(2,1)S(1)} collective-permute-done((bf16[192,128]{1,0:T(8,128)(2,1)S(1)}, bf16[192,128]{1,0:T(8,128)(2,1)S(1)}, u32[]{:S(2)}, u32[]{:S(2)}) %collective-permute-start.14) | collective-permute-done | bytes 49184 | tf_op jit(solution)/shard_map/ppermute | solution.py:409
  58.2 1.1 %collective-permute-done.12 = bf16[192,128]{1,0:T(8,128)(2,1)S(1)} collective-permute-done((bf16[192,128]{1,0:T(8,128)(2,1)S(1)}, bf16[192,128]{1,0:T(8,128)(2,1)S(1)}, u32[]{:S(2)}, u32[]{:S(2)}) %collective-permute-start.12) | collective-permute-done | bytes 49184 | tf_op jit(solution)/shard_map/ppermute | solution.py:409
  59.4 3.1 %collective-permute-start.17 = (bf16[48,128]{1,0:T(8,128)(2,1)S(1)}, bf16[48,128]{1,0:T(8,128)(2,1)S(1)}, u32[]{:S(2)}, u32[]{:S(2)}) collective-permute-start(bf16[48,128]{1,0:T(8,128)(2,1)S(1)} %get-tuple-element.57), channel_id=1, source_target_pairs={{0,30},{1,31},{2,28},{3,29},{4,26},{5,27},{6,24},{7,25},{8,22},{9,... | collective-permute-start | bytes 36872 | tf_op jit(solution)/shard_map/ppermute | solution.py:409
  63.3 4.2 %collective-permute-start.15 = (bf16[48,128]{1,0:T(8,128)(2,1)S(1)}, bf16[48,128]{1,0:T(8,128)(2,1)S(1)}, u32[]{:S(2)}, u32[]{:S(2)}) collective-permute-start(bf16[48,128]{1,0:T(8,128)(2,1)S(1)} %get-tuple-element.55), channel_id=1, source_target_pairs={{0,14},{1,15},{2,12},{3,13},{4,10},{5,11},{6,8},{7,9},{8,6},{9,7},... | collective-permute-start | bytes 36872 | tf_op jit(solution)/shard_map/ppermute | solution.py:409
  67.5 1.1 %collective-permute-done.17 = bf16[48,128]{1,0:T(8,128)(2,1)S(1)} collective-permute-done((bf16[48,128]{1,0:T(8,128)(2,1)S(1)}, bf16[48,128]{1,0:T(8,128)(2,1)S(1)}, u32[]{:S(2)}, u32[]{:S(2)}) %collective-permute-start.17) | collective-permute-done | bytes 12320 | tf_op jit(solution)/shard_map/ppermute | solution.py:409
  68.6 1.4 %collective-permute-done.15 = bf16[48,128]{1,0:T(8,128)(2,1)S(1)} collective-permute-done((bf16[48,128]{1,0:T(8,128)(2,1)S(1)}, bf16[48,128]{1,0:T(8,128)(2,1)S(1)}, u32[]{:S(2)}, u32[]{:S(2)}) %collective-permute-start.15) | collective-permute-done | bytes 12320 | tf_op jit(solution)/shard_map/ppermute | solution.py:409
  70.0 1.5 %collective-permute-start.18 = (bf16[48,128]{1,0:T(8,128)(2,1)S(1)}, bf16[48,128]{1,0:T(8,128)(2,1)S(1)}, u32[]{:S(2)}, u32[]{:S(2)}) collective-permute-start(bf16[48,128]{1,0:T(8,128)(2,1)S(1)} %add_convert_fusion.8), channel_id=1, source_target_pairs={{0,96},{1,97},{2,98},{3,99},{4,100},{5,101},{6,102},{7,103},{8,104... | collective-permute-start | bytes 36872 | tf_op jit(solution)/shard_map/ppermute | solution.py:409
  71.5 3.5 %collective-permute-done.18 = bf16[48,128]{1,0:T(8,128)(2,1)S(1)} collective-permute-done((bf16[48,128]{1,0:T(8,128)(2,1)S(1)}, bf16[48,128]{1,0:T(8,128)(2,1)S(1)}, u32[]{:S(2)}, u32[]{:S(2)}) %collective-permute-start.18) | collective-permute-done | bytes 12320 | tf_op jit(solution)/shard_map/ppermute | solution.py:409
  75.0 1.2 %collective-permute-start.21 = (bf16[48,128]{1,0:T(8,128)(2,1)S(1)}, bf16[48,128]{1,0:T(8,128)(2,1)S(1)}, u32[]{:S(2)}, u32[]{:S(2)}) collective-permute-start(bf16[48,128]{1,0:T(8,128)(2,1)S(1)} %add_convert_fusion.7), channel_id=1, source_target_pairs={{0,32},{1,33},{2,34},{3,35},{4,36},{5,37},{6,38},{7,39},{8,40},{9,... | collective-permute-start | bytes 36872 | tf_op jit(solution)/shard_map/ppermute | solution.py:409
  77.3 1.3 %collective-permute-start.20 = (bf16[48,128]{1,0:T(8,128)(2,1)S(1)}, bf16[48,128]{1,0:T(8,128)(2,1)S(1)}, u32[]{:S(2)}, u32[]{:S(2)}) collective-permute-start(bf16[48,128]{1,0:T(8,128)(2,1)S(1)} %add_convert_fusion.7), channel_id=1, source_target_pairs={{0,128},{1,129},{2,130},{3,131},{4,132},{5,133},{6,134},{7,135},{8... | collective-permute-start | bytes 36872 | tf_op jit(solution)/shard_map/ppermute | solution.py:409
  78.8 2.0 %collective-permute-done.19 = bf16[48,128]{1,0:T(8,128)(2,1)S(1)} collective-permute-done((bf16[48,128]{1,0:T(8,128)(2,1)S(1)}, bf16[48,128]{1,0:T(8,128)(2,1)S(1)}, u32[]{:S(2)}, u32[]{:S(2)}) %collective-permute-start.19) | collective-permute-done | bytes 12320 | tf_op jit(solution)/shard_map/ppermute | solution.py:409
  (45 shorter events, 9.6 us)
Async XLA Ops:
  1.8 2.7 %collective-permute-start = (bf16[32,512]{1,0:T(8,128)(2,1)S(1)}, bf16[32,512]{1,0:T(8,128)(2,1)S(1)}, u32[]{:S(2)}, u32[]{:S(2)}) collective-permute-start(bf16[32,512]{1,0:T(8,128)(2,1)S(1)} %get-tuple-element.27), channel_id=1, source_target_pairs={{0,1},{2,3},{4,5},{6,7},{8,9},{10,11},{12,13},{14,15},{16,17},{18,... | collective-permute-start | bytes 98312 | tf_op jit(solution)/shard_map/ppermute | solution.py:380
  1.9 3.5 %collective-permute-start.1 = (bf16[32,512]{1,0:T(8,128)(2,1)S(1)}, bf16[32,512]{1,0:T(8,128)(2,1)S(1)}, u32[]{:S(2)}, u32[]{:S(2)}) collective-permute-start(bf16[32,512]{1,0:T(8,128)(2,1)S(1)} %get-tuple-element.28), channel_id=1, source_target_pairs={{1,2},{3,4},{5,6},{7,8},{9,10},{11,12},{13,14},{15,16},{17,18},{19... | collective-permute-start | bytes 98312 | tf_op jit(solution)/shard_map/ppermute | solution.py:380
  3.8 3.9 %collective-permute-start.2 = (bf16[32,512]{1,0:T(8,128)(2,1)S(1)}, bf16[32,512]{1,0:T(8,128)(2,1)S(1)}, u32[]{:S(2)}, u32[]{:S(2)}) collective-permute-start(bf16[32,512]{1,0:T(8,128)(2,1)S(1)} %get-tuple-element.29), channel_id=1, source_target_pairs={{0,32},{64,96},{128,160},{192,224},{32,0},{96,64},{160,128},{224,1... | collective-permute-start | bytes 98312 | tf_op jit(solution)/shard_map/ppermute | solution.py:380
  3.8 3.9 %collective-permute-start.3 = (bf16[32,512]{1,0:T(8,128)(2,1)S(1)}, bf16[32,512]{1,0:T(8,128)(2,1)S(1)}, u32[]{:S(2)}, u32[]{:S(2)}) collective-permute-start(bf16[32,512]{1,0:T(8,128)(2,1)S(1)} %get-tuple-element.30), channel_id=1, source_target_pairs={{32,64},{96,128},{160,192},{64,32},{128,96},{192,160},{33,65},{97,... | collective-permute-start | bytes 98312 | tf_op jit(solution)/shard_map/ppermute | solution.py:380
  24.1 2.0 %collective-permute-start.5 = (bf16[768,256]{1,0:T(8,128)(2,1)S(1)}, bf16[768,256]{1,0:T(8,128)(2,1)S(1)}, u32[]{:S(2)}, u32[]{:S(2)}) collective-permute-start(bf16[768,256]{1,0:T(8,128)(2,1)S(1)} %get-tuple-element.38), channel_id=1, source_target_pairs={{0,1},{1,0},{2,3},{3,2},{4,5},{5,4},{6,7},{7,6},{8,9},{9,8},{10,11... | collective-permute-start | bytes 1179656 | tf_op jit(solution)/shard_map/ppermute | solution.py:409
  24.5 5.8 %collective-permute-start.4 = (bf16[832,256]{1,0:T(8,128)(2,1)S(1)}, bf16[832,256]{1,0:T(8,128)(2,1)S(1)}, u32[]{:S(2)}, u32[]{:S(2)}) collective-permute-start(bf16[832,256]{1,0:T(8,128)(2,1)S(1)} %get-tuple-element.34), channel_id=1, source_target_pairs={{0,1},{1,0},{2,3},{3,2},{4,5},{5,4},{6,7},{7,6},{8,9},{9,8},{10,11... | collective-permute-start | bytes 1277960 | tf_op jit(solution)/shard_map/ppermute | solution.py:409
  26.3 11.9 %collective-permute-start.9 = (bf16[896,128]{1,0:T(8,128)(2,1)S(1)}, bf16[896,128]{1,0:T(8,128)(2,1)S(1)}, u32[]{:S(2)}, u32[]{:S(2)}) collective-permute-start(bf16[896,128]{1,0:T(8,128)(2,1)S(1)} %pad_maximum_fusion), channel_id=1, source_target_pairs={{0,32},{1,33},{2,34},{3,35},{4,36},{5,37},{6,38},{7,39},{8,40},{9,... | collective-permute-start | bytes 688136 | tf_op jit(solution)/shard_map/ppermute | solution.py:409
  30.4 17.4 %copy-start = (s32[128]{0:T(128)S(1)}, s32[128]{0:T(128)}, u32[]{:S(2)}) copy-start(s32[128]{0:T(128)} %param.18) | copy-start | bytes 1540
  30.4 12.3 %collective-permute-start.8 = (bf16[384,256]{1,0:T(8,128)(2,1)S(1)}, bf16[384,256]{1,0:T(8,128)(2,1)S(1)}, u32[]{:S(2)}, u32[]{:S(2)}) collective-permute-start(bf16[384,256]{1,0:T(8,128)(2,1)S(1)} %broadcast_select_fusion.1), channel_id=1, source_target_pairs={{0,2},{1,3},{2,0},{3,1},{4,6},{5,7},{6,4},{7,5},{8,10},{9,11},{10,... | collective-permute-start | bytes 589832 | tf_op jit(solution)/shard_map/ppermute | solution.py:409
  37.5 4.8 %collective-permute-start.6 = (bf16[32,512]{1,0:T(8,128)(2,1)S(1)}, bf16[32,512]{1,0:T(8,128)(2,1)S(1)}, u32[]{:S(2)}, u32[]{:S(2)}) collective-permute-start(bf16[32,512]{1,0:T(8,128)(2,1)S(1)} %get-tuple-element.39), channel_id=1, source_target_pairs={{1,2},{3,4},{5,6},{7,8},{9,10},{11,12},{13,14},{15,16},{17,18},{19... | collective-permute-start | bytes 98312 | tf_op jit(solution)/shard_map/ppermute | solution.py:380
  37.5 4.8 %collective-permute-start.7 = (bf16[32,512]{1,0:T(8,128)(2,1)S(1)}, bf16[32,512]{1,0:T(8,128)(2,1)S(1)}, u32[]{:S(2)}, u32[]{:S(2)}) collective-permute-start(bf16[32,512]{1,0:T(8,128)(2,1)S(1)} %get-tuple-element.40), channel_id=1, source_target_pairs={{32,64},{96,128},{160,192},{64,32},{128,96},{192,160},{33,65},{97,... | collective-permute-start | bytes 98312 | tf_op jit(solution)/shard_map/ppermute | solution.py:380
  42.9 6.1 %collective-permute-start.10 = (bf16[384,128]{1,0:T(8,128)(2,1)S(1)}, bf16[384,128]{1,0:T(8,128)(2,1)S(1)}, u32[]{:S(2)}, u32[]{:S(2)}) collective-permute-start(bf16[384,128]{1,0:T(8,128)(2,1)S(1)} %broadcast_select_fusion.3), channel_id=1, source_target_pairs={{0,32},{1,33},{2,34},{3,35},{4,36},{5,37},{6,38},{7,39},{8,40},{9,... | collective-permute-start | bytes 294920 | tf_op jit(solution)/shard_map/ppermute | solution.py:409
  46.4 4.7 %collective-permute-start.11 = (bf16[384,128]{1,0:T(8,128)(2,1)S(1)}, bf16[384,128]{1,0:T(8,128)(2,1)S(1)}, u32[]{:S(2)}, u32[]{:S(2)}) collective-permute-start(bf16[384,128]{1,0:T(8,128)(2,1)S(1)} %broadcast_select_fusion.2), channel_id=1, source_target_pairs={{0,2},{1,3},{2,0},{3,1},{4,6},{5,7},{6,4},{7,5},{8,10},{9,11},{10,... | collective-permute-start | bytes 294920 | tf_op jit(solution)/shard_map/ppermute | solution.py:409
  51.3 6.1 %collective-permute-start.14 = (bf16[192,128]{1,0:T(8,128)(2,1)S(1)}, bf16[192,128]{1,0:T(8,128)(2,1)S(1)}, u32[]{:S(2)}, u32[]{:S(2)}) collective-permute-start(bf16[192,128]{1,0:T(8,128)(2,1)S(1)} %get-tuple-element.52), channel_id=1, source_target_pairs={{0,132},{1,133},{2,134},{3,135},{4,128},{5,129},{6,130},{7,131},{8... | collective-permute-start | bytes 147464 | tf_op jit(solution)/shard_map/ppermute | solution.py:409
  53.2 5.0 %collective-permute-start.13 = (bf16[192,128]{1,0:T(8,128)(2,1)S(1)}, bf16[192,128]{1,0:T(8,128)(2,1)S(1)}, u32[]{:S(2)}, u32[]{:S(2)}) collective-permute-start(bf16[192,128]{1,0:T(8,128)(2,1)S(1)} %get-tuple-element.51), channel_id=1, source_target_pairs={{0,4},{1,5},{2,6},{3,7},{4,0},{5,1},{6,2},{7,3},{8,12},{9,13},{10,... | collective-permute-start | bytes 147464 | tf_op jit(solution)/shard_map/ppermute | solution.py:409
  55.2 4.1 %collective-permute-start.12 = (bf16[192,128]{1,0:T(8,128)(2,1)S(1)}, bf16[192,128]{1,0:T(8,128)(2,1)S(1)}, u32[]{:S(2)}, u32[]{:S(2)}) collective-permute-start(bf16[192,128]{1,0:T(8,128)(2,1)S(1)} %get-tuple-element.50), channel_id=1, source_target_pairs={{0,128},{1,129},{2,130},{3,131},{4,132},{5,133},{6,134},{7,135},{8... | collective-permute-start | bytes 147464 | tf_op jit(solution)/shard_map/ppermute | solution.py:409
  59.4 9.2 %collective-permute-start.17 = (bf16[48,128]{1,0:T(8,128)(2,1)S(1)}, bf16[48,128]{1,0:T(8,128)(2,1)S(1)}, u32[]{:S(2)}, u32[]{:S(2)}) collective-permute-start(bf16[48,128]{1,0:T(8,128)(2,1)S(1)} %get-tuple-element.57), channel_id=1, source_target_pairs={{0,30},{1,31},{2,28},{3,29},{4,26},{5,27},{6,24},{7,25},{8,22},{9,... | collective-permute-start | bytes 36872 | tf_op jit(solution)/shard_map/ppermute | solution.py:409
  62.5 6.1 %collective-permute-start.16 = (bf16[48,128]{1,0:T(8,128)(2,1)S(1)}, bf16[48,128]{1,0:T(8,128)(2,1)S(1)}, u32[]{:S(2)}, u32[]{:S(2)}) collective-permute-start(bf16[48,128]{1,0:T(8,128)(2,1)S(1)} %get-tuple-element.56), channel_id=1, source_target_pairs={{0,16},{1,17},{2,18},{3,19},{4,20},{5,21},{6,22},{7,23},{8,24},{9,... | collective-permute-start | bytes 36872 | tf_op jit(solution)/shard_map/ppermute | solution.py:409
  63.3 6.7 %collective-permute-start.15 = (bf16[48,128]{1,0:T(8,128)(2,1)S(1)}, bf16[48,128]{1,0:T(8,128)(2,1)S(1)}, u32[]{:S(2)}, u32[]{:S(2)}) collective-permute-start(bf16[48,128]{1,0:T(8,128)(2,1)S(1)} %get-tuple-element.55), channel_id=1, source_target_pairs={{0,14},{1,15},{2,12},{3,13},{4,10},{5,11},{6,8},{7,9},{8,6},{9,7},... | collective-permute-start | bytes 36872 | tf_op jit(solution)/shard_map/ppermute | solution.py:409
  70.0 5.0 %collective-permute-start.18 = (bf16[48,128]{1,0:T(8,128)(2,1)S(1)}, bf16[48,128]{1,0:T(8,128)(2,1)S(1)}, u32[]{:S(2)}, u32[]{:S(2)}) collective-permute-start(bf16[48,128]{1,0:T(8,128)(2,1)S(1)} %add_convert_fusion.8), channel_id=1, source_target_pairs={{0,96},{1,97},{2,98},{3,99},{4,100},{5,101},{6,102},{7,103},{8,104... | collective-permute-start | bytes 36872 | tf_op jit(solution)/shard_map/ppermute | solution.py:409
  75.0 3.8 %collective-permute-start.21 = (bf16[48,128]{1,0:T(8,128)(2,1)S(1)}, bf16[48,128]{1,0:T(8,128)(2,1)S(1)}, u32[]{:S(2)}, u32[]{:S(2)}) collective-permute-start(bf16[48,128]{1,0:T(8,128)(2,1)S(1)} %add_convert_fusion.7), channel_id=1, source_target_pairs={{0,32},{1,33},{2,34},{3,35},{4,36},{5,37},{6,38},{7,39},{8,40},{9,... | collective-permute-start | bytes 36872 | tf_op jit(solution)/shard_map/ppermute | solution.py:409
  76.2 4.6 %collective-permute-start.19 = (bf16[48,128]{1,0:T(8,128)(2,1)S(1)}, bf16[48,128]{1,0:T(8,128)(2,1)S(1)}, u32[]{:S(2)}, u32[]{:S(2)}) collective-permute-start(bf16[48,128]{1,0:T(8,128)(2,1)S(1)} %add_convert_fusion.7), channel_id=1, source_target_pairs={{0,160},{1,161},{2,162},{3,163},{4,164},{5,165},{6,166},{7,167},{8... | collective-permute-start | bytes 36872 | tf_op jit(solution)/shard_map/ppermute | solution.py:409
  77.3 3.7 %collective-permute-start.20 = (bf16[48,128]{1,0:T(8,128)(2,1)S(1)}, bf16[48,128]{1,0:T(8,128)(2,1)S(1)}, u32[]{:S(2)}, u32[]{:S(2)}) collective-permute-start(bf16[48,128]{1,0:T(8,128)(2,1)S(1)} %add_convert_fusion.7), channel_id=1, source_target_pairs={{0,128},{1,129},{2,130},{3,131},{4,132},{5,133},{6,134},{7,135},{8... | collective-permute-start | bytes 36872 | tf_op jit(solution)/shard_map/ppermute | solution.py:409
